TPU v7x, 32 devices: a whole 2x2x4 slice. The times are simulated.
32 devices in a mesh: blk: 8 (over z, x), gz: 4 (over y, core).
Axes of the slice: x: 2, y: 2, z: 4, core: 2. Of those that a mesh axis runs over, the one named last changes fastest.
Arguments:
- fixed: bfloat16 [8, 32, 32, 128], P('blk', 'gz'), may hold values from -6 to 6
- moving: bfloat16 [8, 32, 32, 128], P('blk', 'gz'), may hold values from -6 to 6
- block_place: int32 [8], P('blk'), may hold values from 0 to 7, each once
- tissue: int32 [8], P('blk'), may hold values 0 or 1
Outputs:
- velocity: float32 [3, 2, 2, 64], replicated
- cc_map: float32 [8, 32, 32, 128], P('blk', 'gz')
Inputs may be any that keep to these rules, and one draw needn't show every extreme that they name: `block_place`: each block position from 0 to 7 is named by exactly one block.
All inputs are finite; a program needn't handle non-finite values. No bound on the sum of `tissue` on one device may be relied on, other than what follows from the above.
Results may differ from a plain program's by a relative error of at most 0.0004.
Values may be sent and summed in bfloat16 or wider, within the bound.
No kernel may reach another device: no remote copies, remote signals or barrier semaphores. Data moves between devices by JAX's collectives and lax.ppermute only.
A program may use at most 64 MiB of HBM per device.

v0:
```python
import math

import jax
import jax.numpy as jnp
from jax import lax
from jax.sharding import PartitionSpec as P

SCALE = 16
GY = 8
ITERS = 2


EXACT = lax.Precision.HIGHEST
EPSILON = 1e-05
STEP_LENGTH = 0.5
BOX_TAPS = [1.0 / 9.0] * 9
GAUSS_RAW = [math.exp(-((offset - 3) ** 2) / 4.5) for offset in range(7)]
GAUSS_TAPS = [value / sum(GAUSS_RAW) for value in GAUSS_RAW]


def with_halo(block, sides, width):
    for axis, dim in sides:
        count = lax.axis_size(axis)
        forward = [(i, i + 1) for i in range(count - 1)]
        backward = [(target, source) for source, target in forward]
        low = lax.ppermute(
            lax.slice_in_dim(block, block.shape[dim] - width, None, axis=dim), axis, forward
        )
        high = lax.ppermute(lax.slice_in_dim(block, 0, width, axis=dim), axis, backward)
        block = jnp.concatenate([low, block, high], axis=dim)
    return block


def tap_matrix(count, taps):
    radius = len(taps) // 2
    rows = jnp.arange(count)[:, None]
    cols = jnp.arange(count)[None, :]
    matrix = jnp.zeros((count, count), jnp.float32)
    for offset, weight in enumerate(taps):
        matrix = matrix + weight * (rows - cols == offset - radius).astype(jnp.float32)
    return matrix


def along_rows(field, matrix):
    return jnp.einsum("...xy,xu->...uy", field, matrix, precision=EXACT)


def along_cols(field, matrix):
    return jnp.einsum("...y,yv->...v", field, matrix, precision=EXACT)


def planes_filter(field, taps, count):
    total = jnp.zeros(field.shape[:-3] + (count,) + field.shape[-2:], jnp.float32)
    for offset, weight in enumerate(taps):
        total = total + weight * field[..., offset : offset + count, :, :]
    return total


def slope(field, axis):
    widths = [(0, 0)] * field.ndim
    widths[axis] = (1, 1)
    padded = jnp.pad(field, widths)
    length = field.shape[axis]
    upper = lax.slice_in_dim(padded, 2, length + 2, axis=axis)
    lower = lax.slice_in_dim(padded, 0, length, axis=axis)
    return 0.5 * (upper - lower)


def hat_rows(coords, count):
    where = jnp.clip((coords + 0.5) / SCALE - 0.5, 0.0, count - 1.0)
    marks = jnp.arange(count).astype(jnp.float32)
    return jnp.maximum(0.0, 1.0 - jnp.abs(where[..., None] - marks))


def statistics(means, fixed_c, warped_c):
    sii = means[2] - means[0] * means[0]
    sww = means[3] - means[1] * means[1]
    siw = means[4] - means[0] * means[1]
    denom = sii * sww + EPSILON
    similar = siw * siw / denom
    weight = (
        2.0 * siw / denom * (fixed_c - means[0] - siw / (sww + EPSILON) * (warped_c - means[1]))
    )
    return (similar, weight)


def smooth_axis(field, axis):
    widths = [(0, 0)] * field.ndim
    widths[axis] = (1, 1)
    padded = jnp.pad(field, widths)
    length = field.shape[axis]
    upper = lax.slice_in_dim(padded, 2, length + 2, axis=axis)
    lower = lax.slice_in_dim(padded, 0, length, axis=axis)
    return 0.25 * lower + 0.5 * field + 0.25 * upper


def regularize(velocity, total, coarse_rows, coarse_cols):
    block_rows = velocity.shape[2] // coarse_rows
    coarse_depth = velocity.shape[1]
    grid = total.reshape(block_rows, GY, 3, coarse_depth, coarse_rows, coarse_cols)
    grid = grid.transpose(2, 3, 0, 4, 1, 5).reshape(velocity.shape)
    regular = smooth_axis(smooth_axis(smooth_axis(grid, 1), 2), 3)
    return velocity + STEP_LENGTH * regular / jnp.sqrt(jnp.mean(regular * regular) + EPSILON)


def per_device(fixed, moving, block_place, tissue):
    slots, planes, row_side, col_side = fixed.shape
    depth_parts = lax.axis_size("gz")
    depth_index = lax.axis_index("gz")
    blocks = slots * lax.axis_size("blk")
    total_planes = planes * depth_parts
    coarse_depth = total_planes // SCALE
    coarse_rows = row_side // SCALE
    coarse_cols = col_side // SCALE
    grid_rows = blocks // GY * coarse_rows
    grid_cols = GY * coarse_cols
    stacked = jnp.stack([fixed, moving], 0)
    reach = 0
    haloed = with_halo(stacked, (("gz", 2),), 5)
    images = haloed.astype(jnp.float32)
    count_w = planes + 2 * (reach + 4)
    count_m = planes + 2 * reach
    fixed_w = images[0, :, 1 : 1 + count_w]
    moving_w = images[1, :, 1 : 1 + count_w]
    depth_slope = 0.5 * (images[1, :, 2 : 2 + count_w] - images[1, :, 0:count_w])
    row_slope = slope(moving_w, 2)
    col_slope = slope(moving_w, 3)
    depth_w = depth_index * planes - (reach + 4) + jnp.arange(count_w)
    inside_w = ((depth_w >= 0) & (depth_w < total_planes)).astype(jnp.float32)
    depth_hat = hat_rows(depth_w.astype(jnp.float32), coarse_depth)
    depth_m = depth_index * planes - reach + jnp.arange(count_m)
    inside_m = ((depth_m >= 0) & (depth_m < total_planes)).astype(jnp.float32)
    row_cells = jnp.arange(row_side)
    col_cells = jnp.arange(col_side)
    block_row = block_place // GY
    block_col = block_place % GY
    row_hat = hat_rows(
        (block_row[:, None] * row_side + row_cells[None, :]).astype(jnp.float32), grid_rows
    )
    col_hat = hat_rows(
        (block_col[:, None] * col_side + col_cells[None, :]).astype(jnp.float32), grid_cols
    )
    own_depth = depth_index * planes + jnp.arange(planes)
    restrict = (own_depth[None, :] // SCALE == jnp.arange(coarse_depth)[:, None]).astype(
        jnp.float32
    )
    box_rows = tap_matrix(row_side, BOX_TAPS)
    box_cols = tap_matrix(col_side, BOX_TAPS)
    gauss_rows = tap_matrix(row_side, GAUSS_TAPS)
    gauss_cols = tap_matrix(col_side, GAUSS_TAPS)
    tissue_scale = tissue.astype(jnp.float32)[:, None, None, None]
    positions = jnp.arange(blocks)
    velocity = jnp.zeros((3, coarse_depth, grid_rows, grid_cols), jnp.float32)
    correlation = jnp.zeros((slots, planes, row_side, col_side), jnp.float32)
    for rounds in range(ITERS):
        partial_value = jnp.einsum("ckab,sxa->sckxb", velocity, row_hat, precision=EXACT)
        partial_value = jnp.einsum("sckxb,syb->sckxy", partial_value, col_hat, precision=EXACT)
        shift = jnp.einsum("zk,sckxy->cszxy", depth_hat, partial_value, precision=EXACT)
        warped = moving_w + shift[0] * depth_slope + shift[1] * row_slope + shift[2] * col_slope
        warped = warped * inside_w[None, :, None, None]
        fields = jnp.stack(
            [fixed_w, warped, fixed_w * fixed_w, warped * warped, fixed_w * warped], 0
        )
        means = planes_filter(fields, BOX_TAPS, count_m)
        means = along_cols(along_rows(means, box_rows), box_cols)
        fixed_m = fixed_w[:, 4 : 4 + count_m]
        warped_m = warped[:, 4 : 4 + count_m]
        similar, weight = statistics(means, fixed_m, warped_m)
        scale = weight * tissue_scale * inside_m[None, :, None, None]
        depth_grad = 0.5 * (warped[:, 5 : 5 + count_m] - warped[:, 3 : 3 + count_m])
        force = jnp.stack(
            [scale * depth_grad, scale * slope(warped_m, 2), scale * slope(warped_m, 3)], 0
        )
        force = with_halo(force, (("gz", 2),), 3)
        smooth = planes_filter(force, GAUSS_TAPS, planes)
        smooth = along_cols(along_rows(smooth, gauss_rows), gauss_cols)
        local = smooth.reshape(3, slots, planes, coarse_rows, SCALE, coarse_cols, SCALE).sum(
            axis=(4, 6)
        )
        piece = jnp.einsum("kp,cspab->sckab", restrict, local, precision=EXACT).reshape(slots, -1)
        onehot_local = (positions[:, None] == block_place[None, :]).astype(jnp.float32)
        local_grid = jnp.dot(onehot_local, piece, precision=EXACT)
        total = lax.psum(local_grid, ("blk", "gz"))
        velocity = regularize(velocity, total, coarse_rows, coarse_cols)
        correlation = similar
    return (velocity, correlation)


def solution(mesh):
    return jax.shard_map(
        per_device,
        mesh=mesh,
        in_specs=(P("blk", "gz", None, None), P("blk", "gz", None, None), P("blk"), P("blk")),
        out_specs=(P(), P("blk", "gz", None, None)),
        check_vma=False,
    )
```

profile of v0, /device:TPU:0, one launch (start us, length us, event | category | flops | bytes accessed | tf_op | source)
XLA Modules:
  0.0 132.1 jit_solution(11607887490164051860)
XLA Ops:
  0.6 0.9 copy_bitcast_fusion
  1.6 0.1 slice_maximum_fusion
  1.6 2.4 %collective-permute-start = (bf16[2,1,5,32,128]{4,2,3,1,0:T(8,128)(2,1)S(1)}, bf16[2,1,5,32,128]{4,2,3,1,0:T(8,128)(2,1)S(1)}, u32[]{:S(2)}, u32[]{:S(2)}) collective-permute-start(bf16[2,1,5,32,128]{4,2,3,1,0:T(8,128)(2,1)S(1)} %get-tuple-element.42), channel_id=1, source_target_pairs={{0,1},{1,2},{2,3},{4,5},{5,6},{6,7},{8,9},{9,10},{10,11},{12,13},{... | collective-permute-start | bytes 245768 | tf_op jit(solution)/shard_map/ppermute | solution.py:26
  4.0 1.3 collective-permute-start.1
  6.8 0.1 sub.275
  6.8 0.1 select_add_fusion
  7.0 0.4 convolution_bitcast_fusion.4
  7.3 0.3 fusion.100
  7.6 0.9 fusion.78
  8.6 0.0 collective-permute-done
  8.6 0.8 collective-permute-done.1
  9.4 0.2 maximum_convert_fusion
  9.6 0.1 slice_bitcast_fusion.4
  9.6 0.1 copy.140
  9.7 0.2 bitcast_dynamic-update-slice_fusion.5
  10.1 0.5 fusion.3
  10.6 0.7 convolution_bitcast_fusion.2
  11.3 1.0 fusion.6
  12.3 0.2 fusion.70
  12.5 0.1 fusion.50
  12.7 0.1 fusion.252
  12.7 5.5 %collective-permute-start.2 = (f32[3,1,3,32,128]{4,2,3,1,0:T(4,128)S(1)}, f32[3,1,3,32,128]{4,2,3,1,0:T(4,128)S(1)}, u32[]{:S(2)}, u32[]{:S(2)}) collective-permute-start(f32[3,1,3,32,128]{4,2,3,1,0:T(4,128)S(1)} %get-tuple-element.34), channel_id=1, source_target_pairs={{0,1},{1,2},{2,3},{4,5},{5,6},{6,7},{8,9},{9,10},{10,11},{12,13},{... | collective-permute-start | bytes 442376 | tf_op jit(solution)/shard_map/ppermute | solution.py:26
  18.2 1.3 collective-permute-start.3
  19.5 0.0 collective-permute-done.2
  19.6 2.1 %collective-permute-done.3 = f32[3,1,3,32,128]{4,2,3,1,0:T(4,128)S(1)} collective-permute-done((f32[3,1,3,32,128]{4,2,3,1,0:T(4,128)S(1)}, f32[3,1,3,32,128]{4,2,3,1,0:T(4,128)S(1)}, u32[]{:S(2)}, u32[]{:S(2)}) %collective-permute-start.3) | collective-permute-done | bytes 147488 | tf_op jit(solution)/shard_map/ppermute | solution.py:29
  21.7 0.2 maximum_maximum_fusion
  21.8 0.3 fusion.18
  22.1 0.5 fusion.26
  22.6 3.3 %convolution_reduce_fusion.1 = f32[3,8,2,8]{3,2,1,0:T(2,128)S(1)} fusion(f32[3,8,2,16,128,1]{4,3,5,2,1,0:T(8,128)S(1)} %bitcast.236, f32[8,16,128,1,1,1]{2,1,0,5,4,3:T(8,128)S(1)} %bitcast.239), kind=kOutput, calls=%fused_computation.1 | convolution fusion | flops 151092864 | bytes 460288 | tf_op jit(solution)/shard_map/...y,yv->...v/dot_general | solution.py:49
  26.0 0.1 convolution_bitcast_fusion.6
  26.1 0.1 reshape.688
  26.2 0.1 broadcast_multiply_fusion.1
  26.3 0.1 reshape.689
  26.4 0.1 reshape.690
  26.5 43.4 %psum.14 = f32[3,2,2,64]{3,2,1,0:T(2,128)S(1)} all-reduce(f32[3,2,2,64]{3,2,1,0:T(2,128)S(1)} %reshape.690), channel_id=1, replica_groups=mesh['blk'=8,'gz'=4] {'blk','gz'}, use_global_device_ids=true, to_apply=%region_1.2 | all-reduce | flops 768 | bytes 6144 | tf_op jit(solution)/shard_map/psum | solution.py:183
  69.9 0.7 multiply_reduce_fusion.1
  71.3 0.4 convolution_bitcast_fusion.3
  71.7 0.3 fusion.98
  72.0 0.9 convolution_bitcast_fusion
  72.9 0.2 bitcast_dynamic-update-slice_fusion.2
  73.3 0.5 fusion.1
  73.8 0.7 convolution_bitcast_fusion.1
  74.5 1.0 fusion.4
  75.5 0.1 multiply_divide_fusion
  75.6 0.1 fusion.65
  75.7 0.1 fusion.54
  75.9 0.1 fusion.251
  76.0 1.3 collective-permute-start.4
  77.3 1.3 collective-permute-start.5
  78.6 0.7 copy.99
  79.2 0.0 collective-permute-done.4
  79.2 3.8 %collective-permute-done.5 = f32[3,1,3,32,128]{4,2,3,1,0:T(4,128)S(1)} collective-permute-done((f32[3,1,3,32,128]{4,2,3,1,0:T(4,128)S(1)}, f32[3,1,3,32,128]{4,2,3,1,0:T(4,128)S(1)}, u32[]{:S(2)}, u32[]{:S(2)}) %collective-permute-start.5) | collective-permute-done | bytes 147488 | tf_op jit(solution)/shard_map/ppermute | solution.py:29
  83.1 0.2 maximum_maximum_fusion.1
  83.3 0.3 fusion.11
  83.6 0.5 fusion.24
  84.0 3.3 %convolution_reduce_fusion = f32[3,8,2,8]{3,2,1,0:T(2,128)S(1)} fusion(f32[3,8,2,16,128,1]{4,3,5,2,1,0:T(8,128)S(1)} %bitcast.235, f32[8,16,128,1,1,1]{2,1,0,5,4,3:T(8,128)S(1)} %bitcast.240), kind=kOutput, calls=%fused_computation | convolution fusion | flops 151092864 | bytes 460288 | tf_op jit(solution)/shard_map/...y,yv->...v/dot_general | solution.py:49
  87.4 0.1 convolution_bitcast_fusion.5
  87.5 0.1 reshape.696
  87.6 0.1 broadcast_multiply_fusion
  87.7 0.1 reshape.697
  87.8 0.1 reshape.698
  87.9 42.1 %psum.15 = f32[3,2,2,64]{3,2,1,0:T(2,128)S(1)} all-reduce(f32[3,2,2,64]{3,2,1,0:T(2,128)S(1)} %reshape.698), channel_id=1, replica_groups=mesh['blk'=8,'gz'=4] {'blk','gz'}, use_global_device_ids=true, to_apply=%region_4.5 | all-reduce | flops 768 | bytes 6144 | tf_op jit(solution)/shard_map/psum | solution.py:183
  130.1 0.7 multiply_reduce_fusion
  131.4 0.6 divide_add_fusion
  (26 shorter events, 0.4 us)
Async XLA Ops:
  1.6 6.9 %collective-permute-start = (bf16[2,1,5,32,128]{4,2,3,1,0:T(8,128)(2,1)S(1)}, bf16[2,1,5,32,128]{4,2,3,1,0:T(8,128)(2,1)S(1)}, u32[]{:S(2)}, u32[]{:S(2)}) collective-permute-start(bf16[2,1,5,32,128]{4,2,3,1,0:T(8,128)(2,1)S(1)} %get-tuple-element.42), channel_id=1, source_target_pairs={{0,1},{1,2},{2,3},{4,5},{5,6},{6,7},{8,9},{9,10},{10,11},{12,13},{... | collective-permute-start | bytes 245768 | tf_op jit(solution)/shard_map/ppermute | solution.py:26
  4.0 5.4 %collective-permute-start.1 = (bf16[2,1,5,32,128]{4,2,3,1,0:T(8,128)(2,1)S(1)}, bf16[2,1,5,32,128]{4,2,3,1,0:T(8,128)(2,1)S(1)}, u32[]{:S(2)}, u32[]{:S(2)}) collective-permute-start(bf16[2,1,5,32,128]{4,2,3,1,0:T(8,128)(2,1)S(1)} %get-tuple-element.43), channel_id=1, source_target_pairs={{1,0},{2,1},{3,2},{5,4},{6,5},{7,6},{9,8},{10,9},{11,10},{13,12},{... | collective-permute-start | bytes 245768 | tf_op jit(solution)/shard_map/ppermute | solution.py:29
  12.7 6.8 %collective-permute-start.2 = (f32[3,1,3,32,128]{4,2,3,1,0:T(4,128)S(1)}, f32[3,1,3,32,128]{4,2,3,1,0:T(4,128)S(1)}, u32[]{:S(2)}, u32[]{:S(2)}) collective-permute-start(f32[3,1,3,32,128]{4,2,3,1,0:T(4,128)S(1)} %get-tuple-element.34), channel_id=1, source_target_pairs={{0,1},{1,2},{2,3},{4,5},{5,6},{6,7},{8,9},{9,10},{10,11},{12,13},{... | collective-permute-start | bytes 442376 | tf_op jit(solution)/shard_map/ppermute | solution.py:26
  18.2 3.5 %collective-permute-start.3 = (f32[3,1,3,32,128]{4,2,3,1,0:T(4,128)S(1)}, f32[3,1,3,32,128]{4,2,3,1,0:T(4,128)S(1)}, u32[]{:S(2)}, u32[]{:S(2)}) collective-permute-start(f32[3,1,3,32,128]{4,2,3,1,0:T(4,128)S(1)} %get-tuple-element.35), channel_id=1, source_target_pairs={{1,0},{2,1},{3,2},{5,4},{6,5},{7,6},{9,8},{10,9},{11,10},{13,12},{... | collective-permute-start | bytes 442376 | tf_op jit(solution)/shard_map/ppermute | solution.py:29
  76.0 3.3 %collective-permute-start.4 = (f32[3,1,3,32,128]{4,2,3,1,0:T(4,128)S(1)}, f32[3,1,3,32,128]{4,2,3,1,0:T(4,128)S(1)}, u32[]{:S(2)}, u32[]{:S(2)}) collective-permute-start(f32[3,1,3,32,128]{4,2,3,1,0:T(4,128)S(1)} %get-tuple-element.30), channel_id=1, source_target_pairs={{0,1},{1,2},{2,3},{4,5},{5,6},{6,7},{8,9},{9,10},{10,11},{12,13},{... | collective-permute-start | bytes 442376 | tf_op jit(solution)/shard_map/ppermute | solution.py:26
  77.3 5.8 %collective-permute-start.5 = (f32[3,1,3,32,128]{4,2,3,1,0:T(4,128)S(1)}, f32[3,1,3,32,128]{4,2,3,1,0:T(4,128)S(1)}, u32[]{:S(2)}, u32[]{:S(2)}) collective-permute-start(f32[3,1,3,32,128]{4,2,3,1,0:T(4,128)S(1)} %get-tuple-element.31), channel_id=1, source_target_pairs={{1,0},{2,1},{3,2},{5,4},{6,5},{7,6},{9,8},{10,9},{11,10},{13,12},{... | collective-permute-start | bytes 442376 | tf_op jit(solution)/shard_map/ppermute | solution.py:29
where the time goes:
time: 133 us; the launch traced here: 132 us
  blocking collectives  85.5 us (64%)
  matrix products  14.5 us (11%)
  starting transfers between devices  13 us (10%)
  waiting for transfers between devices  6.79 us (5%)
  other arithmetic  5.8 us (4%)
  between operations  3.86 us (3%)
  local copies, waits for them, and re-layouts  2.56 us (2%)
    psum x2, blocking collectives, per_device(): total = lax.psum(local_grid, ('blk', 'gz'))  85.5 us
    ppermute x3, starting transfers between devices, with_halo(): lax.ppermute(lax.slice_in_dim(block, block.shape[dim] - width, None, axis...  9.16 us
    dot_general x4, matrix products, along_cols(): return jnp.einsum('...y,yv->...v', field, matrix, precision=EXACT)  8.74 us
    ppermute x3, waiting for transfers between devices, with_halo(): lax.ppermute(lax.slice_in_dim(block, 0, width, axis=dim), axis, backward)  6.79 us
    ppermute x3, starting transfers between devices, with_halo(): lax.ppermute(lax.slice_in_dim(block, 0, width, axis=dim), axis, backward)  3.88 us
  transfers between devices with their start and end apart: 6, of which 3 were waited for; matrix products, arithmetic and copies ran while one was open for 2% of the time, Pallas kernels for 0%

commit v1 on v0

--- a/solution.py
+++ b/solution.py
@@ -101,6 +101,20 @@
     grid = grid.transpose(2, 3, 0, 4, 1, 5).reshape(velocity.shape)
     regular = smooth_axis(smooth_axis(smooth_axis(grid, 1), 2), 3)
     return velocity + STEP_LENGTH * regular / jnp.sqrt(jnp.mean(regular * regular) + EPSILON)
+
+
+def cell_weights(source, length):
+    target = jnp.arange(length)
+    taps = jnp.zeros((length, source.shape[0]), jnp.float32)
+    for offset, weight in enumerate(GAUSS_TAPS):
+        taps = taps + weight * (target[:, None] - source[None, :] == offset - 3).astype(jnp.float32)
+    return taps.reshape(length // SCALE, SCALE, -1).sum(1)
+
+
+def everywhere(value):
+    count = lax.axis_size("blk") * lax.axis_size("gz")
+    copies = jnp.broadcast_to(value[None], (count,) + value.shape)
+    return lax.all_to_all(copies, ("blk", "gz"), 0, 0).reshape(-1, value.shape[-1])
 
 
 def per_device(fixed, moving, block_place, tissue):
@@ -141,13 +155,11 @@
         (block_col[:, None] * col_side + col_cells[None, :]).astype(jnp.float32), grid_cols
     )
     own_depth = depth_index * planes + jnp.arange(planes)
-    restrict = (own_depth[None, :] // SCALE == jnp.arange(coarse_depth)[:, None]).astype(
-        jnp.float32
-    )
+    cell_planes = cell_weights(own_depth, total_planes)
+    cell_rows = cell_weights(jnp.arange(row_side), row_side).T
+    cell_cols = cell_weights(jnp.arange(col_side), col_side).T
     box_rows = tap_matrix(row_side, BOX_TAPS)
     box_cols = tap_matrix(col_side, BOX_TAPS)
-    gauss_rows = tap_matrix(row_side, GAUSS_TAPS)
-    gauss_cols = tap_matrix(col_side, GAUSS_TAPS)
     tissue_scale = tissue.astype(jnp.float32)[:, None, None, None]
     positions = jnp.arange(blocks)
     velocity = jnp.zeros((3, coarse_depth, grid_rows, grid_cols), jnp.float32)
@@ -171,16 +183,14 @@
         force = jnp.stack(
             [scale * depth_grad, scale * slope(warped_m, 2), scale * slope(warped_m, 3)], 0
         )
-        force = with_halo(force, (("gz", 2),), 3)
-        smooth = planes_filter(force, GAUSS_TAPS, planes)
-        smooth = along_cols(along_rows(smooth, gauss_rows), gauss_cols)
-        local = smooth.reshape(3, slots, planes, coarse_rows, SCALE, coarse_cols, SCALE).sum(
-            axis=(4, 6)
-        )
-        piece = jnp.einsum("kp,cspab->sckab", restrict, local, precision=EXACT).reshape(slots, -1)
-        onehot_local = (positions[:, None] == block_place[None, :]).astype(jnp.float32)
-        local_grid = jnp.dot(onehot_local, piece, precision=EXACT)
-        total = lax.psum(local_grid, ("blk", "gz"))
+        partial = jnp.einsum("cszxy,yb->cszxb", force, cell_cols, precision=EXACT)
+        partial = jnp.einsum("cszxb,xa->cszab", partial, cell_rows, precision=EXACT)
+        piece = jnp.einsum("kz,cszab->sckab", cell_planes, partial, precision=EXACT)
+        piece = piece.reshape(slots, -1)
+        message = jnp.concatenate([piece, block_place[:, None].astype(jnp.float32)], axis=1)
+        received = everywhere(message)
+        onehot = (positions[:, None] == received[None, :, -1].astype(jnp.int32)).astype(jnp.float32)
+        total = jnp.dot(onehot, received[:, :-1], precision=EXACT)
         velocity = regularize(velocity, total, coarse_rows, coarse_cols)
         correlation = similar
     return (velocity, correlation)

time: 133 us -> 50.4 us (0.38)
  blocking collectives: 85.5 us -> 15.6 us
  starting transfers between devices: 13 us -> 6.26 us
  matrix products: 14.5 us -> 8.74 us
    psum x2 -> x0, blocking collectives: 85.5 us -> none  [per_device(): total = lax.psum(local_grid, ('blk', 'gz'))]
    all_to_all x0 -> x1, blocking collectives: none -> 15.6 us  [everywhere(): lax.all_to_all(copies, ('blk', 'gz'), 0, 0).reshape(-1, value.shape[-1])]
    ppermute x3 -> x1, starting transfers between devices: 9.16 us -> 2.4 us  [with_halo(): lax.ppermute(lax.slice_in_dim(block, block.shape[dim] - width, None, axis...]
    dot_general x4 -> x2, matrix products: 8.74 us -> 2.06 us  [along_cols(): return jnp.einsum('...y,yv->...v', field, matrix, precision=EXACT)]
    all_to_all x0 -> x1, waiting for transfers between devices: none -> 6.49 us  [everywhere(): lax.all_to_all(copies, ('blk', 'gz'), 0, 0).reshape(-1, value.shape[-1])]
    ppermute x3 -> x1, waiting for transfers between devices: 6.79 us -> 0.61 us  [with_halo(): lax.ppermute(lax.slice_in_dim(block, 0, width, axis=dim), axis, backward)]
    ppermute x3 -> x1, starting transfers between devices: 3.88 us -> 1.29 us  [with_halo(): lax.ppermute(lax.slice_in_dim(block, 0, width, axis=dim), axis, backward)]
    all_to_all x0 -> x1, starting transfers between devices: none -> 2.57 us  [everywhere(): lax.all_to_all(copies, ('blk', 'gz'), 0, 0).reshape(-1, value.shape[-1])]
  transfers between devices with their start and end apart: 6 -> 3, of which waited for: 3 -> 2; matrix products, arithmetic and copies ran while one was open for 2% -> 5% of each run, Pallas kernels for 0% -> 0%
where the time goes in v1:
time: 50.4 us; the launch traced here: 50.1 us
  blocking collectives  15.6 us (31%)
  matrix products  8.74 us (17%)
  waiting for transfers between devices  7.1 us (14%)
  starting transfers between devices  6.26 us (12%)
  other arithmetic  5.55 us (11%)
  between operations  3.84 us (8%)
  local copies, waits for them, and re-layouts  3 us (6%)
    all_to_all x1, blocking collectives, everywhere(): lax.all_to_all(copies, ('blk', 'gz'), 0, 0).reshape(-1, value.shape[-1])  15.6 us
    all_to_all x1, waiting for transfers between devices, everywhere(): lax.all_to_all(copies, ('blk', 'gz'), 0, 0).reshape(-1, value.shape[-1])  6.49 us
    all_to_all x1, starting transfers between devices, everywhere(): lax.all_to_all(copies, ('blk', 'gz'), 0, 0).reshape(-1, value.shape[-1])  2.57 us
    ppermute x1, starting transfers between devices, with_halo(): lax.ppermute(lax.slice_in_dim(block, block.shape[dim] - width, None, axis...  2.4 us
    dot_general x2, matrix products, along_cols(): return jnp.einsum('...y,yv->...v', field, matrix, precision=EXACT)  2.06 us
    dot_general x2, matrix products, per_device(): jnp.einsum('zk,sckxy->cszxy', depth_hat, partial_value, precision=EXACT)  1.78 us
    reduce_sum x2, other arithmetic, regularize(): jnp.mean(regular * regular) + EPSILON  1.45 us
    dot_general x2, matrix products, along_rows(): return jnp.einsum('...xy,xu->...uy', field, matrix, precision=EXACT)  1.41 us
  transfers between devices with their start and end apart: 3, of which 2 were waited for; matrix products, arithmetic and copies ran while one was open for 5% of the time, Pallas kernels for 0%

profile of v1, /device:TPU:0, one launch (start us, length us, event | category | flops | bytes accessed | tf_op | source)
XLA Modules:
  0.0 50.1 jit_solution(3341486113267290986)
XLA Ops:
  0.6 0.9 %copy_bitcast_fusion = (bf16[1,1,8,32,128]{4,2,3,1,0:T(8,128)(2,1)S(1)}, bf16[1,1,8,32,128]{4,2,3,1,0:T(8,128)(2,1)S(1)}) fusion(bf16[1,8,32,128]{3,2,1,0:T(8,128)(2,1)} %param.5, bf16[1,8,32,128]{3,2,1,0:T(8,128)(2,1)} %param.4), kind=kLoop, calls=%fused_computation.147 | loop fusion | bytes 262144 | tf_op jit(solution)/shard_map/stack | solution.py:131
  1.6 0.1 slice_maximum_fusion
  1.6 2.4 %collective-permute-start = (bf16[2,1,5,32,128]{4,2,3,1,0:T(8,128)(2,1)S(1)}, bf16[2,1,5,32,128]{4,2,3,1,0:T(8,128)(2,1)S(1)}, u32[]{:S(2)}, u32[]{:S(2)}) collective-permute-start(bf16[2,1,5,32,128]{4,2,3,1,0:T(8,128)(2,1)S(1)} %get-tuple-element.34), channel_id=1, source_target_pairs={{0,1},{1,2},{2,3},{4,5},{5,6},{6,7},{8,9},{9,10},{10,11},{12,13},{... | collective-permute-start | bytes 245768 | tf_op jit(solution)/shard_map/ppermute | solution.py:26
  4.0 1.3 %collective-permute-start.1 = (bf16[2,1,5,32,128]{4,2,3,1,0:T(8,128)(2,1)S(1)}, bf16[2,1,5,32,128]{4,2,3,1,0:T(8,128)(2,1)S(1)}, u32[]{:S(2)}, u32[]{:S(2)}) collective-permute-start(bf16[2,1,5,32,128]{4,2,3,1,0:T(8,128)(2,1)S(1)} %get-tuple-element.35), channel_id=1, source_target_pairs={{1,0},{2,1},{3,2},{5,4},{6,5},{7,6},{9,8},{10,9},{11,10},{13,12},{... | collective-permute-start | bytes 245768 | tf_op jit(solution)/shard_map/ppermute | solution.py:29
  6.8 0.1 add_reduce_fusion
  6.9 0.1 add_reduce_fusion.1
  7.0 0.2 add_reduce_fusion.2
  7.2 0.4 convolution_bitcast_fusion.4
  7.5 0.3 fusion.94
  7.9 0.9 %fusion.72 = f32[3,32,128,16]{2,3,1,0:T(8,128)S(1)} fusion(f32[3,2,32,128]{3,2,1,0:T(8,128)S(1)} %fusion.94, f32[16]{0:T(128)S(1)} %add_clamp_fusion, f32[2]{0:T(128)S(1)} %iota_convert_fusion.1), kind=kOutput, calls=%fused_computation.143 | convolution fusion | flops 4718720 | bytes 884808 | tf_op jit(solution)/shard_map/zk,sckxy->cszxy/dot_general | solution.py:170
  8.8 0.0 collective-permute-done
  8.8 0.6 %collective-permute-done.1 = bf16[2,1,5,32,128]{4,2,3,1,0:T(8,128)(2,1)S(1)} collective-permute-done((bf16[2,1,5,32,128]{4,2,3,1,0:T(8,128)(2,1)S(1)}, bf16[2,1,5,32,128]{4,2,3,1,0:T(8,128)(2,1)S(1)}, u32[]{:S(2)}, u32[]{:S(2)}) %collective-permute-start.1) | collective-permute-done | bytes 81952 | tf_op jit(solution)/shard_map/ppermute | solution.py:29
  9.4 0.2 maximum_convert_fusion
  9.6 0.1 slice_bitcast_fusion.4
  9.6 0.1 copy.144
  9.7 0.2 bitcast_dynamic-update-slice_fusion.5
  10.1 0.5 fusion.3
  10.6 0.7 %convolution_bitcast_fusion.2 = f32[5,8,32,128]{3,2,1,0:T(8,128)S(1)} fusion(f32[5,8,32,128]{3,1,2,0:T(8,128)S(1)} %fusion.3), kind=kOutput, calls=%fused_computation.2 | convolution fusion | flops 62942208 | bytes 1310720 | tf_op jit(solution)/shard_map/...xy,xu->...uy/dot_general | solution.py:45
  11.3 1.0 %fusion.6 = f32[5,8,32,128]{3,1,2,0:T(8,128)S(1)} fusion(f32[5,8,32,128]{3,2,1,0:T(8,128)S(1)} %convolution_bitcast_fusion.2), kind=kOutput, calls=%fused_computation.31 | convolution fusion | flops 252100608 | bytes 1310720 | tf_op jit(solution)/shard_map/...y,yv->...v/dot_general | solution.py:49
  12.3 0.2 fusion.64
  12.5 0.1 fusion.44
  12.6 0.5 fusion.10
  13.1 0.3 convolution_bitcast_fusion.6
  13.5 0.2 convolution_bitcast_fusion.8
  13.6 0.1 reshape.519
  13.7 0.1 maximum_bitcast_fusion.4
  13.8 15.6 %all_to_all.10 = f32[32,1,97]{2,1,0:T(1,128)S(1)} all-to-all(f32[32,1,97]{2,1,0:T(1,128)S(1)} %broadcast_in_dim.12), channel_id=1, replica_groups=mesh['blk'=8,'gz'=4] {'blk','gz'}, dimensions={0} | all-to-all | bytes 24832 | tf_op jit(solution)/shard_map/all_to_all | solution.py:117
  29.4 0.2 fusion.103
  29.6 0.1 fusion.101
  29.7 0.1 reshape.521
  29.8 0.1 reshape.522
  30.0 0.8 %multiply_reduce_fusion.1 = (f32[]{:T(128)}, f32[3,2,2,64]{3,2,1,0:T(2,128)S(1)}) fusion(f32[3,2,2,64]{3,2,1,0:T(2,128)S(1)} %fusion.140), kind=kLoop, calls=%fused_computation.249 | loop fusion | flops 5375 | bytes 6148 | tf_op jit(solution)/shard_map/reduce_sum | solution.py:103
  31.5 0.4 convolution_bitcast_fusion.3
  31.9 0.3 fusion.92
  32.2 0.9 %convolution_bitcast_fusion = f32[3,1,16,32,128]{4,2,3,1,0:T(8,128)S(1)} fusion(f32[3,2,32,128]{3,2,1,0:T(8,128)S(1)} %fusion.92, f32[16]{0:T(128)S(1)} %add_clamp_fusion, f32[2]{0:T(128)S(1)} %iota_convert_fusion.1), kind=kOutput, calls=%fused_computation | convolution fusion | flops 4718720 | bytes 884808 | tf_op jit(solution)/shard_map/zk,sckxy->cszxy/dot_general | solution.py:170
  33.1 0.2 bitcast_dynamic-update-slice_fusion.2
  33.4 0.5 fusion.1
  33.9 0.7 %convolution_bitcast_fusion.1 = f32[5,8,32,128]{3,2,1,0:T(8,128)S(1)} fusion(f32[5,8,32,128]{3,1,2,0:T(8,128)S(1)} %fusion.1), kind=kOutput, calls=%fused_computation.1 | convolution fusion | flops 62942208 | bytes 1310720 | tf_op jit(solution)/shard_map/...xy,xu->...uy/dot_general | solution.py:45
  34.6 1.0 %fusion.4 = f32[5,8,32,128]{3,1,2,0:T(8,128)S(1)} fusion(f32[5,8,32,128]{3,2,1,0:T(8,128)S(1)} %convolution_bitcast_fusion.1), kind=kOutput, calls=%fused_computation.29 | convolution fusion | flops 252100608 | bytes 1310720 | tf_op jit(solution)/shard_map/...y,yv->...v/dot_general | solution.py:49
  35.7 0.1 multiply_divide_fusion
  35.7 0.1 fusion.59
  35.9 0.1 fusion.48
  36.0 0.5 fusion.15
  36.5 0.3 convolution_bitcast_fusion.5
  36.8 0.2 convolution_bitcast_fusion.7
  37.0 0.1 reshape.528
  37.1 0.1 maximum_bitcast_fusion.5
  37.2 0.6 %broadcast_in_dim.14 = f32[32,1,97]{2,1,0:T(1,128)} broadcast(f32[97]{0:T(128)S(1)} %maximum_bitcast_fusion.5), dimensions={2} | broadcast | bytes 12804 | tf_op jit(solution)/shard_map/broadcast_in_dim | solution.py:116
  37.8 2.6 %all-to-all-start.1 = ((f32[32,1,97]{2,1,0:T(1,128)}), f32[32,1,97]{2,1,0:T(1,128)S(1)}, u32[]{:S(2)}, u32[]{:S(2)}) async-start(f32[32,1,97]{2,1,0:T(1,128)} %broadcast_in_dim.14), calls=%async_computation.1 | async-start | bytes 32768 | tf_op jit(solution)/shard_map/all_to_all | solution.py:117
  40.4 0.7 %copy.105 = f32[1,8,32,128]{3,2,1,0:T(8,128)} copy(f32[1,8,32,128]{3,1,2,0:T(8,128)S(1)} %get-tuple-element.10) | data formatting | bytes 262144
  41.0 6.5 %all-to-all-done.1 = f32[32,1,97]{2,1,0:T(1,128)S(1)} async-done(((f32[32,1,97]{2,1,0:T(1,128)}), f32[32,1,97]{2,1,0:T(1,128)S(1)}, u32[]{:S(2)}, u32[]{:S(2)}) %all-to-all-start.1) | async-done | bytes 12448 | tf_op jit(solution)/shard_map/all_to_all | solution.py:117
  47.5 0.2 fusion.100
  47.7 0.1 fusion.98
  47.8 0.1 reshape.530
  48.0 0.1 reshape.531
  48.1 0.7 %multiply_reduce_fusion = (f32[]{:T(128)}, f32[3,2,2,64]{3,2,1,0:T(2,128)S(1)}) fusion(f32[3,2,2,64]{3,2,1,0:T(2,128)S(1)} %fusion.144), kind=kLoop, calls=%fused_computation.247 | loop fusion | flops 5375 | bytes 6148 | tf_op jit(solution)/shard_map/reduce_sum | solution.py:103
  49.5 0.6 %divide_add_fusion = f32[3,2,2,64]{3,2,1,0:T(2,128)} fusion(f32[3,2,2,64]{3,2,1,0:T(2,128)S(1)} %get-tuple-element.13, f32[]{:T(128)S(6)} %sqrt.7, f32[]{:T(128)S(6)} %sqrt.6, f32[3,2,2,64]{3,2,1,0:T(2,128)S(1)} %get-tuple-element.19), kind=kLoop, calls=%fused_computation.230 | loop fusion | flops 3840 | bytes 9224 | tf_op jit(solution)/shard_map/add | solution.py:103
  (25 shorter events, 0.3 us)
Async XLA Ops:
  1.6 7.2 %collective-permute-start = (bf16[2,1,5,32,128]{4,2,3,1,0:T(8,128)(2,1)S(1)}, bf16[2,1,5,32,128]{4,2,3,1,0:T(8,128)(2,1)S(1)}, u32[]{:S(2)}, u32[]{:S(2)}) collective-permute-start(bf16[2,1,5,32,128]{4,2,3,1,0:T(8,128)(2,1)S(1)} %get-tuple-element.34), channel_id=1, source_target_pairs={{0,1},{1,2},{2,3},{4,5},{5,6},{6,7},{8,9},{9,10},{10,11},{12,13},{... | collective-permute-start | bytes 245768 | tf_op jit(solution)/shard_map/ppermute | solution.py:26
  4.0 5.4 %collective-permute-start.1 = (bf16[2,1,5,32,128]{4,2,3,1,0:T(8,128)(2,1)S(1)}, bf16[2,1,5,32,128]{4,2,3,1,0:T(8,128)(2,1)S(1)}, u32[]{:S(2)}, u32[]{:S(2)}) collective-permute-start(bf16[2,1,5,32,128]{4,2,3,1,0:T(8,128)(2,1)S(1)} %get-tuple-element.35), channel_id=1, source_target_pairs={{1,0},{2,1},{3,2},{5,4},{6,5},{7,6},{9,8},{10,9},{11,10},{13,12},{... | collective-permute-start | bytes 245768 | tf_op jit(solution)/shard_map/ppermute | solution.py:29
  37.8 9.7 %all-to-all-start.1 = ((f32[32,1,97]{2,1,0:T(1,128)}), f32[32,1,97]{2,1,0:T(1,128)S(1)}, u32[]{:S(2)}, u32[]{:S(2)}) async-start(f32[32,1,97]{2,1,0:T(1,128)} %broadcast_in_dim.14), calls=%async_computation.1 | async-start | bytes 32768 | tf_op jit(solution)/shard_map/all_to_all | solution.py:117

commit v2 on v0

v2 whole, which is shorter than its diff:
```python
import functools
import math

import jax
import jax.numpy as jnp
import numpy as np
from jax import lax
from jax.experimental import pallas as pl
from jax.experimental.pallas import tpu as pltpu
from jax.sharding import PartitionSpec as P

SCALE = 16
GY = 8
EPSILON = 1e-05
STEP_LENGTH = 0.5
GAUSS_RAW = [math.exp(-((offset - 3) ** 2) / 4.5) for offset in range(7)]
GAUSS_TAPS = [value / sum(GAUSS_RAW) for value in GAUSS_RAW]
REACH = 4
LANES = 128
F32 = jnp.float32
BF16 = jnp.bfloat16


def cell_weights(length):
    table = np.zeros((length // SCALE, length))
    for target in range(length):
        for offset, weight in enumerate(GAUSS_TAPS):
            source = target - (offset - 3)
            if 0 <= source < length:
                table[target // SCALE, source] += weight
    return table


def hat_table(length):
    count = length // SCALE
    where = np.clip((np.arange(length) + 0.5) / SCALE - 0.5, 0.0, count - 1.0)
    return np.maximum(0.0, 1.0 - np.abs(where[None, :] - np.arange(count)[:, None]))


def tables(parts, planes, row_side, col_side):
    total = parts * planes
    coarse = total // SCALE
    hats = np.zeros((coarse, total + 2 * REACH))
    hats[:, REACH : REACH + total] = hat_table(total)
    cells = cell_weights(total)
    wide = planes + 2 * REACH
    depth = np.stack(
        [
            np.concatenate(
                [hats[:, g * planes : g * planes + wide].reshape(-1)]
                + [cells[:, g * planes : (g + 1) * planes].reshape(-1)]
            )
            for g in range(parts)
        ]
    )
    depth = np.broadcast_to(depth[:, :, None], depth.shape + (LANES,))
    rows = np.broadcast_to(cell_weights(row_side)[:, :, None], (row_side // SCALE, row_side, LANES))
    cols = np.tile(cell_weights(col_side).T, (1, LANES // (col_side // SCALE)))
    band = np.abs(np.arange(col_side)[:, None] - np.arange(col_side)[None, :]) <= 4
    box = np.kron(np.eye(2), band)
    slope = np.zeros((col_side, col_side))
    for i in range(col_side - 1):
        slope[i + 1, i] = 0.5
        slope[i, i + 1] = -0.5
    return (
        np.asarray(depth, np.float32),
        np.asarray(rows, np.float32),
        np.asarray(cols, np.float32),
        jnp.asarray(box, BF16),
        jnp.asarray(slope, BF16),
    )


def spread_table(groups, coarse_rows, coarse_cols):
    lanes = np.arange(LANES)
    a, l = lanes // (GY * coarse_cols), lanes % (GY * coarse_cols)
    table = np.zeros((groups, LANES, LANES), np.float32)
    for g in range(groups):
        table[g, (g * coarse_rows + a) * coarse_cols + l % coarse_cols, lanes] = 1.0
    return table


def lane_index(shape):
    return lax.broadcasted_iota(jnp.int32, shape, len(shape) - 1)


def sublane_index(shape):
    return lax.broadcasted_iota(jnp.int32, shape, len(shape) - 2)


def tail(plane):
    return jnp.concatenate([plane, jnp.zeros((8, plane.shape[1]), plane.dtype)], axis=0)


def window_of_nine(items):
    two = [a + b for a, b in zip(items[:-1], items[1:])]
    four = [a + b for a, b in zip(two[:-2], two[2:])]
    eight = [a + b for a, b in zip(four[:-4], four[4:])]
    return [a + b for a, b in zip(eight[:-1], items[8:])]


def row_box(plane):
    side = plane.shape[0]
    padded = tail(plane)
    total = padded + pltpu.roll(padded, 1, 0)
    total = total + pltpu.roll(total, 2, 0)
    total = total + pltpu.roll(total, 4, 0)
    total = total + pltpu.roll(padded, 8, 0)
    return pltpu.roll(total, side + 8 - 4, 0)[:side]


def row_slope(plane):
    side = plane.shape[0]
    padded = tail(plane)
    return 0.5 * (pltpu.roll(padded, side + 7, 0)[:side] - pltpu.roll(padded, 1, 0)[:side])


def col_slope(plane):
    width = plane.shape[1]
    lane = lane_index(plane.shape)
    upper = jnp.where(lane < width - 1, pltpu.roll(plane, width - 1, 1), 0.0)
    lower = jnp.where(lane > 0, pltpu.roll(plane, 1, 1), 0.0)
    return 0.5 * (upper - lower)


def load_images(odd, fixed_ref, moving_ref, near_ref, far_ref, image, shifted):
    planes = fixed_ref.shape[1]
    image[REACH : REACH + planes] = fixed_ref[0].astype(F32)
    shifted[REACH + 1 : REACH + 1 + planes] = moving_ref[0].astype(F32)
    near = near_ref[...].astype(F32)
    far = far_ref[...].astype(F32)
    low = jnp.where(odd, near, far)
    high = jnp.where(odd, far, near)
    image[0:REACH] = low[0:REACH]
    image[REACH + planes :] = high[0:REACH]
    shifted[0 : REACH + 1] = low[REACH:]
    shifted[REACH + 1 + planes :] = high[REACH:]


def box_sums(fields, planes, side, sums, parts, box_ref):
    half = planes // 2
    count = 0
    for tile in range(side // 8):
        rows = slice(8 * tile, 8 * tile + 8)
        lists = fields(rows)
        count = len(lists)
        for f, items in enumerate(lists):
            for z, item in enumerate(window_of_nine(items)):
                sums[f, z, rows] = item
    for f in range(count):
        for z in range(planes):
            total = row_box(sums[f, z])
            rows = slice((f * half + z % half) * side, (f * half + z % half + 1) * side)
            lanes = slice((z // half) * LANES, (z // half + 1) * LANES)
            for part in range(3):
                rounded = total.astype(BF16)
                parts[part, rows, lanes] = rounded
                total = total - rounded.astype(F32)
    used = slice(0, count * half * side)
    box = box_ref[...]
    result = jnp.dot(parts[0, used], box, preferred_element_type=F32)
    result = result + jnp.dot(parts[1, used], box, preferred_element_type=F32)
    result = result + jnp.dot(parts[2, used], box, preferred_element_type=F32)

    def of(f, z):
        start = (f * half + z % half) * side
        lane = (z // half) * LANES
        return result[start : start + side, lane : lane + LANES]

    return of


def force_message(weights, warped, planes, depth_ref, part, rows_ref, cols_ref, mark, tissue):
    coarse = depth_ref.shape[1] // (2 * planes + 2 * REACH)
    first = coarse * (planes + 2 * REACH)
    coarse_rows, side, _ = rows_ref.shape
    total = [[None] * coarse for _ in range(3)]
    for z in range(planes):
        plane = warped(z)
        slopes = (0.5 * (warped(z + 1) - warped(z - 1)), row_slope(plane), col_slope(plane))
        for k in range(coarse):
            index = first + k * planes + z
            share = weights(z) * depth_ref[part, index : index + 1, :]
            for c in range(3):
                term = share * slopes[c]
                total[c][k] = term if z == 0 else total[c][k] + term
    tiles = []
    for c in range(3):
        for k in range(coarse):
            for a in range(coarse_rows):
                product = total[c][k] * rows_ref[a]
                tile = product[0:8]
                for start in range(8, side, 8):
                    tile = tile + product[start : start + 8]
                tiles.append(tile)
    sums = jnp.dot(
        jnp.concatenate(tiles, axis=0),
        cols_ref[...],
        precision=lax.Precision.HIGHEST,
        preferred_element_type=F32,
    )
    coarse_cols = LANES // SCALE
    lane = lane_index((8, LANES))
    picked = jnp.zeros((8, LANES), F32)
    for g in range(len(tiles)):
        picked = jnp.where(lane // coarse_cols == g, sums[8 * g : 8 * g + 8], picked)
    row = jnp.sum(picked, axis=0, keepdims=True) * tissue
    return jnp.where(lane[0:1] == len(tiles) * coarse_cols, mark, row)


def regular_grid(received, spread_ref, block_rows, coarse_rows, coarse_cols):
    groups = spread_ref.shape[0]
    used = groups * coarse_rows * coarse_cols
    width = GY * coarse_cols
    place = received[:, used : used + 1].astype(jnp.int32)
    lane = lane_index(received.shape)
    here = (place % GY) == (lane % width) // coarse_cols
    block_row = place // GY
    sub = sublane_index((8, LANES))
    grids = [jnp.zeros((8, LANES), F32) for _ in range(block_rows)]
    for g in range(groups):
        entry = jnp.dot(
            received, spread_ref[g], precision=lax.Precision.HIGHEST, preferred_element_type=F32
        )
        for r in range(block_rows):
            chosen = here if block_rows == 1 else here & (block_row == r)
            total = jnp.sum(jnp.where(chosen, entry, 0.0), axis=0, keepdims=True)
            grids[r] = jnp.where(sub == g, total, grids[r])
    even = sub % 2 == 0
    lane = lane_index((8, LANES))
    column = lane % width
    first = lane < width
    grids = [
        0.5 * g + 0.25 * jnp.where(even, pltpu.roll(g, 7, 0), pltpu.roll(g, 1, 0)) for g in grids
    ]
    other = [pltpu.roll(g, width, 1) for g in grids]
    none = jnp.zeros((8, LANES), F32)
    before = [none] + other[:-1]
    after = other[1:] + [none]
    grids = [
        0.5 * g + 0.25 * (o + jnp.where(first, b, a))
        for g, o, b, a in zip(grids, other, before, after)
    ]
    grids = [
        0.25 * jnp.where(column > 0, pltpu.roll(g, 1, 1), 0.0)
        + 0.5 * g
        + 0.25 * jnp.where(column < width - 1, pltpu.roll(g, LANES - 1, 1), 0.0)
        for g in grids
    ]
    grids = [jnp.where(sub < groups, g, 0.0) for g in grids]
    square = functools.reduce(lambda a, b: a + b, [g * g for g in grids])
    square = jnp.sum(jnp.sum(square, axis=1, keepdims=True), axis=0, keepdims=True)
    mean = square * (1.0 / (groups * block_rows * LANES))
    factor = STEP_LENGTH / jnp.sqrt(mean + EPSILON)
    return [g * factor for g in grids]


def pack_kernel(fixed_ref, moving_ref, near_ref, far_ref):
    planes = fixed_ref.shape[1]
    odd = lax.axis_index("gz") % 2
    for ref, low in ((near_ref, odd == 1), (far_ref, odd == 0)):
        ref[0:REACH] = fixed_ref[0, pl.ds(jnp.where(low, 0, planes - REACH), REACH)]
        ref[REACH:] = moving_ref[0, pl.ds(jnp.where(low, 0, planes - REACH - 1), REACH + 1)]


def first_kernel(
    fixed_ref, moving_ref, near_ref, far_ref, place_ref, tissue_ref,
    depth_ref, rows_ref, cols_ref, box_ref,
    message_ref, mean_ref, variance_ref,
    image, shifted, sums, parts, weight,
):
    _, planes, side, _ = fixed_ref.shape
    part = lax.axis_index("gz")
    load_images(part % 2 == 1, fixed_ref, moving_ref, near_ref, far_ref, image, shifted)
    wide = planes + 2 * REACH

    def fields(rows):
        i = [image[z, rows] for z in range(wide)]
        w = [shifted[z + 1, rows] for z in range(wide)]
        return (
            i,
            w,
            [a * a for a in i],
            [b * b for b in w],
            [a * b for a, b in zip(i, w)],
        )

    of = box_sums(fields, planes, side, sums, parts, box_ref)
    for z in range(planes):
        mean_i, mean_w, mean_ii, mean_ww, mean_iw = [of(f, z) * (1.0 / 729.0) for f in range(5)]
        sii = mean_ii - mean_i * mean_i
        sww = mean_ww - mean_w * mean_w
        siw = mean_iw - mean_i * mean_w
        mean_ref[z] = mean_i
        variance_ref[z] = sii
        ratio = siw / (sii * sww + EPSILON)
        weight[z] = (2.0 * ratio) * (
            (image[z + REACH] - mean_i)
            - siw / (sww + EPSILON) * (shifted[z + REACH + 1] - mean_w)
        )
    row = force_message(
        lambda z: weight[z],
        lambda z: shifted[z + REACH + 1],
        planes, depth_ref, part, rows_ref, cols_ref,
        place_ref[...].astype(F32), tissue_ref[...].astype(F32),
    )
    message_ref[...] = jnp.broadcast_to(row[None], message_ref.shape)


def second_kernel(
    received_ref, fixed_ref, moving_ref, near_ref, far_ref, place_ref, tissue_ref,
    mean_ref, variance_ref, depth_ref, rows_ref, cols_ref, box_ref, slope_ref, spread_ref,
    message_ref, map_ref, velocity_ref,
    image, shifted, warped, sums, parts, weight,
):
    _, planes, side, _ = fixed_ref.shape
    part = lax.axis_index("gz")
    load_images(part % 2 == 1, fixed_ref, moving_ref, near_ref, far_ref, image, shifted)
    wide = planes + 2 * REACH
    coarse_rows = rows_ref.shape[0]
    coarse_cols = LANES // SCALE
    block_rows = velocity_ref.shape[0] // 8
    coarse = depth_ref.shape[1] // (2 * planes + 2 * REACH)
    width = GY * coarse_cols

    grids = regular_grid(received_ref[...], spread_ref, block_rows, coarse_rows, coarse_cols)
    for r in range(block_rows):
        velocity_ref[8 * r : 8 * r + 8] = grids[r]

    place = place_ref[...]
    row_of, col_of = place // GY, place % GY
    y = (lane_index((1, LANES)) + col_of * LANES).astype(F32)
    where_y = jnp.clip((y + 0.5) * (1.0 / SCALE) - 0.5, 0.0, width - 1.0)
    entry = sublane_index((LANES, LANES))
    hat_y = jnp.maximum(0.0, 1.0 - jnp.abs(where_y - (entry % width).astype(F32)))
    hat_y = jnp.concatenate(
        [jnp.where(entry // width == a, hat_y, 0.0) for a in range(coarse_rows)], axis=1
    )
    along = jnp.dot(
        jnp.concatenate(grids, axis=0),
        hat_y,
        precision=lax.Precision.HIGHEST,
        preferred_element_type=F32,
    )
    x = (sublane_index((side, LANES)) + row_of * side).astype(F32)
    where_x = jnp.clip((x + 0.5) * (1.0 / SCALE) - 0.5, 0.0, block_rows * coarse_rows - 1.0)
    shift = [[jnp.zeros((side, LANES), F32) for _ in range(coarse)] for _ in range(3)]
    for r in range(block_rows):
        for a in range(coarse_rows):
            hat_x = jnp.maximum(0.0, 1.0 - jnp.abs(where_x - float(r * coarse_rows + a)))
            for c in range(3):
                for k in range(coarse):
                    g = 8 * r + c * coarse + k
                    line = along[g : g + 1, a * LANES : (a + 1) * LANES]
                    shift[c][k] = shift[c][k] + hat_x * line
    for z in range(wide):
        plane = shifted[z + 1]
        slopes = (
            0.5 * (shifted[z + 2] - shifted[z]),
            row_slope(plane),
            jnp.dot(plane.astype(BF16), slope_ref[...], preferred_element_type=F32),
        )
        hats = [depth_ref[part, k * wide + z : k * wide + z + 1, :] for k in range(coarse)]
        for c in range(3):
            u = hats[0] * shift[c][0]
            for k in range(1, coarse):
                u = u + hats[k] * shift[c][k]
            plane = plane + u * slopes[c]
        warped[z] = plane

    def fields(rows):
        i = [image[z, rows] for z in range(wide)]
        w = [warped[z, rows] for z in range(wide)]
        return (w, [b * b for b in w], [a * b for a, b in zip(i, w)])

    of = box_sums(fields, planes, side, sums, parts, box_ref)
    for z in range(planes):
        mean_w, mean_ww, mean_iw = [of(f, z) * (1.0 / 729.0) for f in range(3)]
        mean_i = mean_ref[z]
        sii = variance_ref[z]
        sww = mean_ww - mean_w * mean_w
        siw = mean_iw - mean_i * mean_w
        ratio = siw / (sii * sww + EPSILON)
        map_ref[0, z] = siw * ratio
        weight[z] = (2.0 * ratio) * (
            (image[z + REACH] - mean_i) - siw / (sww + EPSILON) * (warped[z + REACH] - mean_w)
        )
    row = force_message(
        lambda z: weight[z],
        lambda z: warped[z + REACH],
        planes, depth_ref, part, rows_ref, cols_ref,
        place.astype(F32), tissue_ref[...].astype(F32),
    )
    message_ref[...] = jnp.broadcast_to(row[None], message_ref.shape)


def last_kernel(received_ref, velocity_ref, spread_ref, out_ref):
    _, coarse, rows, width = out_ref.shape
    coarse_rows = LANES // width
    block_rows = rows // coarse_rows
    grids = regular_grid(
        received_ref[...], spread_ref, block_rows, coarse_rows, width // GY
    )
    for r in range(block_rows):
        velocity = velocity_ref[8 * r : 8 * r + 8] + grids[r]
        for c in range(3):
            for k in range(coarse):
                g = c * coarse + k
                for a in range(coarse_rows):
                    out_ref[c, k, r * coarse_rows + a : r * coarse_rows + a + 1, :] = velocity[
                        g : g + 1, a * width : (a + 1) * width
                    ]


def call(kernel, outs, scratch, *operands):
    vmem = pl.BlockSpec(memory_space=pltpu.VMEM)
    return pl.pallas_call(
        kernel,
        out_shape=[jax.ShapeDtypeStruct(shape, dtype) for shape, dtype in outs],
        in_specs=[vmem] * len(operands),
        out_specs=[vmem] * len(outs),
        scratch_shapes=[pltpu.VMEM(shape, dtype) for shape, dtype in scratch],
        compiler_params=pltpu.CompilerParams(vmem_limit_bytes=24 << 20),
    )(*operands)


def per_device(fixed, moving, block_place, tissue):
    slots, planes, side, width = fixed.shape
    assert slots == 1 and width == LANES
    depth_parts = lax.axis_size("gz")
    devices = lax.axis_size("blk") * depth_parts
    blocks = slots * lax.axis_size("blk")
    coarse = planes * depth_parts // SCALE
    coarse_rows, coarse_cols = side // SCALE, width // SCALE
    block_rows = blocks // GY
    place = block_place.reshape(1, 1)
    mask = tissue.reshape(1, 1)
    depth, rows, cols, box, slope = tables(depth_parts, planes, side, width)
    spread = spread_table(3 * coarse, coarse_rows, coarse_cols)

    near, far = call(
        pack_kernel, [((2 * REACH + 1, side, width), BF16)] * 2, [], fixed, moving
    )
    pairs = [(i, i + 1) for i in range(0, depth_parts - 1, 2)]
    near = lax.ppermute(near, "gz", pairs + [(b, a) for a, b in pairs])
    pairs = [(i, i + 1) for i in range(1, depth_parts - 1, 2)]
    far = lax.ppermute(far, "gz", pairs + [(b, a) for a, b in pairs])

    wide = planes + 2 * REACH
    field = (planes, side, width)
    message = ((devices, 1, LANES), F32)

    def scratch(fields):
        return [
            ((fields, planes, side, width), F32),
            ((3, fields * planes * side // 2, 2 * width), BF16),
            (field, F32),
        ]

    images = [((wide, side, width), F32), ((wide + 2, side, width), F32)]
    sent, mean, variance = call(
        first_kernel, [message, (field, F32), (field, F32)], images + scratch(5),
        fixed, moving, near, far, place, mask, depth, rows, cols, box,
    )
    received = lax.all_to_all(sent, ("blk", "gz"), 0, 0).reshape(devices, LANES)
    sent, correlation, velocity = call(
        second_kernel,
        [message, ((1,) + field, F32), ((8 * block_rows, LANES), F32)],
        images + [((wide, side, width), F32)] + scratch(3),
        received, fixed, moving, near, far, place, mask,
        mean, variance, depth, rows, cols, box, slope, spread,
    )
    received = lax.all_to_all(sent, ("blk", "gz"), 0, 0).reshape(devices, LANES)
    (velocity,) = call(
        last_kernel,
        [((3, coarse, block_rows * coarse_rows, GY * coarse_cols), F32)],
        [],
        received, velocity, spread,
    )
    return (velocity, correlation)


def solution(mesh):
    return jax.shard_map(
        per_device,
        mesh=mesh,
        in_specs=(P("blk", "gz", None, None), P("blk", "gz", None, None), P("blk"), P("blk")),
        out_specs=(P(), P("blk", "gz", None, None)),
        check_vma=False,
    )
```

time: 133 us -> 40.5 us (0.30)
  blocking collectives: 85.5 us -> 26.4 us
  matrix products: 14.5 us -> 0 us
  starting transfers between devices: 13 us -> 1.21 us
  waiting for transfers between devices: 6.79 us -> 0.01 us
  other arithmetic: 5.8 us -> 0 us
  Pallas kernels: 0 us -> 5.3 us
  local copies, waits for them, and re-layouts: 2.56 us -> 5.12 us
  between operations: 3.86 us -> 2 us
    psum x2 -> x0, blocking collectives: 85.5 us -> none  [per_device(): total = lax.psum(local_grid, ('blk', 'gz'))]
    all_to_all x0 -> x2, blocking collectives: none -> 26.4 us  [per_device(): received = lax.all_to_all(sent, ('blk', 'gz'), 0, 0).reshape(devices, LANES)]
    dot_general x16 -> x0, matrix products: 14.5 us -> none  [the longest x4 8.74 us: along_cols(): return jnp.einsum('...y,yv->...v', field, matrix, precision=EXACT)]
    ppermute x6 -> x2, starting transfers between devices: 13 us -> 1.21 us  [the longest x1 0.65 us: per_device(): far = lax.ppermute(far, 'gz', pairs + [(b, a) for a, b in pairs])]
    ppermute x6 -> x2, waiting for transfers between devices: 6.79 us -> 0.01 us  [the longest x1 0.01 us: per_device(): near = lax.ppermute(near, 'gz', pairs + [(b, a) for a, b in pairs])]
    pallas_call x0 -> x4, Pallas kernels: none -> 5.3 us  [call(): pl.pallas_call(kernel, out_shape=[jax.ShapeDtypeStruct(shape, dtype) for...]
    unnamed x2 -> x16, local copies, waits for them, and re-layouts: 0.81 us -> 5.12 us
    another operation x14 -> x0, other arithmetic: 2.37 us -> none
  transfers between devices with their start and end apart: 6 -> 2, of which waited for: 3 -> 0; matrix products, arithmetic and copies ran while one was open for 2% -> 0% of each run, Pallas kernels for 0% -> 0%
where the time goes in v2:
time: 40.5 us; the launch traced here: 40 us
  blocking collectives  26.4 us (65%)
  Pallas kernels  5.3 us (13%)
  local copies, waits for them, and re-layouts  5.12 us (13%)
  between operations  2 us (5%)
  starting transfers between devices  1.21 us (3%)
    all_to_all x2, blocking collectives, per_device(): received = lax.all_to_all(sent, ('blk', 'gz'), 0, 0).reshape(devices, LANES)  26.4 us
    pallas_call x4, Pallas kernels, call(): pl.pallas_call(kernel, out_shape=[jax.ShapeDtypeStruct(shape, dtype) for...  5.3 us
    unnamed x16, local copies, waits for them, and re-layouts  5.12 us
  transfers between devices with their start and end apart: 2, of which 0 were waited for; matrix products, arithmetic and copies ran while one was open for 0% of the time, Pallas kernels for 0%

profile of v2, /device:TPU:0, one launch (start us, length us, event | category | flops | bytes accessed | tf_op | source)
XLA Modules:
  0.0 40.0 jit_solution(6696891754955886584)
XLA Ops:
  0.6 0.0 copy-start
  0.6 0.0 copy-start.1
  0.7 0.9 %copy-done.1 = bf16[1,8,32,128]{3,2,1,0:T(8,128)(2,1)S(1)} copy-done((bf16[1,8,32,128]{3,2,1,0:T(8,128)(2,1)S(1)}, bf16[1,8,32,128]{3,2,1,0:T(8,128)(2,1)}, u32[]{:S(2)}) %copy-start.1) | copy-done | bytes 65560
  1.5 0.0 copy-start.2
  1.5 0.8 %copy-done.2 = bf16[1,8,32,128]{3,2,1,0:T(8,128)(2,1)S(1)} copy-done((bf16[1,8,32,128]{3,2,1,0:T(8,128)(2,1)S(1)}, bf16[1,8,32,128]{3,2,1,0:T(8,128)(2,1)}, u32[]{:S(2)}) %copy-start.2) | copy-done | bytes 65560
  2.4 0.6 %collective-permute-start = (bf16[9,32,128]{2,1,0:T(8,128)(2,1)S(1)}, bf16[9,32,128]{2,1,0:T(8,128)(2,1)S(1)}, u32[]{:S(2)}, u32[]{:S(2)}) collective-permute-start(bf16[9,32,128]{2,1,0:T(8,128)(2,1)S(1)} %get-tuple-element.10), channel_id=1, source_target_pairs={{0,1},{2,3},{1,0},{3,2},{4,5},{6,7},{5,4},{7,6},{8,9},{10,11},{9,8... | collective-permute-start | bytes 221192 | tf_op jit(solution)/shard_map/ppermute | solution.py:445
  2.9 0.7 %collective-permute-start.1 = (bf16[9,32,128]{2,1,0:T(8,128)(2,1)S(1)}, bf16[9,32,128]{2,1,0:T(8,128)(2,1)S(1)}, u32[]{:S(2)}, u32[]{:S(2)}) collective-permute-start(bf16[9,32,128]{2,1,0:T(8,128)(2,1)S(1)} %get-tuple-element.11), channel_id=1, source_target_pairs={{1,2},{2,1},{5,6},{6,5},{9,10},{10,9},{13,14},{14,13},{17,18},{18,... | collective-permute-start | bytes 221192 | tf_op jit(solution)/shard_map/ppermute | solution.py:447
  4.9 0.0 collective-permute-done.near_ref
  4.9 0.0 collective-permute-done.1.far_ref
  4.9 0.0 copy-start.3
  4.9 0.9 %copy-done.3 = bf16[256,256]{1,0:T(8,128)(2,1)S(1)} copy-done((bf16[256,256]{1,0:T(8,128)(2,1)S(1)}, bf16[256,256]{1,0:T(8,128)(2,1)}, u32[]{:S(2)}) %copy-start.3) | copy-done | bytes 131096
  5.8 0.0 copy-start.4
  5.8 0.9 %copy-done.4 = f32[4,48,128]{2,1,0:T(8,128)S(1)} copy-done((f32[4,48,128]{2,1,0:T(8,128)S(1)}, f32[4,48,128]{2,1,0:T(8,128)}, u32[]{:S(2)}) %copy-start.4) | copy-done | bytes 98328
  6.7 0.0 copy-start.5
  6.7 0.8 %copy-done.5 = f32[128,128]{1,0:T(8,128)S(1)} copy-done((f32[128,128]{1,0:T(8,128)S(1)}, f32[128,128]{1,0:T(8,128)}, u32[]{:S(2)}) %copy-start.5) | copy-done | bytes 65560
  7.6 0.0 copy-start.6
  7.6 0.8 %copy-done.6 = f32[2,32,128]{2,1,0:T(8,128)S(1)} copy-done((f32[2,32,128]{2,1,0:T(8,128)S(1)}, f32[2,32,128]{2,1,0:T(8,128)}, u32[]{:S(2)}) %copy-start.6) | copy-done | bytes 32792
  8.3 1.4 %shard_map.114 = (f32[32,1,128]{2,1,0:T(1,128)S(1)}, f32[8,32,128]{2,1,0:T(8,128)S(1)}, f32[8,32,128]{2,1,0:T(8,128)S(1)}) custom-call(bf16[1,8,32,128]{3,2,1,0:T(8,128)(2,1)S(1)} %copy-done.1, bf16[1,8,32,128]{3,2,1,0:T(8,128)(2,1)S(1)} %copy-done.2, bf16[9,32,128]{2,1,0:T(8,128)(2,1)S(1)} %collective-permute-done.near_ref, ...), custom_call_target="tpu_custom_call" | custom-call | tf_op jit(solution)/shard_map/pallas_call | solution.py:417
  9.8 0.0 copy-start.7
  9.8 17.5 %all_to_all.10 = f32[32,1,128]{2,1,0:T(1,128)S(1)} all-to-all(f32[32,1,128]{2,1,0:T(1,128)S(1)} %get-tuple-element.12), channel_id=1, replica_groups=mesh['blk'=8,'gz'=4] {'blk','gz'}, dimensions={0} | all-to-all | bytes 32768 | tf_op jit(solution)/shard_map/all_to_all | solution.py:465
  27.3 0.0 copy-done
  27.3 0.0 copy-done.7
  27.3 2.5 %shard_map.115 = (f32[32,1,128]{2,1,0:T(1,128)S(1)}, f32[1,8,32,128]{3,2,1,0:T(8,128)}, f32[8,128]{1,0:T(8,128)S(1)}) custom-call(f32[32,128]{1,0:T(8,128)S(1)} %bitcast.8, bf16[1,8,32,128]{3,2,1,0:T(8,128)(2,1)S(1)} %copy-done.1, bf16[1,8,32,128]{3,2,1,0:T(8,128)(2,1)S(1)} %copy-done.2, bf16[9,32,128]{2,1,0:T(8,128)(2,1)S(1)} %collective-permute-done.near_ref, ...), custom_call_target="tpu_custom_call" | custom-call | tf_op jit(solution)/shard_map/pallas_call | solution.py:417
  29.8 8.9 %all_to_all.11 = f32[32,1,128]{2,1,0:T(1,128)S(1)} all-to-all(f32[32,1,128]{2,1,0:T(1,128)S(1)} %get-tuple-element.15), channel_id=1, replica_groups=mesh['blk'=8,'gz'=4] {'blk','gz'}, dimensions={0} | all-to-all | bytes 32768 | tf_op jit(solution)/shard_map/all_to_all | solution.py:473
  38.7 1.3 %shard_map.116 = f32[3,2,2,64]{3,2,1,0:T(2,128)} custom-call(f32[32,128]{1,0:T(8,128)S(1)} %bitcast.9, f32[8,128]{1,0:T(8,128)S(1)} %get-tuple-element.16.velocity_ref, f32[6,128,128]{2,1,0:T(8,128)S(1)} %copy-done), custom_call_target="tpu_custom_call" | custom-call | tf_op jit(solution)/shard_map/pallas_call | solution.py:417
  (1 shorter events, 0.0 us)
Async XLA Ops:
  0.6 26.7 %copy-start = (f32[6,128,128]{2,1,0:T(8,128)S(1)}, f32[6,128,128]{2,1,0:T(8,128)}, u32[]{:S(2)}) copy-start(f32[6,128,128]{2,1,0:T(8,128)} %constant.17.clone.spread_ref) | copy-start | bytes 1179652
  0.6 0.9 %copy-start.1 = (bf16[1,8,32,128]{3,2,1,0:T(8,128)(2,1)S(1)}, bf16[1,8,32,128]{3,2,1,0:T(8,128)(2,1)}, u32[]{:S(2)}) copy-start(bf16[1,8,32,128]{3,2,1,0:T(8,128)(2,1)} %fixed_ref.5) | copy-start | bytes 196612
  1.5 0.8 %copy-start.2 = (bf16[1,8,32,128]{3,2,1,0:T(8,128)(2,1)S(1)}, bf16[1,8,32,128]{3,2,1,0:T(8,128)(2,1)}, u32[]{:S(2)}) copy-start(bf16[1,8,32,128]{3,2,1,0:T(8,128)(2,1)} %moving_ref.5) | copy-start | bytes 196612
  2.4 2.5 %collective-permute-start = (bf16[9,32,128]{2,1,0:T(8,128)(2,1)S(1)}, bf16[9,32,128]{2,1,0:T(8,128)(2,1)S(1)}, u32[]{:S(2)}, u32[]{:S(2)}) collective-permute-start(bf16[9,32,128]{2,1,0:T(8,128)(2,1)S(1)} %get-tuple-element.10), channel_id=1, source_target_pairs={{0,1},{2,3},{1,0},{3,2},{4,5},{6,7},{5,4},{7,6},{8,9},{10,11},{9,8... | collective-permute-start | bytes 221192 | tf_op jit(solution)/shard_map/ppermute | solution.py:445
  2.9 2.0 %collective-permute-start.1 = (bf16[9,32,128]{2,1,0:T(8,128)(2,1)S(1)}, bf16[9,32,128]{2,1,0:T(8,128)(2,1)S(1)}, u32[]{:S(2)}, u32[]{:S(2)}) collective-permute-start(bf16[9,32,128]{2,1,0:T(8,128)(2,1)S(1)} %get-tuple-element.11), channel_id=1, source_target_pairs={{1,2},{2,1},{5,6},{6,5},{9,10},{10,9},{13,14},{14,13},{17,18},{18,... | collective-permute-start | bytes 221192 | tf_op jit(solution)/shard_map/ppermute | solution.py:447
  4.9 0.9 %copy-start.3 = (bf16[256,256]{1,0:T(8,128)(2,1)S(1)}, bf16[256,256]{1,0:T(8,128)(2,1)}, u32[]{:S(2)}) copy-start(bf16[256,256]{1,0:T(8,128)(2,1)} %constant.12.clone.box_ref) | copy-start | bytes 393220
  5.8 0.9 %copy-start.4 = (f32[4,48,128]{2,1,0:T(8,128)S(1)}, f32[4,48,128]{2,1,0:T(8,128)}, u32[]{:S(2)}) copy-start(f32[4,48,128]{2,1,0:T(8,128)} %constant.14.clone.depth_ref) | copy-start | bytes 294916
  6.7 0.8 %copy-start.5 = (f32[128,128]{1,0:T(8,128)S(1)}, f32[128,128]{1,0:T(8,128)}, u32[]{:S(2)}) copy-start(f32[128,128]{1,0:T(8,128)} %constant.16.clone.cols_ref) | copy-start | bytes 196612
  7.6 0.8 %copy-start.6 = (f32[2,32,128]{2,1,0:T(8,128)S(1)}, f32[2,32,128]{2,1,0:T(8,128)}, u32[]{:S(2)}) copy-start(f32[2,32,128]{2,1,0:T(8,128)} %constant.15.clone.rows_ref) | copy-start | bytes 98308
  9.8 17.5 %copy-start.7 = (bf16[128,128]{1,0:T(8,128)(2,1)S(1)}, bf16[128,128]{1,0:T(8,128)(2,1)}, u32[]{:S(2)}) copy-start(bf16[128,128]{1,0:T(8,128)(2,1)} %constant.13.clone.slope_ref) | copy-start | bytes 98308

commit v3 on v2

v3 whole, which is shorter than its diff:
```python
import functools
import math

import jax
import jax.numpy as jnp
from jax import lax
from jax.experimental import pallas as pl
from jax.experimental.pallas import tpu as pltpu
from jax.sharding import PartitionSpec as P

SCALE = 16
GY = 8
EPSILON = 1e-05
STEP_LENGTH = 0.5
GAUSS_RAW = [math.exp(-((offset - 3) ** 2) / 4.5) for offset in range(7)]
GAUSS_TAPS = [value / sum(GAUSS_RAW) for value in GAUSS_RAW]
REACH = 4
LANES = 128
F32 = jnp.float32
BF16 = jnp.bfloat16


def cell_weights(index, cell, length):
    total = jnp.zeros(index.shape, F32)
    for offset, weight in enumerate(GAUSS_TAPS):
        target = index + (offset - 3)
        inside = (target >= cell * SCALE) & (target < cell * SCALE + SCALE)
        total = total + jnp.where(inside, weight, 0.0)
    return total


def hat(index, cell, count):
    where = jnp.clip((index.astype(F32) + 0.5) * (1.0 / SCALE) - 0.5, 0.0, count - 1.0)
    return jnp.maximum(0.0, 1.0 - jnp.abs(where - cell.astype(F32)))


def lane_index(shape):
    return lax.broadcasted_iota(jnp.int32, shape, len(shape) - 1)


def sublane_index(shape):
    return lax.broadcasted_iota(jnp.int32, shape, len(shape) - 2)


def tail(plane):
    return jnp.concatenate([plane, jnp.zeros((8, plane.shape[1]), plane.dtype)], axis=0)


def split(value, count):
    parts = []
    for _ in range(count):
        parts.append(value.astype(BF16))
        value = value - parts[-1].astype(F32)
    return parts


def exact_dot(value, table):
    rows = value.shape[0]
    stacked = jnp.concatenate(split(value, 3), axis=0)
    product = jnp.dot(stacked, table, preferred_element_type=F32)
    return product[:rows] + product[rows : 2 * rows] + product[2 * rows :]


def window_of_nine(items):
    two = [a + b for a, b in zip(items[:-1], items[1:])]
    four = [a + b for a, b in zip(two[:-2], two[2:])]
    eight = [a + b for a, b in zip(four[:-4], four[4:])]
    return [a + b for a, b in zip(eight[:-1], items[8:])]


def row_box(plane):
    side = plane.shape[0]
    padded = tail(plane)
    total = padded + pltpu.roll(padded, 1, 0)
    total = total + pltpu.roll(total, 2, 0)
    total = total + pltpu.roll(total, 4, 0)
    total = total + pltpu.roll(padded, 8, 0)
    return pltpu.roll(total, side + 8 - 4, 0)[:side]


def row_slope(plane):
    side = plane.shape[0]
    padded = tail(plane)
    return 0.5 * (pltpu.roll(padded, side + 7, 0)[:side] - pltpu.roll(padded, 1, 0)[:side])


def col_slope(plane):
    width = plane.shape[1]
    lane = lane_index(plane.shape)
    upper = jnp.where(lane < width - 1, pltpu.roll(plane, width - 1, 1), 0.0)
    lower = jnp.where(lane > 0, pltpu.roll(plane, 1, 1), 0.0)
    return 0.5 * (upper - lower)


def load_images(odd, fixed_ref, moving_ref, near_ref, far_ref, image, shifted):
    planes = fixed_ref.shape[0]
    image[REACH : REACH + planes] = fixed_ref[...].astype(F32)
    shifted[REACH + 1 : REACH + 1 + planes] = moving_ref[...].astype(F32)
    near = near_ref[...].astype(F32)
    far = far_ref[...].astype(F32)
    low = jnp.where(odd, near, far)
    high = jnp.where(odd, far, near)
    image[0:REACH] = low[0:REACH]
    image[REACH + planes :] = high[0:REACH]
    shifted[0 : REACH + 1] = low[REACH:]
    shifted[REACH + 1 + planes :] = high[REACH:]


def box_sums(fields, planes, side, sums, parts, box_ref):
    half = planes // 2
    count = 0
    for tile in range(side // 8):
        rows = slice(8 * tile, 8 * tile + 8)
        lists = fields(rows)
        count = len(lists)
        for f, items in enumerate(lists):
            for z, item in enumerate(window_of_nine(items)):
                sums[f, z, rows] = item
    for f in range(count):
        for z in range(planes):
            total = row_box(sums[f, z])
            rows = slice((f * half + z % half) * side, (f * half + z % half + 1) * side)
            lanes = slice((z // half) * LANES, (z // half + 1) * LANES)
            for part, rounded in enumerate(split(total, 3)):
                parts[part, rows, lanes] = rounded
    used = slice(0, count * half * side)
    box = box_ref[...]
    result = jnp.dot(parts[0, used], box, preferred_element_type=F32)
    result = result + jnp.dot(parts[1, used], box, preferred_element_type=F32)
    result = result + jnp.dot(parts[2, used], box, preferred_element_type=F32)

    def of(f, z):
        start = (f * half + z % half) * side
        lane = (z // half) * LANES
        return result[start : start + side, lane : lane + LANES]

    return of


def force_message(weights, warped, planes, cells_ref, rows_ref, cols_ref, marks_ref):
    coarse = cells_ref.shape[0] // planes
    coarse_rows, side, _ = rows_ref.shape
    total = [[None] * coarse for _ in range(3)]
    for z in range(planes):
        plane = warped(z)
        slopes = (0.5 * (warped(z + 1) - warped(z - 1)), row_slope(plane), col_slope(plane))
        for k in range(coarse):
            index = k * planes + z
            share = weights(z) * cells_ref[index : index + 1, :]
            for c in range(3):
                term = share * slopes[c]
                total[c][k] = term if z == 0 else total[c][k] + term
    tiles = []
    for c in range(3):
        for k in range(coarse):
            for a in range(coarse_rows):
                product = total[c][k] * rows_ref[a]
                tile = product[0:8]
                for start in range(8, side, 8):
                    tile = tile + product[start : start + 8]
                tiles.append(tile)
    sums = exact_dot(jnp.concatenate(tiles, axis=0), cols_ref[...])
    sums = sums[:, :LANES] + sums[:, LANES:]
    coarse_cols = LANES // SCALE
    lane = lane_index((8, LANES))
    picked = jnp.zeros((8, LANES), F32)
    for g in range(len(tiles)):
        picked = jnp.where(lane // coarse_cols == g, sums[8 * g : 8 * g + 8], picked)
    row = jnp.sum(picked, axis=0, keepdims=True) * marks_ref[1:2]
    return jnp.where(lane[0:1] == len(tiles) * coarse_cols, marks_ref[0:1], row)


def regular_grid(received, spread_ref, block_rows, coarse_rows, coarse_cols):
    groups = spread_ref.shape[1] // LANES
    used = groups * coarse_rows * coarse_cols
    width = GY * coarse_cols
    place = received[:, used : used + 1].astype(jnp.int32)
    lane = lane_index(received.shape)
    here = (place % GY) == (lane % width) // coarse_cols
    block_row = place // GY
    sub = sublane_index((8, LANES))
    grids = [jnp.zeros((8, LANES), F32) for _ in range(block_rows)]
    entries = exact_dot(received, spread_ref[...])
    for g in range(groups):
        entry = entries[:, g * LANES : (g + 1) * LANES]
        for r in range(block_rows):
            chosen = here if block_rows == 1 else here & (block_row == r)
            total = jnp.sum(jnp.where(chosen, entry, 0.0), axis=0, keepdims=True)
            grids[r] = jnp.where(sub == g, total, grids[r])
    even = sub % 2 == 0
    lane = lane_index((8, LANES))
    column = lane % width
    first = lane < width
    grids = [
        0.5 * g + 0.25 * jnp.where(even, pltpu.roll(g, 7, 0), pltpu.roll(g, 1, 0)) for g in grids
    ]
    other = [pltpu.roll(g, width, 1) for g in grids]
    none = jnp.zeros((8, LANES), F32)
    before = [none] + other[:-1]
    after = other[1:] + [none]
    grids = [
        0.5 * g + 0.25 * (o + jnp.where(first, b, a))
        for g, o, b, a in zip(grids, other, before, after)
    ]
    grids = [
        0.25 * jnp.where(column > 0, pltpu.roll(g, 1, 1), 0.0)
        + 0.5 * g
        + 0.25 * jnp.where(column < width - 1, pltpu.roll(g, LANES - 1, 1), 0.0)
        for g in grids
    ]
    grids = [jnp.where(sub < groups, g, 0.0) for g in grids]
    square = functools.reduce(lambda a, b: a + b, [g * g for g in grids])
    square = jnp.sum(jnp.sum(square, axis=1, keepdims=True), axis=0, keepdims=True)
    mean = square * (1.0 / (groups * block_rows * LANES))
    factor = STEP_LENGTH / jnp.sqrt(mean + EPSILON)
    return [g * factor for g in grids]


def pack_kernel(fixed_hbm, moving_hbm, near_ref, far_ref, fixed_ref, moving_ref, sems):
    copies = [
        pltpu.make_async_copy(source.at[0], target, sems.at[i])
        for i, (source, target) in enumerate(((fixed_hbm, fixed_ref), (moving_hbm, moving_ref)))
    ]
    for copy in copies:
        copy.start()
    planes = fixed_ref.shape[0]
    part = lax.axis_index("gz")
    odd = part % 2
    inner = (part > 0) & (part < lax.axis_size("gz") - 1)
    for copy in copies:
        copy.wait()
    for ref, low, keep in ((far_ref, odd == 0, inner), (near_ref, odd == 1, None)):
        i = fixed_ref[pl.ds(jnp.where(low, 0, planes - REACH), REACH)]
        j = moving_ref[pl.ds(jnp.where(low, 0, planes - REACH - 1), REACH + 1)]
        if keep is not None:
            i = jnp.where(keep, i.astype(F32), 0.0).astype(BF16)
            j = jnp.where(keep, j.astype(F32), 0.0).astype(BF16)
        ref[0:REACH] = i
        ref[REACH:] = j


def table_kernel(
    both_ref,
    marks_ref, hats_ref, cells_ref, rows_ref, cols_ref, box_ref, slope_ref, spread_ref, hat_x_ref, hat_y_ref,
    *, planes, block_rows,
):
    part = lax.axis_index("gz")
    total = planes * lax.axis_size("gz")
    coarse_rows, side, _ = rows_ref.shape
    coarse_cols = LANES // SCALE
    width = GY * coarse_cols
    wide = planes + 2 * REACH
    row = sublane_index(hats_ref.shape)
    z = part * planes + row % wide - REACH
    hats_ref[...] = jnp.where((z >= 0) & (z < total), hat(z, row // wide, total // SCALE), 0.0)
    row = sublane_index(cells_ref.shape)
    cells_ref[...] = cell_weights(part * planes + row % planes, row // planes, total)
    for a in range(coarse_rows):
        rows_ref[a] = cell_weights(sublane_index((side, LANES)), a, side)
    square = (LANES, LANES)
    cols = cell_weights(sublane_index(square), lane_index(square) % coarse_cols, LANES)
    for i, value in enumerate(split(cols, 2)):
        cols_ref[:, i * LANES : (i + 1) * LANES] = value
    apart = sublane_index(square) - lane_index(square)
    band = jnp.where(jnp.abs(apart) <= 4, 1.0, 0.0).astype(BF16)
    box_ref[...] = jnp.zeros(box_ref.shape, BF16)
    for i in range(2):
        box_ref[i * LANES : (i + 1) * LANES, i * LANES : (i + 1) * LANES] = band
    slope_ref[...] = jnp.where(apart == 1, 0.5, jnp.where(apart == -1, -0.5, 0.0)).astype(BF16)
    lane = lane_index(square)
    source = (lane // width) * coarse_cols + lane % coarse_cols
    for g in range(spread_ref.shape[1] // LANES):
        hit = sublane_index(square) == source + g * coarse_rows * coarse_cols
        spread_ref[:, g * LANES : (g + 1) * LANES] = jnp.where(hit, 1.0, 0.0).astype(BF16)
    row = sublane_index(marks_ref.shape)
    marks_ref[...] = jnp.where(row == 0, both_ref[0:1, 0:1], both_ref[1:2, 0:1]).astype(F32)
    place = both_ref[0:1, 0:1]
    y = lane + (place % GY) * LANES
    entry = sublane_index(square)
    hat_y = hat(y, entry % width, width)
    for a in range(coarse_rows):
        chosen = jnp.where(entry // width == a, hat_y, 0.0).astype(BF16)
        hat_y_ref[:, a * LANES : (a + 1) * LANES] = chosen
    x = sublane_index((side, LANES)) + (place // GY) * side
    for r in range(block_rows * coarse_rows):
        hat_x_ref[r] = hat(x, jnp.full((1, 1), r, jnp.int32), block_rows * coarse_rows)


def first_kernel(
    fixed_ref, moving_ref, near_ref, far_ref, marks_ref,
    cells_ref, rows_ref, cols_ref, box_ref,
    message_ref, mean_ref, variance_ref,
    image, shifted, sums, parts, weight,
):
    planes, side, _ = fixed_ref.shape
    odd = lax.axis_index("gz") % 2 == 1
    load_images(odd, fixed_ref, moving_ref, near_ref, far_ref, image, shifted)
    wide = planes + 2 * REACH

    def fields(rows):
        i = [image[z, rows] for z in range(wide)]
        w = [shifted[z + 1, rows] for z in range(wide)]
        return (
            i,
            w,
            [a * a for a in i],
            [b * b for b in w],
            [a * b for a, b in zip(i, w)],
        )

    of = box_sums(fields, planes, side, sums, parts, box_ref)
    for z in range(planes):
        mean_i, mean_w, mean_ii, mean_ww, mean_iw = [of(f, z) * (1.0 / 729.0) for f in range(5)]
        sii = mean_ii - mean_i * mean_i
        sww = mean_ww - mean_w * mean_w
        siw = mean_iw - mean_i * mean_w
        mean_ref[z] = mean_i
        variance_ref[z] = sii
        ratio = siw / (sii * sww + EPSILON)
        weight[z] = (2.0 * ratio) * (
            (image[z + REACH] - mean_i)
            - siw / (sww + EPSILON) * (shifted[z + REACH + 1] - mean_w)
        )
    row = force_message(
        lambda z: weight[z],
        lambda z: shifted[z + REACH + 1],
        planes, cells_ref, rows_ref, cols_ref, marks_ref,
    )
    message_ref[...] = jnp.broadcast_to(row[None], message_ref.shape)


def second_kernel(
    received_ref, fixed_ref, moving_ref, near_ref, far_ref, marks_ref,
    mean_ref, variance_ref, hats_ref, cells_ref, rows_ref, cols_ref, box_ref, slope_ref,
    spread_ref, hat_x_ref, hat_y_ref,
    message_ref, map_ref, velocity_ref,
    image, shifted, warped, sums, parts, weight,
):
    planes, side, _ = fixed_ref.shape
    odd = lax.axis_index("gz") % 2 == 1
    load_images(odd, fixed_ref, moving_ref, near_ref, far_ref, image, shifted)
    wide = planes + 2 * REACH
    coarse_rows = rows_ref.shape[0]
    coarse_cols = LANES // SCALE
    block_rows = velocity_ref.shape[0] // 8
    coarse = hats_ref.shape[0] // wide

    grids = regular_grid(received_ref[...], spread_ref, block_rows, coarse_rows, coarse_cols)
    for r in range(block_rows):
        velocity_ref[8 * r : 8 * r + 8] = grids[r]
    along = exact_dot(jnp.concatenate(grids, axis=0), hat_y_ref[...])
    shift = [[None] * coarse for _ in range(3)]
    for r in range(block_rows):
        for a in range(coarse_rows):
            hat_x = hat_x_ref[r * coarse_rows + a]
            for c in range(3):
                for k in range(coarse):
                    g = 8 * r + c * coarse + k
                    term = hat_x * along[g : g + 1, a * LANES : (a + 1) * LANES]
                    shift[c][k] = term if r + a == 0 else shift[c][k] + term
    inner = shifted[1 : wide + 1].reshape(wide * side, LANES).astype(BF16)
    across = jnp.dot(inner, slope_ref[...], preferred_element_type=F32)
    for z in range(wide):
        plane = shifted[z + 1]
        slopes = (
            0.5 * (shifted[z + 2] - shifted[z]),
            row_slope(plane),
            across[z * side : (z + 1) * side],
        )
        hats = [hats_ref[k * wide + z : k * wide + z + 1, :] for k in range(coarse)]
        for c in range(3):
            u = hats[0] * shift[c][0]
            for k in range(1, coarse):
                u = u + hats[k] * shift[c][k]
            plane = plane + u * slopes[c]
        warped[z] = plane

    def fields(rows):
        i = [image[z, rows] for z in range(wide)]
        w = [warped[z, rows] for z in range(wide)]
        return (w, [b * b for b in w], [a * b for a, b in zip(i, w)])

    of = box_sums(fields, planes, side, sums, parts, box_ref)
    for z in range(planes):
        mean_w, mean_ww, mean_iw = [of(f, z) * (1.0 / 729.0) for f in range(3)]
        mean_i = mean_ref[z]
        sii = variance_ref[z]
        sww = mean_ww - mean_w * mean_w
        siw = mean_iw - mean_i * mean_w
        ratio = siw / (sii * sww + EPSILON)
        map_ref[z] = siw * ratio
        weight[z] = (2.0 * ratio) * (
            (image[z + REACH] - mean_i) - siw / (sww + EPSILON) * (warped[z + REACH] - mean_w)
        )
    row = force_message(
        lambda z: weight[z],
        lambda z: warped[z + REACH],
        planes, cells_ref, rows_ref, cols_ref, marks_ref,
    )
    message_ref[...] = jnp.broadcast_to(row[None], message_ref.shape)


def last_kernel(received_ref, velocity_ref, spread_ref, map_ref, out_ref, map_hbm, sem):
    copy = pltpu.make_async_copy(map_ref, map_hbm.at[0], sem)
    copy.start()
    _, coarse, rows, width = out_ref.shape
    coarse_rows = LANES // width
    block_rows = rows // coarse_rows
    grids = regular_grid(received_ref[...], spread_ref, block_rows, coarse_rows, width // GY)
    for r in range(block_rows):
        velocity = velocity_ref[8 * r : 8 * r + 8] + grids[r]
        for c in range(3):
            for k in range(coarse):
                g = c * coarse + k
                for a in range(coarse_rows):
                    out_ref[c, k, r * coarse_rows + a : r * coarse_rows + a + 1, :] = velocity[
                        g : g + 1, a * width : (a + 1) * width
                    ]
    copy.wait()


def far_pairs(blocks, parts):
    pairs = []
    for block in range(blocks):
        for part in range(1, parts - 1, 2):
            low, high = block * parts + part, block * parts + part + 1
            pairs += [(low, high), (high, low)]
        for part in (0, parts - 1):
            pairs.append((block * parts + part, (block ^ 1) * parts + part))
    return pairs


VMEM = pl.BlockSpec(memory_space=pltpu.VMEM)
HBM = pl.BlockSpec(memory_space=pl.ANY)


def call(kernel, outs, scratch, *operands, in_specs=None, out_specs=None):
    return pl.pallas_call(
        kernel,
        out_shape=[jax.ShapeDtypeStruct(shape, dtype) for shape, dtype in outs],
        in_specs=in_specs or [VMEM] * len(operands),
        out_specs=out_specs or [VMEM] * len(outs),
        scratch_shapes=scratch,
        compiler_params=pltpu.CompilerParams(vmem_limit_bytes=24 << 20),
    )(*operands)


def per_device(fixed, moving, block_place, tissue):
    slots, planes, side, width = fixed.shape
    assert slots == 1 and width == LANES
    depth_parts = lax.axis_size("gz")
    devices = lax.axis_size("blk") * depth_parts
    blocks = slots * lax.axis_size("blk")
    coarse = planes * depth_parts // SCALE
    coarse_rows, coarse_cols = side // SCALE, width // SCALE
    block_rows = blocks // GY
    wide = planes + 2 * REACH
    field = (planes, side, width)
    halo = ((2 * REACH + 1, side, width), BF16)

    near, far, fixed, moving = call(
        pack_kernel,
        [halo, halo, (field, BF16), (field, BF16)],
        [pltpu.SemaphoreType.DMA((2,))],
        pltpu.with_memory_space_constraint(fixed, pltpu.HBM),
        pltpu.with_memory_space_constraint(moving, pltpu.HBM),
        in_specs=[HBM] * 2,
    )
    far = lax.ppermute(far, ("blk", "gz"), far_pairs(lax.axis_size("blk"), depth_parts))
    pairs = [(i, i + 1) for i in range(0, depth_parts, 2)]
    near = lax.ppermute(near, "gz", pairs + [(b, a) for a, b in pairs])
    marks, hats, cells, rows, cols, box, slope, spread, hat_x, hat_y = call(
        functools.partial(table_kernel, planes=planes, block_rows=block_rows),
        [
            ((8, width), F32),
            ((coarse * wide, width), F32),
            ((coarse * planes, width), F32),
            ((coarse_rows, side, width), F32),
            ((width, 2 * width), BF16),
            ((2 * width, 2 * width), BF16),
            ((width, width), BF16),
            ((width, 3 * coarse * width), BF16),
            ((block_rows * coarse_rows, side, width), F32),
            ((width, coarse_rows * width), BF16),
        ],
        [],
        jnp.stack([block_place, tissue]),
    )

    message = ((devices, 1, LANES), F32)

    def scratch(fields):
        return [
            pltpu.VMEM((fields, planes, side, width), F32),
            pltpu.VMEM((3, fields * planes * side // 2, 2 * width), BF16),
            pltpu.VMEM(field, F32),
        ]

    images = [pltpu.VMEM((wide, side, width), F32), pltpu.VMEM((wide + 2, side, width), F32)]
    sent, mean, variance = call(
        first_kernel, [message, (field, F32), (field, F32)], images + scratch(5),
        fixed, moving, near, far, marks, cells, rows, cols, box,
    )
    received = lax.all_to_all(sent, ("blk", "gz"), 0, 0).reshape(devices, LANES)
    sent, correlation, velocity = call(
        second_kernel,
        [message, (field, F32), ((8 * block_rows, LANES), F32)],
        images + [pltpu.VMEM((wide, side, width), F32)] + scratch(3),
        received, fixed, moving, near, far, marks,
        mean, variance, hats, cells, rows, cols, box, slope, spread, hat_x, hat_y,
    )
    received = lax.all_to_all(sent, ("blk", "gz"), 0, 0).reshape(devices, LANES)
    return tuple(
        call(
            last_kernel,
            [
                ((3, coarse, block_rows * coarse_rows, GY * coarse_cols), F32),
                ((slots,) + field, F32),
            ],
            [pltpu.SemaphoreType.DMA(())],
            received, velocity, spread, correlation,
            out_specs=[VMEM, HBM],
        )
    )


def solution(mesh):
    return jax.shard_map(
        per_device,
        mesh=mesh,
        in_specs=(P("blk", "gz", None, None), P("blk", "gz", None, None), P("blk"), P("blk")),
        out_specs=(P(), P("blk", "gz", None, None)),
        check_vma=False,
    )
```

time: 40.5 us -> 33.4 us (0.82)
  local copies, waits for them, and re-layouts: 5.12 us -> 0 us
  blocking collectives: 26.4 us -> 21.7 us
  starting transfers between devices: 1.21 us -> 3.11 us
  waiting for transfers between devices: 0.01 us -> 0.69 us
  Pallas kernels: 5.3 us -> 5.72 us
    unnamed x16 -> x0, local copies, waits for them, and re-layouts: 5.12 us -> none
    all_to_all x2, blocking collectives: 26.4 us -> 21.7 us  [per_device(): received = lax.all_to_all(sent, ('blk', 'gz'), 0, 0).reshape(devices, LANES)]
    ppermute x1, starting transfers between devices: 0.65 us -> 2.55 us  [per_device(): lax.ppermute(far, ('blk', 'gz'), far_pairs(lax.axis_size('blk'), depth_pa...]
    ppermute x1, waiting for transfers between devices: 0.01 us -> 0.68 us  [per_device(): lax.ppermute(far, ('blk', 'gz'), far_pairs(lax.axis_size('blk'), depth_pa...]
    pallas_call x4 -> x5, Pallas kernels: 5.3 us -> 5.72 us  [call(): pl.pallas_call(kernel, out_shape=[jax.ShapeDtypeStruct(shape, dtype) for...]
  transfers between devices with their start and end apart: 2 -> 2, of which waited for: 0 -> 1; matrix products, arithmetic and copies ran while one was open for 0% -> 0% of each run, Pallas kernels for 0% -> 1%
where the time goes in v3:
time: 33.4 us; the launch traced here: 33.2 us
  blocking collectives  21.7 us (65%)
  Pallas kernels  5.72 us (17%)
  starting transfers between devices  3.11 us (9%)
  between operations  1.98 us (6%)
  waiting for transfers between devices  0.69 us (2%)
    all_to_all x2, blocking collectives, per_device(): received = lax.all_to_all(sent, ('blk', 'gz'), 0, 0).reshape(devices, LANES)  21.7 us
    pallas_call x5, Pallas kernels, call(): pl.pallas_call(kernel, out_shape=[jax.ShapeDtypeStruct(shape, dtype) for...  5.72 us
    ppermute x1, starting transfers between devices, per_device(): lax.ppermute(far, ('blk', 'gz'), far_pairs(lax.axis_size('blk'), depth_pa...  2.55 us
    ppermute x1, waiting for transfers between devices, per_device(): lax.ppermute(far, ('blk', 'gz'), far_pairs(lax.axis_size('blk'), depth_pa...  0.68 us
  transfers between devices with their start and end apart: 2, of which 1 were waited for; matrix products, arithmetic and copies ran while one was open for 0% of the time, Pallas kernels for 1%

profile of v3, /device:TPU:0, one launch (start us, length us, event | category | flops | bytes accessed | tf_op | source)
XLA Modules:
  0.0 33.2 jit_solution(3502648640055070686)
XLA Ops:
  0.6 0.9 %shard_map.59 = (bf16[9,32,128]{2,1,0:T(8,128)(2,1)S(1)}, bf16[9,32,128]{2,1,0:T(8,128)(2,1)S(1)}, bf16[8,32,128]{2,1,0:T(8,128)(2,1)S(1)}, bf16[8,32,128]{2,1,0:T(8,128)(2,1)S(1)}) custom-call(bf16[1,8,32,128]{3,2,1,0:T(8,128)(2,1)} %fixed_hbm.1, bf16[1,8,32,128]{3,2,1,0:T(8,128)(2,1)} %moving_hbm.1), custom_call_target="tpu_custom_call" | custom-call | tf_op jit(solution)/shard_map/pallas_call | solution.py:438
  1.5 0.6 %collective-permute-start = (bf16[9,32,128]{2,1,0:T(8,128)(2,1)S(1)}, bf16[9,32,128]{2,1,0:T(8,128)(2,1)S(1)}, u32[]{:S(2)}, u32[]{:S(2)}) collective-permute-start(bf16[9,32,128]{2,1,0:T(8,128)(2,1)S(1)} %get-tuple-element.24), channel_id=1, source_target_pairs={{0,1},{2,3},{1,0},{3,2},{4,5},{6,7},{5,4},{7,6},{8,9},{10,11},{9,8... | collective-permute-start | bytes 221192 | tf_op jit(solution)/shard_map/ppermute | solution.py:471
  2.1 2.6 %collective-permute-start.1 = (bf16[9,32,128]{2,1,0:T(8,128)(2,1)S(1)}, bf16[9,32,128]{2,1,0:T(8,128)(2,1)S(1)}, u32[]{:S(2)}, u32[]{:S(2)}) collective-permute-start(bf16[9,32,128]{2,1,0:T(8,128)(2,1)S(1)} %get-tuple-element.25), channel_id=1, source_target_pairs={{1,2},{2,1},{0,4},{3,7},{5,6},{6,5},{4,0},{7,3},{9,10},{10,9},{8,1... | collective-permute-start | bytes 221192 | tf_op jit(solution)/shard_map/ppermute | solution.py:469
  6.0 0.3 shard_map.60
  6.3 0.0 collective-permute-done.near_ref
  6.3 0.7 %collective-permute-done.1.far_ref = bf16[9,32,128]{2,1,0:T(8,128)(2,1)S(1)} collective-permute-done((bf16[9,32,128]{2,1,0:T(8,128)(2,1)S(1)}, bf16[9,32,128]{2,1,0:T(8,128)(2,1)S(1)}, u32[]{:S(2)}, u32[]{:S(2)}) %collective-permute-start.1) | collective-permute-done | bytes 73760 | tf_op jit(solution)/shard_map/ppermute | solution.py:469
  7.0 1.4 %shard_map.61 = (f32[32,1,128]{2,1,0:T(1,128)S(1)}, f32[8,32,128]{2,1,0:T(8,128)S(1)}, f32[8,32,128]{2,1,0:T(8,128)S(1)}) custom-call(bf16[8,32,128]{2,1,0:T(8,128)(2,1)S(1)} %get-tuple-element.22.fixed_ref, bf16[8,32,128]{2,1,0:T(8,128)(2,1)S(1)} %get-tuple-element.23.moving_ref, bf16[9,32,128]{2,1,0:T(8,128)(2,1)S(1)} %collective-permute-done.near_ref, ...), custom_call_target="tpu_custom_call" | custom-call | tf_op jit(solution)/shard_map/pallas_call | solution.py:438
  8.4 12.8 %all_to_all.10 = f32[32,1,128]{2,1,0:T(1,128)S(1)} all-to-all(f32[32,1,128]{2,1,0:T(1,128)S(1)} %get-tuple-element.31), channel_id=1, replica_groups=mesh['blk'=8,'gz'=4] {'blk','gz'}, dimensions={0} | all-to-all | bytes 32768 | tf_op jit(solution)/shard_map/all_to_all | solution.py:504
  21.2 1.8 %shard_map.62 = (f32[32,1,128]{2,1,0:T(1,128)S(1)}, f32[8,32,128]{2,1,0:T(8,128)S(1)}, f32[8,128]{1,0:T(8,128)S(1)}) custom-call(f32[32,128]{1,0:T(8,128)S(1)} %bitcast.6, bf16[8,32,128]{2,1,0:T(8,128)(2,1)S(1)} %get-tuple-element.22.fixed_ref, bf16[8,32,128]{2,1,0:T(8,128)(2,1)S(1)} %get-tuple-element.23.moving_ref, ...), custom_call_target="tpu_custom_call" | custom-call | tf_op jit(solution)/shard_map/pallas_call | solution.py:438
  23.0 8.9 %all_to_all.11 = f32[32,1,128]{2,1,0:T(1,128)S(1)} all-to-all(f32[32,1,128]{2,1,0:T(1,128)S(1)} %get-tuple-element.39), channel_id=1, replica_groups=mesh['blk'=8,'gz'=4] {'blk','gz'}, dimensions={0} | all-to-all | bytes 32768 | tf_op jit(solution)/shard_map/all_to_all | solution.py:512
  31.9 1.3 %shard_map.63 = (f32[3,2,2,64]{3,2,1,0:T(2,128)}, f32[1,8,32,128]{3,2,1,0:T(8,128)}) custom-call(f32[32,128]{1,0:T(8,128)S(1)} %bitcast.7, f32[8,128]{1,0:T(8,128)S(1)} %get-tuple-element.40.velocity_ref, bf16[128,768]{1,0:T(8,128)(2,1)S(1)} %get-tuple-element.36.spread_ref, f32[8,32,128]{2,1,0:T(8,128)S(1)} %get-tuple-element.41.map_ref), custom_call_target="tpu_custom_call" | custom-call | tf_op jit(solution)/shard_map/pallas_call | solution.py:438
  (1 shorter events, 0.0 us)
Async XLA Ops:
  1.5 4.8 %collective-permute-start = (bf16[9,32,128]{2,1,0:T(8,128)(2,1)S(1)}, bf16[9,32,128]{2,1,0:T(8,128)(2,1)S(1)}, u32[]{:S(2)}, u32[]{:S(2)}) collective-permute-start(bf16[9,32,128]{2,1,0:T(8,128)(2,1)S(1)} %get-tuple-element.24), channel_id=1, source_target_pairs={{0,1},{2,3},{1,0},{3,2},{4,5},{6,7},{5,4},{7,6},{8,9},{10,11},{9,8... | collective-permute-start | bytes 221192 | tf_op jit(solution)/shard_map/ppermute | solution.py:471
  2.1 4.9 %collective-permute-start.1 = (bf16[9,32,128]{2,1,0:T(8,128)(2,1)S(1)}, bf16[9,32,128]{2,1,0:T(8,128)(2,1)S(1)}, u32[]{:S(2)}, u32[]{:S(2)}) collective-permute-start(bf16[9,32,128]{2,1,0:T(8,128)(2,1)S(1)} %get-tuple-element.25), channel_id=1, source_target_pairs={{1,2},{2,1},{0,4},{3,7},{5,6},{6,5},{4,0},{7,3},{9,10},{10,9},{8,1... | collective-permute-start | bytes 221192 | tf_op jit(solution)/shard_map/ppermute | solution.py:469

commit v4 on v3

--- a/solution.py
+++ b/solution.py
@@ -15,12 +15,13 @@
 GAUSS_RAW = [math.exp(-((offset - 3) ** 2) / 4.5) for offset in range(7)]
 GAUSS_TAPS = [value / sum(GAUSS_RAW) for value in GAUSS_RAW]
 REACH = 4
+PAD = 8
 LANES = 128
 F32 = jnp.float32
 BF16 = jnp.bfloat16
 
 
-def cell_weights(index, cell, length):
+def cell_weights(index, cell):
     total = jnp.zeros(index.shape, F32)
     for offset, weight in enumerate(GAUSS_TAPS):
         target = index + (offset - 3)
@@ -42,10 +43,6 @@
     return lax.broadcasted_iota(jnp.int32, shape, len(shape) - 2)
 
 
-def tail(plane):
-    return jnp.concatenate([plane, jnp.zeros((8, plane.shape[1]), plane.dtype)], axis=0)
-
-
 def split(value, count):
     parts = []
     for _ in range(count):
@@ -68,66 +65,67 @@
     return [a + b for a, b in zip(eight[:-1], items[8:])]
 
 
-def row_box(plane):
-    side = plane.shape[0]
-    padded = tail(plane)
-    total = padded + pltpu.roll(padded, 1, 0)
-    total = total + pltpu.roll(total, 2, 0)
-    total = total + pltpu.roll(total, 4, 0)
-    total = total + pltpu.roll(padded, 8, 0)
-    return pltpu.roll(total, side + 8 - 4, 0)[:side]
-
-
-def row_slope(plane):
-    side = plane.shape[0]
-    padded = tail(plane)
-    return 0.5 * (pltpu.roll(padded, side + 7, 0)[:side] - pltpu.roll(padded, 1, 0)[:side])
-
-
-def col_slope(plane):
+def padded_rows(side):
+    return slice(PAD, PAD + side)
+
+
+def clear_edges(ref, side):
+    edge = jnp.zeros(ref.shape[:-2] + (PAD, LANES), F32)
+    ref[..., 0:PAD, :] = edge
+    ref[..., PAD + side :, :] = edge
+
+
+def row_box(padded, three, side):
+    count = side + 8
+    three[...] = (
+        padded[PAD - 5 : PAD - 5 + count]
+        + padded[PAD - 4 : PAD - 4 + count]
+        + padded[PAD - 3 : PAD - 3 + count]
+    )
+    return three[1 : 1 + side] + three[4 : 4 + side] + three[7 : 7 + side]
+
+
+def row_difference(padded, side):
+    return padded[PAD + 1 : PAD + 1 + side] - padded[PAD - 1 : PAD - 1 + side]
+
+
+def col_difference(plane):
     width = plane.shape[1]
     lane = lane_index(plane.shape)
     upper = jnp.where(lane < width - 1, pltpu.roll(plane, width - 1, 1), 0.0)
     lower = jnp.where(lane > 0, pltpu.roll(plane, 1, 1), 0.0)
-    return 0.5 * (upper - lower)
+    return upper - lower
 
 
 def load_images(odd, fixed_ref, moving_ref, near_ref, far_ref, image, shifted):
-    planes = fixed_ref.shape[0]
+    planes, side, _ = fixed_ref.shape
+    rows = padded_rows(side)
+    clear_edges(shifted, side)
     image[REACH : REACH + planes] = fixed_ref[...].astype(F32)
-    shifted[REACH + 1 : REACH + 1 + planes] = moving_ref[...].astype(F32)
-    near = near_ref[...].astype(F32)
-    far = far_ref[...].astype(F32)
-    low = jnp.where(odd, near, far)
-    high = jnp.where(odd, far, near)
-    image[0:REACH] = low[0:REACH]
-    image[REACH + planes :] = high[0:REACH]
-    shifted[0 : REACH + 1] = low[REACH:]
-    shifted[REACH + 1 + planes :] = high[REACH:]
-
-
-def box_sums(fields, planes, side, sums, parts, box_ref):
+    shifted[REACH + 1 : REACH + 1 + planes, rows] = moving_ref[...].astype(F32)
+    for ref, low in ((near_ref, odd), (far_ref, ~odd)):
+        start = jnp.where(low, 0, REACH + planes)
+        image[pl.ds(start, REACH)] = ref[0:REACH].astype(F32)
+        start = jnp.where(low, 0, REACH + 1 + planes)
+        shifted[pl.ds(start, REACH + 1), rows] = ref[REACH:].astype(F32)
+
+
+def box_sums(fields, planes, side, sums, threes, parts, box_ref):
     half = planes // 2
-    count = 0
+    count = sums.shape[0]
+    clear_edges(sums, side)
     for tile in range(side // 8):
-        rows = slice(8 * tile, 8 * tile + 8)
-        lists = fields(rows)
-        count = len(lists)
-        for f, items in enumerate(lists):
+        for f, items in enumerate(fields(8 * tile)):
             for z, item in enumerate(window_of_nine(items)):
-                sums[f, z, rows] = item
+                sums[f, z, PAD + 8 * tile : PAD + 8 * tile + 8] = item
     for f in range(count):
         for z in range(planes):
-            total = row_box(sums[f, z])
+            total = row_box(sums.at[f, z], threes.at[f, z], side)
             rows = slice((f * half + z % half) * side, (f * half + z % half + 1) * side)
-            lanes = slice((z // half) * LANES, (z // half + 1) * LANES)
             for part, rounded in enumerate(split(total, 3)):
-                parts[part, rows, lanes] = rounded
-    used = slice(0, count * half * side)
-    box = box_ref[...]
-    result = jnp.dot(parts[0, used], box, preferred_element_type=F32)
-    result = result + jnp.dot(parts[1, used], box, preferred_element_type=F32)
-    result = result + jnp.dot(parts[2, used], box, preferred_element_type=F32)
+                lane = (2 * part + z // half) * LANES
+                parts[rows, lane : lane + LANES] = rounded
+    result = jnp.dot(parts[...], box_ref[...], preferred_element_type=F32)
 
     def of(f, z):
         start = (f * half + z % half) * side
@@ -140,10 +138,14 @@
 def force_message(weights, warped, planes, cells_ref, rows_ref, cols_ref, marks_ref):
     coarse = cells_ref.shape[0] // planes
     coarse_rows, side, _ = rows_ref.shape
+    rows = padded_rows(side)
     total = [[None] * coarse for _ in range(3)]
     for z in range(planes):
-        plane = warped(z)
-        slopes = (0.5 * (warped(z + 1) - warped(z - 1)), row_slope(plane), col_slope(plane))
+        slopes = (
+            warped(z + 1)[rows] - warped(z - 1)[rows],
+            row_difference(warped(z), side),
+            col_difference(warped(z)[rows]),
+        )
         for k in range(coarse):
             index = k * planes + z
             share = weights(z) * cells_ref[index : index + 1, :]
@@ -254,19 +256,20 @@
     z = part * planes + row % wide - REACH
     hats_ref[...] = jnp.where((z >= 0) & (z < total), hat(z, row // wide, total // SCALE), 0.0)
     row = sublane_index(cells_ref.shape)
-    cells_ref[...] = cell_weights(part * planes + row % planes, row // planes, total)
+    cells_ref[...] = cell_weights(part * planes + row % planes, row // planes)
     for a in range(coarse_rows):
-        rows_ref[a] = cell_weights(sublane_index((side, LANES)), a, side)
+        rows_ref[a] = 0.5 * cell_weights(sublane_index((side, LANES)), a)
     square = (LANES, LANES)
-    cols = cell_weights(sublane_index(square), lane_index(square) % coarse_cols, LANES)
+    cols = cell_weights(sublane_index(square), lane_index(square) % coarse_cols)
     for i, value in enumerate(split(cols, 2)):
         cols_ref[:, i * LANES : (i + 1) * LANES] = value
     apart = sublane_index(square) - lane_index(square)
     band = jnp.where(jnp.abs(apart) <= 4, 1.0, 0.0).astype(BF16)
     box_ref[...] = jnp.zeros(box_ref.shape, BF16)
-    for i in range(2):
-        box_ref[i * LANES : (i + 1) * LANES, i * LANES : (i + 1) * LANES] = band
-    slope_ref[...] = jnp.where(apart == 1, 0.5, jnp.where(apart == -1, -0.5, 0.0)).astype(BF16)
+    for i in range(6):
+        lane = (i % 2) * LANES
+        box_ref[i * LANES : (i + 1) * LANES, lane : lane + LANES] = band
+    slope_ref[...] = jnp.where(apart == 1, 1.0, jnp.where(apart == -1, -1.0, 0.0)).astype(BF16)
     lane = lane_index(square)
     source = (lane // width) * coarse_cols + lane % coarse_cols
     for g in range(spread_ref.shape[1] // LANES):
@@ -283,23 +286,23 @@
         hat_y_ref[:, a * LANES : (a + 1) * LANES] = chosen
     x = sublane_index((side, LANES)) + (place // GY) * side
     for r in range(block_rows * coarse_rows):
-        hat_x_ref[r] = hat(x, jnp.full((1, 1), r, jnp.int32), block_rows * coarse_rows)
+        hat_x_ref[r] = 0.5 * hat(x, jnp.full((1, 1), r, jnp.int32), block_rows * coarse_rows)
 
 
 def first_kernel(
     fixed_ref, moving_ref, near_ref, far_ref, marks_ref,
     cells_ref, rows_ref, cols_ref, box_ref,
     message_ref, mean_ref, variance_ref,
-    image, shifted, sums, parts, weight,
+    image, shifted, sums, threes, parts, weight,
 ):
     planes, side, _ = fixed_ref.shape
     odd = lax.axis_index("gz") % 2 == 1
     load_images(odd, fixed_ref, moving_ref, near_ref, far_ref, image, shifted)
     wide = planes + 2 * REACH
 
-    def fields(rows):
-        i = [image[z, rows] for z in range(wide)]
-        w = [shifted[z + 1, rows] for z in range(wide)]
+    def fields(start):
+        i = [image[z, start : start + 8] for z in range(wide)]
+        w = [shifted[z + 1, PAD + start : PAD + start + 8] for z in range(wide)]
         return (
             i,
             w,
@@ -308,7 +311,7 @@
             [a * b for a, b in zip(i, w)],
         )
 
-    of = box_sums(fields, planes, side, sums, parts, box_ref)
+    of = box_sums(fields, planes, side, sums, threes, parts, box_ref)
     for z in range(planes):
         mean_i, mean_w, mean_ii, mean_ww, mean_iw = [of(f, z) * (1.0 / 729.0) for f in range(5)]
         sii = mean_ii - mean_i * mean_i
@@ -319,11 +322,11 @@
         ratio = siw / (sii * sww + EPSILON)
         weight[z] = (2.0 * ratio) * (
             (image[z + REACH] - mean_i)
-            - siw / (sww + EPSILON) * (shifted[z + REACH + 1] - mean_w)
+            - siw / (sww + EPSILON) * (shifted[z + REACH + 1, padded_rows(side)] - mean_w)
         )
     row = force_message(
         lambda z: weight[z],
-        lambda z: shifted[z + REACH + 1],
+        lambda z: shifted.at[z + REACH + 1],
         planes, cells_ref, rows_ref, cols_ref, marks_ref,
     )
     message_ref[...] = jnp.broadcast_to(row[None], message_ref.shape)
@@ -334,7 +337,7 @@
     mean_ref, variance_ref, hats_ref, cells_ref, rows_ref, cols_ref, box_ref, slope_ref,
     spread_ref, hat_x_ref, hat_y_ref,
     message_ref, map_ref, velocity_ref,
-    image, shifted, warped, sums, parts, weight,
+    image, shifted, warped, sums, threes, parts, weight,
 ):
     planes, side, _ = fixed_ref.shape
     odd = lax.axis_index("gz") % 2 == 1
@@ -358,13 +361,14 @@
                     g = 8 * r + c * coarse + k
                     term = hat_x * along[g : g + 1, a * LANES : (a + 1) * LANES]
                     shift[c][k] = term if r + a == 0 else shift[c][k] + term
-    inner = shifted[1 : wide + 1].reshape(wide * side, LANES).astype(BF16)
+    rows = padded_rows(side)
+    inner = shifted[1 : wide + 1, rows].reshape(wide * side, LANES).astype(BF16)
     across = jnp.dot(inner, slope_ref[...], preferred_element_type=F32)
     for z in range(wide):
-        plane = shifted[z + 1]
+        plane = shifted[z + 1, rows]
         slopes = (
-            0.5 * (shifted[z + 2] - shifted[z]),
-            row_slope(plane),
+            shifted[z + 2, rows] - shifted[z, rows],
+            row_difference(shifted.at[z + 1], side),
             across[z * side : (z + 1) * side],
         )
         hats = [hats_ref[k * wide + z : k * wide + z + 1, :] for k in range(coarse)]
@@ -373,14 +377,15 @@
             for k in range(1, coarse):
                 u = u + hats[k] * shift[c][k]
             plane = plane + u * slopes[c]
-        warped[z] = plane
-
-    def fields(rows):
-        i = [image[z, rows] for z in range(wide)]
-        w = [warped[z, rows] for z in range(wide)]
+        warped[z, rows] = plane
+    clear_edges(warped, side)
+
+    def fields(start):
+        i = [image[z, start : start + 8] for z in range(wide)]
+        w = [warped[z, PAD + start : PAD + start + 8] for z in range(wide)]
         return (w, [b * b for b in w], [a * b for a, b in zip(i, w)])
 
-    of = box_sums(fields, planes, side, sums, parts, box_ref)
+    of = box_sums(fields, planes, side, sums, threes, parts, box_ref)
     for z in range(planes):
         mean_w, mean_ww, mean_iw = [of(f, z) * (1.0 / 729.0) for f in range(3)]
         mean_i = mean_ref[z]
@@ -390,11 +395,11 @@
         ratio = siw / (sii * sww + EPSILON)
         map_ref[z] = siw * ratio
         weight[z] = (2.0 * ratio) * (
-            (image[z + REACH] - mean_i) - siw / (sww + EPSILON) * (warped[z + REACH] - mean_w)
+            (image[z + REACH] - mean_i) - siw / (sww + EPSILON) * (warped[z + REACH, padded_rows(side)] - mean_w)
         )
     row = force_message(
         lambda z: weight[z],
-        lambda z: warped[z + REACH],
+        lambda z: warped.at[z + REACH],
         planes, cells_ref, rows_ref, cols_ref, marks_ref,
     )
     message_ref[...] = jnp.broadcast_to(row[None], message_ref.shape)
@@ -477,7 +482,7 @@
             ((coarse * planes, width), F32),
             ((coarse_rows, side, width), F32),
             ((width, 2 * width), BF16),
-            ((2 * width, 2 * width), BF16),
+            ((6 * width, 2 * width), BF16),
             ((width, width), BF16),
             ((width, 3 * coarse * width), BF16),
             ((block_rows * coarse_rows, side, width), F32),
@@ -491,12 +496,16 @@
 
     def scratch(fields):
         return [
-            pltpu.VMEM((fields, planes, side, width), F32),
-            pltpu.VMEM((3, fields * planes * side // 2, 2 * width), BF16),
+            pltpu.VMEM((fields, planes, side + 2 * PAD, width), F32),
+            pltpu.VMEM((fields, planes, side + 8, width), F32),
+            pltpu.VMEM((fields * planes * side // 2, 6 * width), BF16),
             pltpu.VMEM(field, F32),
         ]
 
-    images = [pltpu.VMEM((wide, side, width), F32), pltpu.VMEM((wide + 2, side, width), F32)]
+    images = [
+        pltpu.VMEM((wide, side, width), F32),
+        pltpu.VMEM((wide + 2, side + 2 * PAD, width), F32),
+    ]
     sent, mean, variance = call(
         first_kernel, [message, (field, F32), (field, F32)], images + scratch(5),
         fixed, moving, near, far, marks, cells, rows, cols, box,
@@ -505,7 +514,7 @@
     sent, correlation, velocity = call(
         second_kernel,
         [message, (field, F32), ((8 * block_rows, LANES), F32)],
-        images + [pltpu.VMEM((wide, side, width), F32)] + scratch(3),
+        images + [pltpu.VMEM((wide, side + 2 * PAD, width), F32)] + scratch(3),
         received, fixed, moving, near, far, marks,
         mean, variance, hats, cells, rows, cols, box, slope, spread, hat_x, hat_y,
     )

time: 33.4 us -> 33.1 us (level)
  no operation moved by 1% of the time
where the time goes in v4:
time: 33.1 us; the launch traced here: 32.8 us
  blocking collectives  21.7 us (66%)
  Pallas kernels  5.42 us (16%)
  starting transfers between devices  3.11 us (9%)
  between operations  1.98 us (6%)
  waiting for transfers between devices  0.67 us (2%)
    all_to_all x2, blocking collectives, per_device(): received = lax.all_to_all(sent, ('blk', 'gz'), 0, 0).reshape(devices, LANES)  21.7 us
    pallas_call x5, Pallas kernels, call(): pl.pallas_call(kernel, out_shape=[jax.ShapeDtypeStruct(shape, dtype) for...  5.42 us
    ppermute x1, starting transfers between devices, per_device(): lax.ppermute(far, ('blk', 'gz'), far_pairs(lax.axis_size('blk'), depth_pa...  2.55 us
    ppermute x1, waiting for transfers between devices, per_device(): lax.ppermute(far, ('blk', 'gz'), far_pairs(lax.axis_size('blk'), depth_pa...  0.67 us
  transfers between devices with their start and end apart: 2, of which 1 were waited for; matrix products, arithmetic and copies ran while one was open for 0% of the time, Pallas kernels for 1%

profile of v4, /device:TPU:0, one launch (start us, length us, event | category | flops | bytes accessed | tf_op | source)
XLA Modules:
  0.0 32.8 jit_solution(13334041626998733999)
XLA Ops:
  0.6 0.9 %shard_map.59 = (bf16[9,32,128]{2,1,0:T(8,128)(2,1)S(1)}, bf16[9,32,128]{2,1,0:T(8,128)(2,1)S(1)}, bf16[8,32,128]{2,1,0:T(8,128)(2,1)S(1)}, bf16[8,32,128]{2,1,0:T(8,128)(2,1)S(1)}) custom-call(bf16[1,8,32,128]{3,2,1,0:T(8,128)(2,1)} %fixed_hbm.1, bf16[1,8,32,128]{3,2,1,0:T(8,128)(2,1)} %moving_hbm.1), custom_call_target="tpu_custom_call" | custom-call | tf_op jit(solution)/shard_map/pallas_call | solution.py:443
  1.5 0.6 %collective-permute-start = (bf16[9,32,128]{2,1,0:T(8,128)(2,1)S(1)}, bf16[9,32,128]{2,1,0:T(8,128)(2,1)S(1)}, u32[]{:S(2)}, u32[]{:S(2)}) collective-permute-start(bf16[9,32,128]{2,1,0:T(8,128)(2,1)S(1)} %get-tuple-element.24), channel_id=1, source_target_pairs={{0,1},{2,3},{1,0},{3,2},{4,5},{6,7},{5,4},{7,6},{8,9},{10,11},{9,8... | collective-permute-start | bytes 221192 | tf_op jit(solution)/shard_map/ppermute | solution.py:476
  2.1 2.6 %collective-permute-start.1 = (bf16[9,32,128]{2,1,0:T(8,128)(2,1)S(1)}, bf16[9,32,128]{2,1,0:T(8,128)(2,1)S(1)}, u32[]{:S(2)}, u32[]{:S(2)}) collective-permute-start(bf16[9,32,128]{2,1,0:T(8,128)(2,1)S(1)} %get-tuple-element.25), channel_id=1, source_target_pairs={{1,2},{2,1},{0,4},{3,7},{5,6},{6,5},{4,0},{7,3},{9,10},{10,9},{8,1... | collective-permute-start | bytes 221192 | tf_op jit(solution)/shard_map/ppermute | solution.py:474
  6.0 0.3 %shard_map.60 = (f32[8,128]{1,0:T(8,128)S(1)}, f32[32,128]{1,0:T(8,128)S(1)}, f32[16,128]{1,0:T(8,128)S(1)}, f32[2,32,128]{2,1,0:T(8,128)S(1)}, bf16[128,256]{1,...) custom-call(s32[2,1]{1,0:T(2,128)S(1)} %pad_add_fusion.both_ref), custom_call_target="tpu_custom_call" | custom-call | tf_op jit(solution)/shard_map/pallas_call | solution.py:443
  6.3 0.0 collective-permute-done.near_ref
  6.3 0.7 %collective-permute-done.1.far_ref = bf16[9,32,128]{2,1,0:T(8,128)(2,1)S(1)} collective-permute-done((bf16[9,32,128]{2,1,0:T(8,128)(2,1)S(1)}, bf16[9,32,128]{2,1,0:T(8,128)(2,1)S(1)}, u32[]{:S(2)}, u32[]{:S(2)}) %collective-permute-start.1) | collective-permute-done | bytes 73760 | tf_op jit(solution)/shard_map/ppermute | solution.py:474
  7.0 1.2 %shard_map.61 = (f32[32,1,128]{2,1,0:T(1,128)S(1)}, f32[8,32,128]{2,1,0:T(8,128)S(1)}, f32[8,32,128]{2,1,0:T(8,128)S(1)}) custom-call(bf16[8,32,128]{2,1,0:T(8,128)(2,1)S(1)} %get-tuple-element.22.fixed_ref, bf16[8,32,128]{2,1,0:T(8,128)(2,1)S(1)} %get-tuple-element.23.moving_ref, bf16[9,32,128]{2,1,0:T(8,128)(2,1)S(1)} %collective-permute-done.near_ref, ...), custom_call_target="tpu_custom_call" | custom-call | tf_op jit(solution)/shard_map/pallas_call | solution.py:443
  8.2 12.8 %all_to_all.10 = f32[32,1,128]{2,1,0:T(1,128)S(1)} all-to-all(f32[32,1,128]{2,1,0:T(1,128)S(1)} %get-tuple-element.31), channel_id=1, replica_groups=mesh['blk'=8,'gz'=4] {'blk','gz'}, dimensions={0} | all-to-all | bytes 32768 | tf_op jit(solution)/shard_map/all_to_all | solution.py:513
  21.0 1.7 %shard_map.62 = (f32[32,1,128]{2,1,0:T(1,128)S(1)}, f32[8,32,128]{2,1,0:T(8,128)S(1)}, f32[8,128]{1,0:T(8,128)S(1)}) custom-call(f32[32,128]{1,0:T(8,128)S(1)} %bitcast.6, bf16[8,32,128]{2,1,0:T(8,128)(2,1)S(1)} %get-tuple-element.22.fixed_ref, bf16[8,32,128]{2,1,0:T(8,128)(2,1)S(1)} %get-tuple-element.23.moving_ref, ...), custom_call_target="tpu_custom_call" | custom-call | tf_op jit(solution)/shard_map/pallas_call | solution.py:443
  22.7 8.9 %all_to_all.11 = f32[32,1,128]{2,1,0:T(1,128)S(1)} all-to-all(f32[32,1,128]{2,1,0:T(1,128)S(1)} %get-tuple-element.39), channel_id=1, replica_groups=mesh['blk'=8,'gz'=4] {'blk','gz'}, dimensions={0} | all-to-all | bytes 32768 | tf_op jit(solution)/shard_map/all_to_all | solution.py:521
  31.6 1.3 %shard_map.63 = (f32[3,2,2,64]{3,2,1,0:T(2,128)}, f32[1,8,32,128]{3,2,1,0:T(8,128)}) custom-call(f32[32,128]{1,0:T(8,128)S(1)} %bitcast.7, f32[8,128]{1,0:T(8,128)S(1)} %get-tuple-element.40.velocity_ref, bf16[128,768]{1,0:T(8,128)(2,1)S(1)} %get-tuple-element.36.spread_ref, f32[8,32,128]{2,1,0:T(8,128)S(1)} %get-tuple-element.41.map_ref), custom_call_target="tpu_custom_call" | custom-call | tf_op jit(solution)/shard_map/pallas_call | solution.py:443
  (1 shorter events, 0.0 us)
Async XLA Ops:
  1.5 4.8 %collective-permute-start = (bf16[9,32,128]{2,1,0:T(8,128)(2,1)S(1)}, bf16[9,32,128]{2,1,0:T(8,128)(2,1)S(1)}, u32[]{:S(2)}, u32[]{:S(2)}) collective-permute-start(bf16[9,32,128]{2,1,0:T(8,128)(2,1)S(1)} %get-tuple-element.24), channel_id=1, source_target_pairs={{0,1},{2,3},{1,0},{3,2},{4,5},{6,7},{5,4},{7,6},{8,9},{10,11},{9,8... | collective-permute-start | bytes 221192 | tf_op jit(solution)/shard_map/ppermute | solution.py:476
  2.1 4.9 %collective-permute-start.1 = (bf16[9,32,128]{2,1,0:T(8,128)(2,1)S(1)}, bf16[9,32,128]{2,1,0:T(8,128)(2,1)S(1)}, u32[]{:S(2)}, u32[]{:S(2)}) collective-permute-start(bf16[9,32,128]{2,1,0:T(8,128)(2,1)S(1)} %get-tuple-element.25), channel_id=1, source_target_pairs={{1,2},{2,1},{0,4},{3,7},{5,6},{6,5},{4,0},{7,3},{9,10},{10,9},{8,1... | collective-permute-start | bytes 221192 | tf_op jit(solution)/shard_map/ppermute | solution.py:474

commit v5 on v4

--- a/solution.py
+++ b/solution.py
@@ -97,17 +97,19 @@
     return upper - lower
 
 
-def load_images(odd, fixed_ref, moving_ref, near_ref, far_ref, image, shifted):
+def load_images(odd, fixed_ref, moving_ref, near_ref, far_ref, halves, image, shifted):
     planes, side, _ = fixed_ref.shape
     rows = padded_rows(side)
+    below = jnp.where(odd, 0, 1)
+    halves[below] = near_ref[...]
+    halves[1 - below] = far_ref[...]
     clear_edges(shifted, side)
+    image[0:REACH] = halves[0, 0:REACH].astype(F32)
     image[REACH : REACH + planes] = fixed_ref[...].astype(F32)
+    image[REACH + planes :] = halves[1, 0:REACH].astype(F32)
+    shifted[0 : REACH + 1, rows] = halves[0, REACH:].astype(F32)
     shifted[REACH + 1 : REACH + 1 + planes, rows] = moving_ref[...].astype(F32)
-    for ref, low in ((near_ref, odd), (far_ref, ~odd)):
-        start = jnp.where(low, 0, REACH + planes)
-        image[pl.ds(start, REACH)] = ref[0:REACH].astype(F32)
-        start = jnp.where(low, 0, REACH + 1 + planes)
-        shifted[pl.ds(start, REACH + 1), rows] = ref[REACH:].astype(F32)
+    shifted[REACH + 1 + planes :, rows] = halves[1, REACH:].astype(F32)
 
 
 def box_sums(fields, planes, side, sums, threes, parts, box_ref):
@@ -133,6 +135,38 @@
         return result[start : start + side, lane : lane + LANES]
 
     return of
+
+
+def column_boxes(fixed, moving, side, single, double, box_ref):
+    for i in range(REACH):
+        for h in range(2):
+            lane = h * LANES
+            planes = (fixed(i, h), moving(i, h))
+            for f, plane in enumerate(planes):
+                start = (f * REACH + i) * side
+                single[start : start + side, lane : lane + LANES] = plane
+            a, b = (plane.astype(F32) for plane in planes)
+            for f, product in enumerate((a * a, b * b, a * b)):
+                start = (f * REACH + i) * side
+                high, low = split(product, 2)
+                double[start : start + side, lane : lane + LANES] = high
+                double[start : start + side, 2 * LANES + lane : 3 * LANES + lane] = low
+    ones = jnp.dot(single[...], box_ref[0 : 2 * LANES], preferred_element_type=F32)
+    twos = jnp.dot(double[...], box_ref[0 : 4 * LANES], preferred_element_type=F32)
+
+    def of(f, i, h):
+        source, f = (ones, f) if f < 2 else (twos, f - 2)
+        start = (f * REACH + i) * side
+        return source[start : start + side, h * LANES : (h + 1) * LANES]
+
+    return of
+
+
+def running(items):
+    total = [items[0]]
+    for item in items[1:]:
+        total.append(total[-1] + item)
+    return total
 
 
 def force_message(weights, warped, planes, cells_ref, rows_ref, cols_ref, marks_ref):
@@ -172,48 +206,40 @@
     return jnp.where(lane[0:1] == len(tiles) * coarse_cols, marks_ref[0:1], row)
 
 
-def regular_grid(received, spread_ref, block_rows, coarse_rows, coarse_cols):
-    groups = spread_ref.shape[1] // LANES
+def regular_grid(received, spread_ref, coarse, block_rows, coarse_rows, coarse_cols):
+    groups = 3 * coarse
     used = groups * coarse_rows * coarse_cols
     width = GY * coarse_cols
     place = received[:, used : used + 1].astype(jnp.int32)
-    lane = lane_index(received.shape)
-    here = (place % GY) == (lane % width) // coarse_cols
+    here = (place % GY) == lane_index(received.shape) // coarse_cols
     block_row = place // GY
     sub = sublane_index((8, LANES))
-    grids = [jnp.zeros((8, LANES), F32) for _ in range(block_rows)]
     entries = exact_dot(received, spread_ref[...])
-    for g in range(groups):
-        entry = entries[:, g * LANES : (g + 1) * LANES]
-        for r in range(block_rows):
-            chosen = here if block_rows == 1 else here & (block_row == r)
-            total = jnp.sum(jnp.where(chosen, entry, 0.0), axis=0, keepdims=True)
-            grids[r] = jnp.where(sub == g, total, grids[r])
-    even = sub % 2 == 0
-    lane = lane_index((8, LANES))
-    column = lane % width
-    first = lane < width
+    grids = []
+    for r in range(block_rows):
+        chosen = here if block_rows == 1 else here & (block_row == r)
+        for a in range(coarse_rows):
+            grid = jnp.zeros((8, LANES), F32)
+            for g in range(groups):
+                start = (a * groups + g) * LANES
+                entry = jnp.where(chosen, entries[:, start : start + LANES], 0.0)
+                grid = jnp.where(sub == g, jnp.sum(entry, axis=0, keepdims=True), grid)
+            grids.append(grid)
+    none = [jnp.zeros((8, LANES), F32)]
     grids = [
-        0.5 * g + 0.25 * jnp.where(even, pltpu.roll(g, 7, 0), pltpu.roll(g, 1, 0)) for g in grids
+        0.5 * g + 0.25 * (before + after)
+        for g, before, after in zip(grids, none + grids[:-1], grids[1:] + none)
     ]
-    other = [pltpu.roll(g, width, 1) for g in grids]
-    none = jnp.zeros((8, LANES), F32)
-    before = [none] + other[:-1]
-    after = other[1:] + [none]
+    inside = lane_index((8, LANES)) < width
     grids = [
-        0.5 * g + 0.25 * (o + jnp.where(first, b, a))
-        for g, o, b, a in zip(grids, other, before, after)
-    ]
-    grids = [
-        0.25 * jnp.where(column > 0, pltpu.roll(g, 1, 1), 0.0)
-        + 0.5 * g
-        + 0.25 * jnp.where(column < width - 1, pltpu.roll(g, LANES - 1, 1), 0.0)
+        jnp.where(
+            inside, 0.5 * g + 0.25 * (pltpu.roll(g, 1, 1) + pltpu.roll(g, LANES - 1, 1)), 0.0
+        )
         for g in grids
     ]
-    grids = [jnp.where(sub < groups, g, 0.0) for g in grids]
     square = functools.reduce(lambda a, b: a + b, [g * g for g in grids])
-    square = jnp.sum(jnp.sum(square, axis=1, keepdims=True), axis=0, keepdims=True)
-    mean = square * (1.0 / (groups * block_rows * LANES))
+    square = jnp.sum(jnp.sum(square, axis=0, keepdims=True), axis=1, keepdims=True)
+    mean = square * (1.0 / (groups * len(grids) * width))
     factor = STEP_LENGTH / jnp.sqrt(mean + EPSILON)
     return [g * factor for g in grids]
 
@@ -242,10 +268,12 @@
 
 
 def table_kernel(
-    both_ref,
+    both_ref, fixed_ref, moving_ref,
     marks_ref, hats_ref, cells_ref, rows_ref, cols_ref, box_ref, slope_ref, spread_ref, hat_x_ref, hat_y_ref,
-    *, planes, block_rows,
+    own_ref, single, double, sums, threes,
+    *, block_rows,
 ):
+    planes = fixed_ref.shape[0]
     part = lax.axis_index("gz")
     total = planes * lax.axis_size("gz")
     coarse_rows, side, _ = rows_ref.shape
@@ -271,49 +299,68 @@
         box_ref[i * LANES : (i + 1) * LANES, lane : lane + LANES] = band
     slope_ref[...] = jnp.where(apart == 1, 1.0, jnp.where(apart == -1, -1.0, 0.0)).astype(BF16)
     lane = lane_index(square)
-    source = (lane // width) * coarse_cols + lane % coarse_cols
-    for g in range(spread_ref.shape[1] // LANES):
-        hit = sublane_index(square) == source + g * coarse_rows * coarse_cols
-        spread_ref[:, g * LANES : (g + 1) * LANES] = jnp.where(hit, 1.0, 0.0).astype(BF16)
+    entry = sublane_index(square)
+    coarse = total // SCALE
+    group = coarse_rows * coarse_cols
+    for a in range(coarse_rows):
+        for c in range(3):
+            for k in range(coarse):
+                value = jnp.zeros(square, F32)
+                for other, weight in ((k - 1, 0.25), (k, 0.5), (k + 1, 0.25)):
+                    if 0 <= other < coarse:
+                        start = (c * coarse + other) * group + a * coarse_cols
+                        hit = (entry == start + lane % coarse_cols) & (lane < width)
+                        value = jnp.where(hit, weight, value)
+                start = ((a * 3 + c) * coarse + k) * LANES
+                spread_ref[:, start : start + LANES] = value.astype(BF16)
     row = sublane_index(marks_ref.shape)
     marks_ref[...] = jnp.where(row == 0, both_ref[0:1, 0:1], both_ref[1:2, 0:1]).astype(F32)
     place = both_ref[0:1, 0:1]
     y = lane + (place % GY) * LANES
-    entry = sublane_index(square)
-    hat_y = hat(y, entry % width, width)
-    for a in range(coarse_rows):
-        chosen = jnp.where(entry // width == a, hat_y, 0.0).astype(BF16)
-        hat_y_ref[:, a * LANES : (a + 1) * LANES] = chosen
+    hat_y_ref[...] = jnp.where(entry < width, hat(y, entry, width), 0.0).astype(BF16)
     x = sublane_index((side, LANES)) + (place // GY) * side
     for r in range(block_rows * coarse_rows):
         hat_x_ref[r] = 0.5 * hat(x, jnp.full((1, 1), r, jnp.int32), block_rows * coarse_rows)
 
+    of = column_boxes(
+        lambda i, h: fixed_ref[i + REACH * h],
+        lambda i, h: moving_ref[i + REACH * h],
+        side, single, double, box_ref,
+    )
+    clear_edges(sums, side)
+    for f in range(5):
+        boxed = [of(f, i, h) for h in range(2) for i in range(REACH)]
+        up, down = running(boxed), running(boxed[::-1])[::-1]
+        for z in range(planes):
+            sums[f, z, padded_rows(side)] = up[z + REACH] if z < REACH else down[z - REACH]
+            own_ref[f, z] = row_box(sums.at[f, z], threes.at[f, z], side)
+
 
 def first_kernel(
     fixed_ref, moving_ref, near_ref, far_ref, marks_ref,
-    cells_ref, rows_ref, cols_ref, box_ref,
-    message_ref, mean_ref, variance_ref,
-    image, shifted, sums, threes, parts, weight,
+    cells_ref, rows_ref, cols_ref, box_ref, own_ref,
+    message_ref, mean_ref, variance_ref, image, shifted,
+    halves, single, double, sums, threes, weight,
 ):
     planes, side, _ = fixed_ref.shape
     odd = lax.axis_index("gz") % 2 == 1
-    load_images(odd, fixed_ref, moving_ref, near_ref, far_ref, image, shifted)
-    wide = planes + 2 * REACH
-
-    def fields(start):
-        i = [image[z, start : start + 8] for z in range(wide)]
-        w = [shifted[z + 1, PAD + start : PAD + start + 8] for z in range(wide)]
-        return (
-            i,
-            w,
-            [a * a for a in i],
-            [b * b for b in w],
-            [a * b for a, b in zip(i, w)],
-        )
-
-    of = box_sums(fields, planes, side, sums, threes, parts, box_ref)
+    load_images(odd, fixed_ref, moving_ref, near_ref, far_ref, halves, image, shifted)
+    of = column_boxes(
+        lambda i, h: halves[h, i],
+        lambda i, h: halves[h, REACH + i + 1 - h],
+        side, single, double, box_ref,
+    )
+    clear_edges(sums, side)
+    for f in range(5):
+        below = running([of(f, i, 0) for i in range(REACH)][::-1])[::-1]
+        above = running([of(f, i, 1) for i in range(REACH)])
+        for z, item in enumerate(below + above):
+            sums[f, z, padded_rows(side)] = item
     for z in range(planes):
-        mean_i, mean_w, mean_ii, mean_ww, mean_iw = [of(f, z) * (1.0 / 729.0) for f in range(5)]
+        mean_i, mean_w, mean_ii, mean_ww, mean_iw = [
+            (row_box(sums.at[f, z], threes.at[f, z], side) + own_ref[f, z]) * (1.0 / 729.0)
+            for f in range(5)
+        ]
         sii = mean_ii - mean_i * mean_i
         sww = mean_ww - mean_w * mean_w
         siw = mean_iw - mean_i * mean_w
@@ -333,50 +380,47 @@
 
 
 def second_kernel(
-    received_ref, fixed_ref, moving_ref, near_ref, far_ref, marks_ref,
+    received_ref, image, shifted, marks_ref,
     mean_ref, variance_ref, hats_ref, cells_ref, rows_ref, cols_ref, box_ref, slope_ref,
     spread_ref, hat_x_ref, hat_y_ref,
     message_ref, map_ref, velocity_ref,
-    image, shifted, warped, sums, threes, parts, weight,
+    slopes, warped, sums, threes, parts, weight,
 ):
-    planes, side, _ = fixed_ref.shape
-    odd = lax.axis_index("gz") % 2 == 1
-    load_images(odd, fixed_ref, moving_ref, near_ref, far_ref, image, shifted)
+    planes, side, _ = mean_ref.shape
     wide = planes + 2 * REACH
     coarse_rows = rows_ref.shape[0]
     coarse_cols = LANES // SCALE
-    block_rows = velocity_ref.shape[0] // 8
+    block_rows = velocity_ref.shape[0] // 8 // coarse_rows
     coarse = hats_ref.shape[0] // wide
-
-    grids = regular_grid(received_ref[...], spread_ref, block_rows, coarse_rows, coarse_cols)
-    for r in range(block_rows):
-        velocity_ref[8 * r : 8 * r + 8] = grids[r]
-    along = exact_dot(jnp.concatenate(grids, axis=0), hat_y_ref[...])
-    shift = [[None] * coarse for _ in range(3)]
-    for r in range(block_rows):
-        for a in range(coarse_rows):
-            hat_x = hat_x_ref[r * coarse_rows + a]
-            for c in range(3):
-                for k in range(coarse):
-                    g = 8 * r + c * coarse + k
-                    term = hat_x * along[g : g + 1, a * LANES : (a + 1) * LANES]
-                    shift[c][k] = term if r + a == 0 else shift[c][k] + term
     rows = padded_rows(side)
     inner = shifted[1 : wide + 1, rows].reshape(wide * side, LANES).astype(BF16)
     across = jnp.dot(inner, slope_ref[...], preferred_element_type=F32)
     for z in range(wide):
+        slopes[0, z] = shifted[z + 2, rows] - shifted[z, rows]
+        slopes[1, z] = row_difference(shifted.at[z + 1], side)
+        slopes[2, z] = across[z * side : (z + 1) * side]
+
+    grids = regular_grid(
+        received_ref[...], spread_ref, coarse, block_rows, coarse_rows, coarse_cols
+    )
+    for r, grid in enumerate(grids):
+        velocity_ref[8 * r : 8 * r + 8] = grid
+    along = exact_dot(jnp.concatenate(grids, axis=0), hat_y_ref[...])
+    shift = [[None] * coarse for _ in range(3)]
+    for r in range(len(grids)):
+        for c in range(3):
+            for k in range(coarse):
+                g = 8 * r + c * coarse + k
+                term = hat_x_ref[r] * along[g : g + 1]
+                shift[c][k] = term if r == 0 else shift[c][k] + term
+    for z in range(wide):
         plane = shifted[z + 1, rows]
-        slopes = (
-            shifted[z + 2, rows] - shifted[z, rows],
-            row_difference(shifted.at[z + 1], side),
-            across[z * side : (z + 1) * side],
-        )
         hats = [hats_ref[k * wide + z : k * wide + z + 1, :] for k in range(coarse)]
         for c in range(3):
             u = hats[0] * shift[c][0]
             for k in range(1, coarse):
                 u = u + hats[k] * shift[c][k]
-            plane = plane + u * slopes[c]
+            plane = plane + u * slopes[c, z]
         warped[z, rows] = plane
     clear_edges(warped, side)
 
@@ -405,23 +449,28 @@
     message_ref[...] = jnp.broadcast_to(row[None], message_ref.shape)
 
 
-def last_kernel(received_ref, velocity_ref, spread_ref, map_ref, out_ref, map_hbm, sem):
-    copy = pltpu.make_async_copy(map_ref, map_hbm.at[0], sem)
-    copy.start()
+def last_kernel(
+    received_ref, velocity_ref, spread_ref, map_ref, out_hbm, map_hbm, out_ref, sems
+):
+    map_copy = pltpu.make_async_copy(map_ref, map_hbm.at[0], sems.at[0])
+    map_copy.start()
     _, coarse, rows, width = out_ref.shape
-    coarse_rows = LANES // width
+    coarse_cols = width // GY
+    coarse_rows = spread_ref.shape[1] // (3 * coarse * LANES)
     block_rows = rows // coarse_rows
-    grids = regular_grid(received_ref[...], spread_ref, block_rows, coarse_rows, width // GY)
-    for r in range(block_rows):
-        velocity = velocity_ref[8 * r : 8 * r + 8] + grids[r]
+    grids = regular_grid(
+        received_ref[...], spread_ref, coarse, block_rows, coarse_rows, coarse_cols
+    )
+    for r, grid in enumerate(grids):
+        velocity = velocity_ref[8 * r : 8 * r + 8] + grid
         for c in range(3):
             for k in range(coarse):
                 g = c * coarse + k
-                for a in range(coarse_rows):
-                    out_ref[c, k, r * coarse_rows + a : r * coarse_rows + a + 1, :] = velocity[
-                        g : g + 1, a * width : (a + 1) * width
-                    ]
-    copy.wait()
+                out_ref[c, k, r : r + 1, :] = velocity[g : g + 1, :width]
+    out_copy = pltpu.make_async_copy(out_ref, out_hbm, sems.at[1])
+    out_copy.start()
+    map_copy.wait()
+    out_copy.wait()
 
 
 def far_pairs(blocks, parts):
@@ -452,7 +501,7 @@
 
 def per_device(fixed, moving, block_place, tissue):
     slots, planes, side, width = fixed.shape
-    assert slots == 1 and width == LANES
+    assert slots == 1 and width == LANES and planes == 2 * REACH
     depth_parts = lax.axis_size("gz")
     devices = lax.axis_size("blk") * depth_parts
     blocks = slots * lax.axis_size("blk")
@@ -474,8 +523,14 @@
     far = lax.ppermute(far, ("blk", "gz"), far_pairs(lax.axis_size("blk"), depth_parts))
     pairs = [(i, i + 1) for i in range(0, depth_parts, 2)]
     near = lax.ppermute(near, "gz", pairs + [(b, a) for a, b in pairs])
-    marks, hats, cells, rows, cols, box, slope, spread, hat_x, hat_y = call(
-        functools.partial(table_kernel, planes=planes, block_rows=block_rows),
+    boxes = [
+        pltpu.VMEM((2 * REACH * side, 2 * width), BF16),
+        pltpu.VMEM((3 * REACH * side, 4 * width), BF16),
+        pltpu.VMEM((5, planes, side + 2 * PAD, width), F32),
+        pltpu.VMEM((5, planes, side + 8, width), F32),
+    ]
+    marks, hats, cells, rows, cols, box, slope, spread, hat_x, hat_y, own = call(
+        functools.partial(table_kernel, block_rows=block_rows),
         [
             ((8, width), F32),
             ((coarse * wide, width), F32),
@@ -484,51 +539,53 @@
             ((width, 2 * width), BF16),
             ((6 * width, 2 * width), BF16),
             ((width, width), BF16),
-            ((width, 3 * coarse * width), BF16),
+            ((width, coarse_rows * 3 * coarse * width), BF16),
             ((block_rows * coarse_rows, side, width), F32),
-            ((width, coarse_rows * width), BF16),
+            ((width, width), BF16),
+            ((5,) + field, F32),
         ],
-        [],
-        jnp.stack([block_place, tissue]),
+        boxes,
+        jnp.stack([block_place, tissue]), fixed, moving,
     )
 
     message = ((devices, 1, LANES), F32)
 
-    def scratch(fields):
-        return [
-            pltpu.VMEM((fields, planes, side + 2 * PAD, width), F32),
-            pltpu.VMEM((fields, planes, side + 8, width), F32),
-            pltpu.VMEM((fields * planes * side // 2, 6 * width), BF16),
-            pltpu.VMEM(field, F32),
-        ]
-
-    images = [
-        pltpu.VMEM((wide, side, width), F32),
-        pltpu.VMEM((wide + 2, side + 2 * PAD, width), F32),
-    ]
-    sent, mean, variance = call(
-        first_kernel, [message, (field, F32), (field, F32)], images + scratch(5),
-        fixed, moving, near, far, marks, cells, rows, cols, box,
+    sent, mean, variance, image, shifted = call(
+        first_kernel,
+        [
+            message,
+            (field, F32),
+            (field, F32),
+            ((wide, side, width), F32),
+            ((wide + 2, side + 2 * PAD, width), F32),
+        ],
+        [pltpu.VMEM((2,) + halo[0], BF16)] + boxes + [pltpu.VMEM(field, F32)],
+        fixed, moving, near, far, marks, cells, rows, cols, box, own,
     )
     received = lax.all_to_all(sent, ("blk", "gz"), 0, 0).reshape(devices, LANES)
     sent, correlation, velocity = call(
         second_kernel,
-        [message, (field, F32), ((8 * block_rows, LANES), F32)],
-        images + [pltpu.VMEM((wide, side + 2 * PAD, width), F32)] + scratch(3),
-        received, fixed, moving, near, far, marks,
+        [message, (field, F32), ((8 * block_rows * coarse_rows, LANES), F32)],
+        [
+            pltpu.VMEM((3, wide, side, width), F32),
+            pltpu.VMEM((wide, side + 2 * PAD, width), F32),
+            pltpu.VMEM((3, planes, side + 2 * PAD, width), F32),
+            pltpu.VMEM((3, planes, side + 8, width), F32),
+            pltpu.VMEM((3 * planes * side // 2, 6 * width), BF16),
+            pltpu.VMEM(field, F32),
+        ],
+        received, image, shifted, marks,
         mean, variance, hats, cells, rows, cols, box, slope, spread, hat_x, hat_y,
     )
     received = lax.all_to_all(sent, ("blk", "gz"), 0, 0).reshape(devices, LANES)
+    grid = (3, coarse, block_rows * coarse_rows, GY * coarse_cols)
     return tuple(
         call(
             last_kernel,
-            [
-                ((3, coarse, block_rows * coarse_rows, GY * coarse_cols), F32),
-                ((slots,) + field, F32),
-            ],
-            [pltpu.SemaphoreType.DMA(())],
+            [(grid, F32), ((slots,) + field, F32)],
+            [pltpu.VMEM(grid, F32), pltpu.SemaphoreType.DMA((2,))],
             received, velocity, spread, correlation,
-            out_specs=[VMEM, HBM],
+            out_specs=[HBM, HBM],
         )
     )
 

time: 33.1 us -> 32.5 us (0.982)
  waiting for transfers between devices: 0.67 us -> 0.23 us
    ppermute x1, waiting for transfers between devices: 0.67 us -> 0.22 us  [per_device(): lax.ppermute(far, ('blk', 'gz'), far_pairs(lax.axis_size('blk'), depth_pa...]
  transfers between devices with their start and end apart: 2 -> 2, of which waited for: 1 -> 1; matrix products, arithmetic and copies ran while one was open for 0% -> 0% of each run, Pallas kernels for 1% -> 2%
where the time goes in v5:
time: 32.5 us; the launch traced here: 32.3 us
  blocking collectives  21.7 us (67%)
  Pallas kernels  5.32 us (16%)
  starting transfers between devices  3.11 us (10%)
  between operations  1.97 us (6%)
    all_to_all x2, blocking collectives, per_device(): received = lax.all_to_all(sent, ('blk', 'gz'), 0, 0).reshape(devices, LANES)  21.7 us
    pallas_call x5, Pallas kernels, call(): pl.pallas_call(kernel, out_shape=[jax.ShapeDtypeStruct(shape, dtype) for...  5.32 us
    ppermute x1, starting transfers between devices, per_device(): lax.ppermute(far, ('blk', 'gz'), far_pairs(lax.axis_size('blk'), depth_pa...  2.55 us
  transfers between devices with their start and end apart: 2, of which 1 were waited for; matrix products, arithmetic and copies ran while one was open for 0% of the time, Pallas kernels for 2%

profile of v5, /device:TPU:0, one launch (start us, length us, event | category | flops | bytes accessed | tf_op | source)
XLA Modules:
  0.0 32.3 jit_solution(17044244684804567943)
XLA Ops:
  0.6 0.9 %shard_map.59 = (bf16[9,32,128]{2,1,0:T(8,128)(2,1)S(1)}, bf16[9,32,128]{2,1,0:T(8,128)(2,1)S(1)}, bf16[8,32,128]{2,1,0:T(8,128)(2,1)S(1)}, bf16[8,32,128]{2,1,0:T(8,128)(2,1)S(1)}) custom-call(bf16[1,8,32,128]{3,2,1,0:T(8,128)(2,1)} %fixed_hbm.1, bf16[1,8,32,128]{3,2,1,0:T(8,128)(2,1)} %moving_hbm.1), custom_call_target="tpu_custom_call" | custom-call | tf_op jit(solution)/shard_map/pallas_call | solution.py:492
  1.5 0.6 %collective-permute-start = (bf16[9,32,128]{2,1,0:T(8,128)(2,1)S(1)}, bf16[9,32,128]{2,1,0:T(8,128)(2,1)S(1)}, u32[]{:S(2)}, u32[]{:S(2)}) collective-permute-start(bf16[9,32,128]{2,1,0:T(8,128)(2,1)S(1)} %get-tuple-element.27), channel_id=1, source_target_pairs={{0,1},{2,3},{1,0},{3,2},{4,5},{6,7},{5,4},{7,6},{8,9},{10,11},{9,8... | collective-permute-start | bytes 221192 | tf_op jit(solution)/shard_map/ppermute | solution.py:525
  2.1 2.6 %collective-permute-start.1 = (bf16[9,32,128]{2,1,0:T(8,128)(2,1)S(1)}, bf16[9,32,128]{2,1,0:T(8,128)(2,1)S(1)}, u32[]{:S(2)}, u32[]{:S(2)}) collective-permute-start(bf16[9,32,128]{2,1,0:T(8,128)(2,1)S(1)} %get-tuple-element.28), channel_id=1, source_target_pairs={{1,2},{2,1},{0,4},{3,7},{5,6},{6,5},{4,0},{7,3},{9,10},{10,9},{8,1... | collective-permute-start | bytes 221192 | tf_op jit(solution)/shard_map/ppermute | solution.py:523
  6.0 0.8 %shard_map.60 = (f32[8,128]{1,0:T(8,128)S(1)}, f32[32,128]{1,0:T(8,128)S(1)}, f32[16,128]{1,0:T(8,128)S(1)}, f32[2,32,128]{2,1,0:T(8,128)S(1)}, bf16[128,256]{1,...) custom-call(s32[2,1]{1,0:T(2,128)S(1)} %pad_add_fusion.both_ref, ...), custom_call_target="tpu_custom_call" | custom-call | tf_op jit(solution)/shard_map/pallas_call | solution.py:492
  6.8 0.0 collective-permute-done.near_ref
  6.8 0.2 collective-permute-done.1.far_ref
  7.0 1.0 %shard_map.61 = (f32[32,1,128]{2,1,0:T(1,128)S(1)}, f32[8,32,128]{2,1,0:T(8,128)S(1)}, f32[8,32,128]{2,1,0:T(8,128)S(1)}, f32[16,32,128]{2,1,0:T(8,128)S(1)}, f32[18,48,128]{2,1,0:T(8,128)S(1)}) custom-call(bf16[8,32,128]{2,1,0:T(8,128)(2,1)S(1)} %get-tuple-element.25.fixed_ref, bf16[8,32,128]{2,1,0:T(8,128)(2,1)S(1)} %get-tuple-element.26.moving_ref, ...), custom_call_target="tpu_custom_call" | custom-call | tf_op jit(solution)/shard_map/pallas_call | solution.py:492
  7.9 12.8 %all_to_all.10 = f32[32,1,128]{2,1,0:T(1,128)S(1)} all-to-all(f32[32,1,128]{2,1,0:T(1,128)S(1)} %get-tuple-element.35), channel_id=1, replica_groups=mesh['blk'=8,'gz'=4] {'blk','gz'}, dimensions={0} | all-to-all | bytes 32768 | tf_op jit(solution)/shard_map/all_to_all | solution.py:565
  20.7 1.7 %shard_map.62 = (f32[32,1,128]{2,1,0:T(1,128)S(1)}, f32[8,32,128]{2,1,0:T(8,128)S(1)}, f32[16,128]{1,0:T(8,128)S(1)}) custom-call(f32[32,128]{1,0:T(8,128)S(1)} %bitcast.6, f32[16,32,128]{2,1,0:T(8,128)S(1)} %get-tuple-element.36.image, f32[18,48,128]{2,1,0:T(8,128)S(1)} %get-tuple-element.37.shifted, f32[8,128]{1,0:T(8,128)S(1)} %get-tuple-element.29.marks_ref, ...), custom_call_target="tpu_custom_call" | custom-call | tf_op jit(solution)/shard_map/pallas_call | solution.py:492
  22.4 8.9 %all_to_all.11 = f32[32,1,128]{2,1,0:T(1,128)S(1)} all-to-all(f32[32,1,128]{2,1,0:T(1,128)S(1)} %get-tuple-element.45), channel_id=1, replica_groups=mesh['blk'=8,'gz'=4] {'blk','gz'}, dimensions={0} | all-to-all | bytes 32768 | tf_op jit(solution)/shard_map/all_to_all | solution.py:580
  31.3 1.0 %shard_map.63 = (f32[3,2,2,64]{3,2,1,0:T(2,128)}, f32[1,8,32,128]{3,2,1,0:T(8,128)}) custom-call(f32[32,128]{1,0:T(8,128)S(1)} %bitcast.7, f32[16,128]{1,0:T(8,128)S(1)} %get-tuple-element.46.velocity_ref, bf16[128,1536]{1,0:T(8,128)(2,1)S(1)} %get-tuple-element.42.spread_ref, f32[8,32,128]{2,1,0:T(8,128)S(1)} %get-tuple-element.47.map_ref), custom_call_target="tpu_custom_call" | custom-call | tf_op jit(solution)/shard_map/pallas_call | solution.py:492
  (1 shorter events, 0.0 us)
Async XLA Ops:
  1.5 5.2 %collective-permute-start = (bf16[9,32,128]{2,1,0:T(8,128)(2,1)S(1)}, bf16[9,32,128]{2,1,0:T(8,128)(2,1)S(1)}, u32[]{:S(2)}, u32[]{:S(2)}) collective-permute-start(bf16[9,32,128]{2,1,0:T(8,128)(2,1)S(1)} %get-tuple-element.27), channel_id=1, source_target_pairs={{0,1},{2,3},{1,0},{3,2},{4,5},{6,7},{5,4},{7,6},{8,9},{10,11},{9,8... | collective-permute-start | bytes 221192 | tf_op jit(solution)/shard_map/ppermute | solution.py:525
  2.1 4.9 %collective-permute-start.1 = (bf16[9,32,128]{2,1,0:T(8,128)(2,1)S(1)}, bf16[9,32,128]{2,1,0:T(8,128)(2,1)S(1)}, u32[]{:S(2)}, u32[]{:S(2)}) collective-permute-start(bf16[9,32,128]{2,1,0:T(8,128)(2,1)S(1)} %get-tuple-element.28), channel_id=1, source_target_pairs={{1,2},{2,1},{0,4},{3,7},{5,6},{6,5},{4,0},{7,3},{9,10},{10,9},{8,1... | collective-permute-start | bytes 221192 | tf_op jit(solution)/shard_map/ppermute | solution.py:523

commit v6 on v5

--- a/solution.py
+++ b/solution.py
@@ -51,11 +51,12 @@
     return parts
 
 
-def exact_dot(value, table):
+def close_dot(value, table):
     rows = value.shape[0]
-    stacked = jnp.concatenate(split(value, 3), axis=0)
-    product = jnp.dot(stacked, table, preferred_element_type=F32)
-    return product[:rows] + product[rows : 2 * rows] + product[2 * rows :]
+    product = jnp.dot(
+        jnp.concatenate(split(value, 2), axis=0), table, preferred_element_type=F32
+    )
+    return product[:rows] + product[rows:]
 
 
 def window_of_nine(items):
@@ -120,44 +121,59 @@
         for f, items in enumerate(fields(8 * tile)):
             for z, item in enumerate(window_of_nine(items)):
                 sums[f, z, PAD + 8 * tile : PAD + 8 * tile + 8] = item
-    for f in range(count):
-        for z in range(planes):
-            total = row_box(sums.at[f, z], threes.at[f, z], side)
-            rows = slice((f * half + z % half) * side, (f * half + z % half + 1) * side)
-            for part, rounded in enumerate(split(total, 3)):
-                lane = (2 * part + z // half) * LANES
-                parts[rows, lane : lane + LANES] = rounded
-    result = jnp.dot(parts[...], box_ref[...], preferred_element_type=F32)
+    step = half // 4
+    results = []
+    for first in range(0, half, step):
+        for i in range(first, first + step):
+            for f in range(count):
+                start = (i * count + f) * side
+                for h in range(2):
+                    z = i + h * half
+                    total = row_box(sums.at[f, z], threes.at[f, z], side)
+                    for part, rounded in enumerate(split(total, 3)):
+                        lane = (2 * part + h) * LANES
+                        parts[start : start + side, lane : lane + LANES] = rounded
+        used = slice(first * count * side, (first + step) * count * side)
+        results.append(jnp.dot(parts[used], box_ref[...], preferred_element_type=F32))
 
     def of(f, z):
-        start = (f * half + z % half) * side
-        lane = (z // half) * LANES
-        return result[start : start + side, lane : lane + LANES]
+        i, lane = z % half, (z // half) * LANES
+        start = ((i % step) * count + f) * side
+        return results[i // step][start : start + side, lane : lane + LANES]
 
     return of
 
 
 def column_boxes(fixed, moving, side, single, double, box_ref):
-    for i in range(REACH):
-        for h in range(2):
-            lane = h * LANES
-            planes = (fixed(i, h), moving(i, h))
-            for f, plane in enumerate(planes):
-                start = (f * REACH + i) * side
-                single[start : start + side, lane : lane + LANES] = plane
-            a, b = (plane.astype(F32) for plane in planes)
-            for f, product in enumerate((a * a, b * b, a * b)):
-                start = (f * REACH + i) * side
-                high, low = split(product, 2)
-                double[start : start + side, lane : lane + LANES] = high
-                double[start : start + side, 2 * LANES + lane : 3 * LANES + lane] = low
-    ones = jnp.dot(single[...], box_ref[0 : 2 * LANES], preferred_element_type=F32)
-    twos = jnp.dot(double[...], box_ref[0 : 4 * LANES], preferred_element_type=F32)
+    step = REACH // 1
+    results = []
+    for first in range(0, REACH, step):
+        for i in range(first, first + step):
+            for h in range(2):
+                lane = h * LANES
+                planes = (fixed(i, h), moving(i, h))
+                for f, plane in enumerate(planes):
+                    start = (2 * i + f) * side
+                    single[start : start + side, lane : lane + LANES] = plane
+                a, b = (plane.astype(F32) for plane in planes)
+                for f, product in enumerate((a * a, b * b, a * b)):
+                    start = (3 * i + f) * side
+                    high, low = split(product, 2)
+                    double[start : start + side, lane : lane + LANES] = high
+                    double[start : start + side, 2 * LANES + lane : 3 * LANES + lane] = low
+        ones = single[2 * first * side : 2 * (first + step) * side]
+        twos = double[3 * first * side : 3 * (first + step) * side]
+        results.append(
+            (
+                jnp.dot(ones, box_ref[0 : 2 * LANES], preferred_element_type=F32),
+                jnp.dot(twos, box_ref[0 : 4 * LANES], preferred_element_type=F32),
+            )
+        )
 
     def of(f, i, h):
-        source, f = (ones, f) if f < 2 else (twos, f - 2)
-        start = (f * REACH + i) * side
-        return source[start : start + side, h * LANES : (h + 1) * LANES]
+        source, count, f = (0, 2, f) if f < 2 else (1, 3, f - 2)
+        start = ((i % step) * count + f) * side
+        return results[i // step][source][start : start + side, h * LANES : (h + 1) * LANES]
 
     return of
 
@@ -195,7 +211,7 @@
                 for start in range(8, side, 8):
                     tile = tile + product[start : start + 8]
                 tiles.append(tile)
-    sums = exact_dot(jnp.concatenate(tiles, axis=0), cols_ref[...])
+    sums = close_dot(jnp.concatenate(tiles, axis=0), cols_ref[...])
     sums = sums[:, :LANES] + sums[:, LANES:]
     coarse_cols = LANES // SCALE
     lane = lane_index((8, LANES))
@@ -214,7 +230,7 @@
     here = (place % GY) == lane_index(received.shape) // coarse_cols
     block_row = place // GY
     sub = sublane_index((8, LANES))
-    entries = exact_dot(received, spread_ref[...])
+    entries = close_dot(received, spread_ref[...])
     grids = []
     for r in range(block_rows):
         chosen = here if block_rows == 1 else here & (block_row == r)
@@ -240,8 +256,7 @@
     square = functools.reduce(lambda a, b: a + b, [g * g for g in grids])
     square = jnp.sum(jnp.sum(square, axis=0, keepdims=True), axis=1, keepdims=True)
     mean = square * (1.0 / (groups * len(grids) * width))
-    factor = STEP_LENGTH / jnp.sqrt(mean + EPSILON)
-    return [g * factor for g in grids]
+    return grids, STEP_LENGTH / jnp.sqrt(mean + EPSILON)
 
 
 def pack_kernel(fixed_hbm, moving_hbm, near_ref, far_ref, fixed_ref, moving_ref, sems):
@@ -270,7 +285,7 @@
 def table_kernel(
     both_ref, fixed_ref, moving_ref,
     marks_ref, hats_ref, cells_ref, rows_ref, cols_ref, box_ref, slope_ref, spread_ref, hat_x_ref, hat_y_ref,
-    own_ref, single, double, sums, threes,
+    own_ref, across_ref, single, double, sums, threes,
     *, block_rows,
 ):
     planes = fixed_ref.shape[0]
@@ -297,7 +312,12 @@
     for i in range(6):
         lane = (i % 2) * LANES
         box_ref[i * LANES : (i + 1) * LANES, lane : lane + LANES] = band
-    slope_ref[...] = jnp.where(apart == 1, 1.0, jnp.where(apart == -1, -1.0, 0.0)).astype(BF16)
+    slope = jnp.where(apart == 1, 1.0, jnp.where(apart == -1, -1.0, 0.0)).astype(BF16)
+    slope_ref[...] = slope
+    across = jnp.dot(
+        moving_ref[...].reshape(planes * side, LANES), slope, preferred_element_type=F32
+    )
+    across_ref[...] = across.reshape(across_ref.shape)
     lane = lane_index(square)
     entry = sublane_index(square)
     coarse = total // SCALE
@@ -338,8 +358,8 @@
 
 def first_kernel(
     fixed_ref, moving_ref, near_ref, far_ref, marks_ref,
-    cells_ref, rows_ref, cols_ref, box_ref, own_ref,
-    message_ref, mean_ref, variance_ref, image, shifted,
+    cells_ref, rows_ref, cols_ref, box_ref, slope_ref, own_ref,
+    message_ref, mean_ref, variance_ref, image, shifted, across_ref,
     halves, single, double, sums, threes, weight,
 ):
     planes, side, _ = fixed_ref.shape
@@ -350,6 +370,12 @@
         lambda i, h: halves[h, REACH + i + 1 - h],
         side, single, double, box_ref,
     )
+    for h in range(2):
+        planes_h = halves[h, REACH + 1 - h : 2 * REACH + 1 - h]
+        across = jnp.dot(
+            planes_h.reshape(REACH * side, LANES), slope_ref[...], preferred_element_type=F32
+        )
+        across_ref[h] = across.reshape(across_ref.shape[1:])
     clear_edges(sums, side)
     for f in range(5):
         below = running([of(f, i, 0) for i in range(REACH)][::-1])[::-1]
@@ -381,8 +407,8 @@
 
 def second_kernel(
     received_ref, image, shifted, marks_ref,
-    mean_ref, variance_ref, hats_ref, cells_ref, rows_ref, cols_ref, box_ref, slope_ref,
-    spread_ref, hat_x_ref, hat_y_ref,
+    mean_ref, variance_ref, hats_ref, cells_ref, rows_ref, cols_ref, box_ref, own_across_ref,
+    across_ref, spread_ref, hat_x_ref, hat_y_ref,
     message_ref, map_ref, velocity_ref,
     slopes, warped, sums, threes, parts, weight,
 ):
@@ -393,19 +419,16 @@
     block_rows = velocity_ref.shape[0] // 8 // coarse_rows
     coarse = hats_ref.shape[0] // wide
     rows = padded_rows(side)
-    inner = shifted[1 : wide + 1, rows].reshape(wide * side, LANES).astype(BF16)
-    across = jnp.dot(inner, slope_ref[...], preferred_element_type=F32)
     for z in range(wide):
         slopes[0, z] = shifted[z + 2, rows] - shifted[z, rows]
         slopes[1, z] = row_difference(shifted.at[z + 1], side)
-        slopes[2, z] = across[z * side : (z + 1) * side]
-
-    grids = regular_grid(
+
+    grids, factor = regular_grid(
         received_ref[...], spread_ref, coarse, block_rows, coarse_rows, coarse_cols
     )
+    along = close_dot(jnp.concatenate(grids, axis=0), hat_y_ref[...]) * factor
     for r, grid in enumerate(grids):
-        velocity_ref[8 * r : 8 * r + 8] = grid
-    along = exact_dot(jnp.concatenate(grids, axis=0), hat_y_ref[...])
+        velocity_ref[8 * r : 8 * r + 8] = grid * factor
     shift = [[None] * coarse for _ in range(3)]
     for r in range(len(grids)):
         for c in range(3):
@@ -413,14 +436,24 @@
                 g = 8 * r + c * coarse + k
                 term = hat_x_ref[r] * along[g : g + 1]
                 shift[c][k] = term if r == 0 else shift[c][k] + term
+    change = [[shift[c][k] - shift[c][0] for k in range(coarse)] for c in range(3)]
     for z in range(wide):
         plane = shifted[z + 1, rows]
         hats = [hats_ref[k * wide + z : k * wide + z + 1, :] for k in range(coarse)]
-        for c in range(3):
-            u = hats[0] * shift[c][0]
+        inside = functools.reduce(lambda a, b: a + b, hats)
+        if z < REACH:
+            across = across_ref[0, z]
+        elif z < REACH + planes:
+            across = own_across_ref[z - REACH]
+        else:
+            across = across_ref[1, z - REACH - planes]
+        for c, slope in enumerate((slopes[0, z], slopes[1, z], across)):
+            if c == 0 and not REACH <= z < REACH + planes:
+                slope = slope * inside
+            u = shift[c][0]
             for k in range(1, coarse):
-                u = u + hats[k] * shift[c][k]
-            plane = plane + u * slopes[c, z]
+                u = u + hats[k] * change[c][k]
+            plane = plane + u * slope
         warped[z, rows] = plane
     clear_edges(warped, side)
 
@@ -458,11 +491,11 @@
     coarse_cols = width // GY
     coarse_rows = spread_ref.shape[1] // (3 * coarse * LANES)
     block_rows = rows // coarse_rows
-    grids = regular_grid(
+    grids, factor = regular_grid(
         received_ref[...], spread_ref, coarse, block_rows, coarse_rows, coarse_cols
     )
     for r, grid in enumerate(grids):
-        velocity = velocity_ref[8 * r : 8 * r + 8] + grid
+        velocity = velocity_ref[8 * r : 8 * r + 8] + grid * factor
         for c in range(3):
             for k in range(coarse):
                 g = c * coarse + k
@@ -529,7 +562,7 @@
         pltpu.VMEM((5, planes, side + 2 * PAD, width), F32),
         pltpu.VMEM((5, planes, side + 8, width), F32),
     ]
-    marks, hats, cells, rows, cols, box, slope, spread, hat_x, hat_y, own = call(
+    marks, hats, cells, rows, cols, box, slope, spread, hat_x, hat_y, own, own_across = call(
         functools.partial(table_kernel, block_rows=block_rows),
         [
             ((8, width), F32),
@@ -543,6 +576,7 @@
             ((block_rows * coarse_rows, side, width), F32),
             ((width, width), BF16),
             ((5,) + field, F32),
+            (field, F32),
         ],
         boxes,
         jnp.stack([block_place, tissue]), fixed, moving,
@@ -550,7 +584,7 @@
 
     message = ((devices, 1, LANES), F32)
 
-    sent, mean, variance, image, shifted = call(
+    sent, mean, variance, image, shifted, across = call(
         first_kernel,
         [
             message,
@@ -558,16 +592,17 @@
             (field, F32),
             ((wide, side, width), F32),
             ((wide + 2, side + 2 * PAD, width), F32),
+            ((2, REACH, side, width), F32),
         ],
         [pltpu.VMEM((2,) + halo[0], BF16)] + boxes + [pltpu.VMEM(field, F32)],
-        fixed, moving, near, far, marks, cells, rows, cols, box, own,
+        fixed, moving, near, far, marks, cells, rows, cols, box, slope, own,
     )
     received = lax.all_to_all(sent, ("blk", "gz"), 0, 0).reshape(devices, LANES)
     sent, correlation, velocity = call(
         second_kernel,
         [message, (field, F32), ((8 * block_rows * coarse_rows, LANES), F32)],
         [
-            pltpu.VMEM((3, wide, side, width), F32),
+            pltpu.VMEM((2, wide, side, width), F32),
             pltpu.VMEM((wide, side + 2 * PAD, width), F32),
             pltpu.VMEM((3, planes, side + 2 * PAD, width), F32),
             pltpu.VMEM((3, planes, side + 8, width), F32),
@@ -575,7 +610,8 @@
             pltpu.VMEM(field, F32),
         ],
         received, image, shifted, marks,
-        mean, variance, hats, cells, rows, cols, box, slope, spread, hat_x, hat_y,
+        mean, variance, hats, cells, rows, cols, box, own_across, across,
+        spread, hat_x, hat_y,
     )
     received = lax.all_to_all(sent, ("blk", "gz"), 0, 0).reshape(devices, LANES)
     grid = (3, coarse, block_rows * coarse_rows, GY * coarse_cols)

time: 32.5 us -> 32.2 us (level)
  no operation moved by 1% of the time
where the time goes in v6:
time: 32.2 us; the launch traced here: 32 us
  blocking collectives  21.7 us (67%)
  Pallas kernels  5.02 us (16%)
  starting transfers between devices  3.11 us (10%)
  between operations  1.97 us (6%)
    all_to_all x2, blocking collectives, per_device(): received = lax.all_to_all(sent, ('blk', 'gz'), 0, 0).reshape(devices, LANES)  21.7 us
    pallas_call x5, Pallas kernels, call(): pl.pallas_call(kernel, out_shape=[jax.ShapeDtypeStruct(shape, dtype) for...  5.02 us
    ppermute x1, starting transfers between devices, per_device(): lax.ppermute(far, ('blk', 'gz'), far_pairs(lax.axis_size('blk'), depth_pa...  2.55 us
  transfers between devices with their start and end apart: 2, of which 1 were waited for; matrix products, arithmetic and copies ran while one was open for 0% of the time, Pallas kernels for 2%

profile of v6, /device:TPU:0, one launch (start us, length us, event | category | flops | bytes accessed | tf_op | source)
XLA Modules:
  0.0 32.0 jit_solution(4596918677617549030)
XLA Ops:
  0.6 0.9 %shard_map.59 = (bf16[9,32,128]{2,1,0:T(8,128)(2,1)S(1)}, bf16[9,32,128]{2,1,0:T(8,128)(2,1)S(1)}, bf16[8,32,128]{2,1,0:T(8,128)(2,1)S(1)}, bf16[8,32,128]{2,1,0:T(8,128)(2,1)S(1)}) custom-call(bf16[1,8,32,128]{3,2,1,0:T(8,128)(2,1)} %fixed_hbm.1, bf16[1,8,32,128]{3,2,1,0:T(8,128)(2,1)} %moving_hbm.1), custom_call_target="tpu_custom_call" | custom-call | tf_op jit(solution)/shard_map/pallas_call | solution.py:525
  1.5 0.6 %collective-permute-start = (bf16[9,32,128]{2,1,0:T(8,128)(2,1)S(1)}, bf16[9,32,128]{2,1,0:T(8,128)(2,1)S(1)}, u32[]{:S(2)}, u32[]{:S(2)}) collective-permute-start(bf16[9,32,128]{2,1,0:T(8,128)(2,1)S(1)} %get-tuple-element.29), channel_id=1, source_target_pairs={{0,1},{2,3},{1,0},{3,2},{4,5},{6,7},{5,4},{7,6},{8,9},{10,11},{9,8... | collective-permute-start | bytes 221192 | tf_op jit(solution)/shard_map/ppermute | solution.py:558
  2.1 2.6 %collective-permute-start.1 = (bf16[9,32,128]{2,1,0:T(8,128)(2,1)S(1)}, bf16[9,32,128]{2,1,0:T(8,128)(2,1)S(1)}, u32[]{:S(2)}, u32[]{:S(2)}) collective-permute-start(bf16[9,32,128]{2,1,0:T(8,128)(2,1)S(1)} %get-tuple-element.30), channel_id=1, source_target_pairs={{1,2},{2,1},{0,4},{3,7},{5,6},{6,5},{4,0},{7,3},{9,10},{10,9},{8,1... | collective-permute-start | bytes 221192 | tf_op jit(solution)/shard_map/ppermute | solution.py:556
  6.0 0.8 %shard_map.60 = (f32[8,128]{1,0:T(8,128)S(1)}, f32[32,128]{1,0:T(8,128)S(1)}, f32[16,128]{1,0:T(8,128)S(1)}, f32[2,32,128]{2,1,0:T(8,128)S(1)}, bf16[128,256]{1,...) custom-call(s32[2,1]{1,0:T(2,128)S(1)} %pad_add_fusion.both_ref, ...), custom_call_target="tpu_custom_call" | custom-call | tf_op jit(solution)/shard_map/pallas_call | solution.py:525
  6.7 0.0 collective-permute-done.near_ref
  6.8 0.2 collective-permute-done.1.far_ref
  7.0 0.9 %shard_map.61 = (f32[32,1,128]{2,1,0:T(1,128)S(1)}, f32[8,32,128]{2,1,0:T(8,128)S(1)}, f32[8,32,128]{2,1,0:T(8,128)S(1)}, f32[16,32,128]{2,1,0:T(8,128)S(1)}, f3...) custom-call(bf16[8,32,128]{2,1,0:T(8,128)(2,1)S(1)} %get-tuple-element.27.fixed_ref, ...), custom_call_target="tpu_custom_call" | custom-call | tf_op jit(solution)/shard_map/pallas_call | solution.py:525
  7.9 12.8 %all_to_all.10 = f32[32,1,128]{2,1,0:T(1,128)S(1)} all-to-all(f32[32,1,128]{2,1,0:T(1,128)S(1)} %get-tuple-element.38), channel_id=1, replica_groups=mesh['blk'=8,'gz'=4] {'blk','gz'}, dimensions={0} | all-to-all | bytes 32768 | tf_op jit(solution)/shard_map/all_to_all | solution.py:600
  20.7 1.4 %shard_map.62 = (f32[32,1,128]{2,1,0:T(1,128)S(1)}, f32[8,32,128]{2,1,0:T(8,128)S(1)}, f32[16,128]{1,0:T(8,128)S(1)}) custom-call(f32[32,128]{1,0:T(8,128)S(1)} %bitcast.6, f32[16,32,128]{2,1,0:T(8,128)S(1)} %get-tuple-element.39.image, f32[18,48,128]{2,1,0:T(8,128)S(1)} %get-tuple-element.40.shifted, f32[8,128]{1,0:T(8,128)S(1)} %get-tuple-element.31.marks_ref, ...), custom_call_target="tpu_custom_call" | custom-call | tf_op jit(solution)/shard_map/pallas_call | solution.py:525
  22.1 8.9 %all_to_all.11 = f32[32,1,128]{2,1,0:T(1,128)S(1)} all-to-all(f32[32,1,128]{2,1,0:T(1,128)S(1)} %get-tuple-element.49), channel_id=1, replica_groups=mesh['blk'=8,'gz'=4] {'blk','gz'}, dimensions={0} | all-to-all | bytes 32768 | tf_op jit(solution)/shard_map/all_to_all | solution.py:616
  31.0 1.0 %shard_map.63 = (f32[3,2,2,64]{3,2,1,0:T(2,128)}, f32[1,8,32,128]{3,2,1,0:T(8,128)}) custom-call(f32[32,128]{1,0:T(8,128)S(1)} %bitcast.7, f32[16,128]{1,0:T(8,128)S(1)} %get-tuple-element.50.velocity_ref, bf16[128,1536]{1,0:T(8,128)(2,1)S(1)} %get-tuple-element.46.spread_ref, f32[8,32,128]{2,1,0:T(8,128)S(1)} %get-tuple-element.51.map_ref), custom_call_target="tpu_custom_call" | custom-call | tf_op jit(solution)/shard_map/pallas_call | solution.py:525
  (1 shorter events, 0.0 us)
Async XLA Ops:
  1.5 5.2 %collective-permute-start = (bf16[9,32,128]{2,1,0:T(8,128)(2,1)S(1)}, bf16[9,32,128]{2,1,0:T(8,128)(2,1)S(1)}, u32[]{:S(2)}, u32[]{:S(2)}) collective-permute-start(bf16[9,32,128]{2,1,0:T(8,128)(2,1)S(1)} %get-tuple-element.29), channel_id=1, source_target_pairs={{0,1},{2,3},{1,0},{3,2},{4,5},{6,7},{5,4},{7,6},{8,9},{10,11},{9,8... | collective-permute-start | bytes 221192 | tf_op jit(solution)/shard_map/ppermute | solution.py:558
  2.1 4.9 %collective-permute-start.1 = (bf16[9,32,128]{2,1,0:T(8,128)(2,1)S(1)}, bf16[9,32,128]{2,1,0:T(8,128)(2,1)S(1)}, u32[]{:S(2)}, u32[]{:S(2)}) collective-permute-start(bf16[9,32,128]{2,1,0:T(8,128)(2,1)S(1)} %get-tuple-element.30), channel_id=1, source_target_pairs={{1,2},{2,1},{0,4},{3,7},{5,6},{6,5},{4,0},{7,3},{9,10},{10,9},{8,1... | collective-permute-start | bytes 221192 | tf_op jit(solution)/shard_map/ppermute | solution.py:556

commit v7 on v6

--- a/solution.py
+++ b/solution.py
@@ -96,21 +96,6 @@
     upper = jnp.where(lane < width - 1, pltpu.roll(plane, width - 1, 1), 0.0)
     lower = jnp.where(lane > 0, pltpu.roll(plane, 1, 1), 0.0)
     return upper - lower
-
-
-def load_images(odd, fixed_ref, moving_ref, near_ref, far_ref, halves, image, shifted):
-    planes, side, _ = fixed_ref.shape
-    rows = padded_rows(side)
-    below = jnp.where(odd, 0, 1)
-    halves[below] = near_ref[...]
-    halves[1 - below] = far_ref[...]
-    clear_edges(shifted, side)
-    image[0:REACH] = halves[0, 0:REACH].astype(F32)
-    image[REACH : REACH + planes] = fixed_ref[...].astype(F32)
-    image[REACH + planes :] = halves[1, 0:REACH].astype(F32)
-    shifted[0 : REACH + 1, rows] = halves[0, REACH:].astype(F32)
-    shifted[REACH + 1 : REACH + 1 + planes, rows] = moving_ref[...].astype(F32)
-    shifted[REACH + 1 + planes :, rows] = halves[1, REACH:].astype(F32)
 
 
 def box_sums(fields, planes, side, sums, threes, parts, box_ref):
@@ -185,22 +170,17 @@
     return total
 
 
-def force_message(weights, warped, planes, cells_ref, rows_ref, cols_ref, marks_ref):
+def force_message(weights, slopes, planes, cells_ref, rows_ref, cols_ref, marks_ref):
     coarse = cells_ref.shape[0] // planes
     coarse_rows, side, _ = rows_ref.shape
-    rows = padded_rows(side)
     total = [[None] * coarse for _ in range(3)]
     for z in range(planes):
-        slopes = (
-            warped(z + 1)[rows] - warped(z - 1)[rows],
-            row_difference(warped(z), side),
-            col_difference(warped(z)[rows]),
-        )
+        directions = slopes(z)
         for k in range(coarse):
             index = k * planes + z
             share = weights(z) * cells_ref[index : index + 1, :]
             for c in range(3):
-                term = share * slopes[c]
+                term = share * directions[c]
                 total[c][k] = term if z == 0 else total[c][k] + term
     tiles = []
     for c in range(3):
@@ -246,6 +226,7 @@
         0.5 * g + 0.25 * (before + after)
         for g, before, after in zip(grids, none + grids[:-1], grids[1:] + none)
     ]
+    before_columns = grids
     inside = lane_index((8, LANES)) < width
     grids = [
         jnp.where(
@@ -256,7 +237,7 @@
     square = functools.reduce(lambda a, b: a + b, [g * g for g in grids])
     square = jnp.sum(jnp.sum(square, axis=0, keepdims=True), axis=1, keepdims=True)
     mean = square * (1.0 / (groups * len(grids) * width))
-    return grids, STEP_LENGTH / jnp.sqrt(mean + EPSILON)
+    return before_columns, grids, STEP_LENGTH / jnp.sqrt(mean + EPSILON)
 
 
 def pack_kernel(fixed_hbm, moving_hbm, near_ref, far_ref, fixed_ref, moving_ref, sems):
@@ -285,7 +266,8 @@
 def table_kernel(
     both_ref, fixed_ref, moving_ref,
     marks_ref, hats_ref, cells_ref, rows_ref, cols_ref, box_ref, slope_ref, spread_ref, hat_x_ref, hat_y_ref,
-    own_ref, across_ref, single, double, sums, threes,
+    own_ref, image_ref, planes_ref, down_ref, across_ref,
+    single, double, sums, threes,
     *, block_rows,
 ):
     planes = fixed_ref.shape[0]
@@ -318,6 +300,11 @@
         moving_ref[...].reshape(planes * side, LANES), slope, preferred_element_type=F32
     )
     across_ref[...] = across.reshape(across_ref.shape)
+    image_ref[...] = fixed_ref[...].astype(F32)
+    clear_edges(planes_ref, side)
+    planes_ref[:, padded_rows(side)] = moving_ref[...].astype(F32)
+    for z in range(planes):
+        down_ref[z] = row_difference(planes_ref.at[z], side)
     lane = lane_index(square)
     entry = sublane_index(square)
     coarse = total // SCALE
@@ -337,7 +324,9 @@
     marks_ref[...] = jnp.where(row == 0, both_ref[0:1, 0:1], both_ref[1:2, 0:1]).astype(F32)
     place = both_ref[0:1, 0:1]
     y = lane + (place % GY) * LANES
-    hat_y_ref[...] = jnp.where(entry < width, hat(y, entry, width), 0.0).astype(BF16)
+    hat_y = jnp.where(entry < width, hat(y, entry, width), 0.0)
+    hat_y = 0.5 * hat_y + 0.25 * (pltpu.roll(hat_y, 1, 0) + pltpu.roll(hat_y, LANES - 1, 0))
+    hat_y_ref[...] = jnp.where(entry < width, hat_y, 0.0).astype(BF16)
     x = sublane_index((side, LANES)) + (place // GY) * side
     for r in range(block_rows * coarse_rows):
         hat_x_ref[r] = 0.5 * hat(x, jnp.full((1, 1), r, jnp.int32), block_rows * coarse_rows)
@@ -357,30 +346,26 @@
 
 
 def first_kernel(
-    fixed_ref, moving_ref, near_ref, far_ref, marks_ref,
-    cells_ref, rows_ref, cols_ref, box_ref, slope_ref, own_ref,
-    message_ref, mean_ref, variance_ref, image, shifted, across_ref,
-    halves, single, double, sums, threes, weight,
+    image_ref, planes_ref, down_ref, across_ref, near_ref, far_ref, marks_ref,
+    cells_ref, rows_ref, cols_ref, box_ref, own_ref,
+    message_ref, mean_ref, variance_ref, halves,
+    single, double, sums, threes, weight,
 ):
-    planes, side, _ = fixed_ref.shape
-    odd = lax.axis_index("gz") % 2 == 1
-    load_images(odd, fixed_ref, moving_ref, near_ref, far_ref, halves, image, shifted)
+    planes, side, _ = image_ref.shape
+    rows = padded_rows(side)
+    below = lax.rem(lax.axis_index("gz") + 1, 2)
+    halves[below] = near_ref[...]
+    halves[1 - below] = far_ref[...]
     of = column_boxes(
         lambda i, h: halves[h, i],
         lambda i, h: halves[h, REACH + i + 1 - h],
         side, single, double, box_ref,
     )
-    for h in range(2):
-        planes_h = halves[h, REACH + 1 - h : 2 * REACH + 1 - h]
-        across = jnp.dot(
-            planes_h.reshape(REACH * side, LANES), slope_ref[...], preferred_element_type=F32
-        )
-        across_ref[h] = across.reshape(across_ref.shape[1:])
     clear_edges(sums, side)
     for f in range(5):
-        below = running([of(f, i, 0) for i in range(REACH)][::-1])[::-1]
-        above = running([of(f, i, 1) for i in range(REACH)])
-        for z, item in enumerate(below + above):
+        low = running([of(f, i, 0) for i in range(REACH)][::-1])[::-1]
+        high = running([of(f, i, 1) for i in range(REACH)])
+        for z, item in enumerate(low + high):
             sums[f, z, padded_rows(side)] = item
     for z in range(planes):
         mean_i, mean_w, mean_ii, mean_ww, mean_iw = [
@@ -394,23 +379,28 @@
         variance_ref[z] = sii
         ratio = siw / (sii * sww + EPSILON)
         weight[z] = (2.0 * ratio) * (
-            (image[z + REACH] - mean_i)
-            - siw / (sww + EPSILON) * (shifted[z + REACH + 1, padded_rows(side)] - mean_w)
+            (image_ref[z] - mean_i) - siw / (sww + EPSILON) * (planes_ref[z, rows] - mean_w)
         )
+
+    def plane(z):
+        if z < 0:
+            return halves[0, 2 * REACH + 1 + z].astype(F32)
+        return planes_ref[z, rows] if z < planes else halves[1, REACH + z - planes].astype(F32)
+
     row = force_message(
         lambda z: weight[z],
-        lambda z: shifted.at[z + REACH + 1],
+        lambda z: (plane(z + 1) - plane(z - 1), down_ref[z], across_ref[z]),
         planes, cells_ref, rows_ref, cols_ref, marks_ref,
     )
     message_ref[...] = jnp.broadcast_to(row[None], message_ref.shape)
 
 
 def second_kernel(
-    received_ref, image, shifted, marks_ref,
-    mean_ref, variance_ref, hats_ref, cells_ref, rows_ref, cols_ref, box_ref, own_across_ref,
-    across_ref, spread_ref, hat_x_ref, hat_y_ref,
+    received_ref, halves, image_ref, planes_ref, down_ref, across_ref, marks_ref,
+    mean_ref, variance_ref, hats_ref, cells_ref, rows_ref, cols_ref, box_ref, slope_ref,
+    spread_ref, hat_x_ref, hat_y_ref,
     message_ref, map_ref, velocity_ref,
-    slopes, warped, sums, threes, parts, weight,
+    images, outer, outer_across, slopes, shift_ref, warped, sums, threes, parts, weight,
 ):
     planes, side, _ = mean_ref.shape
     wide = planes + 2 * REACH
@@ -419,14 +409,21 @@
     block_rows = velocity_ref.shape[0] // 8 // coarse_rows
     coarse = hats_ref.shape[0] // wide
     rows = padded_rows(side)
-    for z in range(wide):
-        slopes[0, z] = shifted[z + 2, rows] - shifted[z, rows]
-        slopes[1, z] = row_difference(shifted.at[z + 1], side)
-
-    grids, factor = regular_grid(
+
+    def image(z):
+        if z < 0:
+            return images.at[0, z + REACH]
+        return image_ref.at[z] if z < planes else images.at[1, z - planes]
+
+    def moving(z):
+        if z < 0:
+            return outer.at[0, z + REACH + 1]
+        return planes_ref.at[z] if z < planes else outer.at[1, z - planes]
+
+    before_columns, grids, factor = regular_grid(
         received_ref[...], spread_ref, coarse, block_rows, coarse_rows, coarse_cols
     )
-    along = close_dot(jnp.concatenate(grids, axis=0), hat_y_ref[...]) * factor
+    along = close_dot(jnp.concatenate(before_columns, axis=0), hat_y_ref[...]) * factor
     for r, grid in enumerate(grids):
         velocity_ref[8 * r : 8 * r + 8] = grid * factor
     shift = [[None] * coarse for _ in range(3)]
@@ -436,50 +433,75 @@
                 g = 8 * r + c * coarse + k
                 term = hat_x_ref[r] * along[g : g + 1]
                 shift[c][k] = term if r == 0 else shift[c][k] + term
-    change = [[shift[c][k] - shift[c][0] for k in range(coarse)] for c in range(3)]
-    for z in range(wide):
-        plane = shifted[z + 1, rows]
-        hats = [hats_ref[k * wide + z : k * wide + z + 1, :] for k in range(coarse)]
-        inside = functools.reduce(lambda a, b: a + b, hats)
-        if z < REACH:
-            across = across_ref[0, z]
-        elif z < REACH + planes:
-            across = own_across_ref[z - REACH]
-        else:
-            across = across_ref[1, z - REACH - planes]
-        for c, slope in enumerate((slopes[0, z], slopes[1, z], across)):
-            if c == 0 and not REACH <= z < REACH + planes:
-                slope = slope * inside
-            u = shift[c][0]
-            for k in range(1, coarse):
-                u = u + hats[k] * change[c][k]
-            plane = plane + u * slope
-        warped[z, rows] = plane
-    clear_edges(warped, side)
-
-    def fields(start):
-        i = [image[z, start : start + 8] for z in range(wide)]
-        w = [warped[z, PAD + start : PAD + start + 8] for z in range(wide)]
-        return (w, [b * b for b in w], [a * b for a, b in zip(i, w)])
-
-    of = box_sums(fields, planes, side, sums, threes, parts, box_ref)
-    for z in range(planes):
-        mean_w, mean_ww, mean_iw = [of(f, z) * (1.0 / 729.0) for f in range(3)]
-        mean_i = mean_ref[z]
-        sii = variance_ref[z]
-        sww = mean_ww - mean_w * mean_w
-        siw = mean_iw - mean_i * mean_w
-        ratio = siw / (sii * sww + EPSILON)
-        map_ref[z] = siw * ratio
-        weight[z] = (2.0 * ratio) * (
-            (image[z + REACH] - mean_i) - siw / (sww + EPSILON) * (warped[z + REACH, padded_rows(side)] - mean_w)
+    for c in range(3):
+        for k in range(coarse):
+            shift_ref[c, k] = shift[c][k] if k == 0 else shift[c][k] - shift[c][0]
+
+    clear_edges(outer, side)
+    for h in range(2):
+        images[h] = halves[h, 0:REACH].astype(F32)
+        outer[h, :, rows] = halves[h, REACH:].astype(F32)
+        across = jnp.dot(
+            halves[h, REACH + 1 - h : 2 * REACH + 1 - h].reshape(REACH * side, LANES),
+            slope_ref[...],
+            preferred_element_type=F32,
         )
-    row = force_message(
-        lambda z: weight[z],
-        lambda z: warped.at[z + REACH],
-        planes, cells_ref, rows_ref, cols_ref, marks_ref,
-    )
-    message_ref[...] = jnp.broadcast_to(row[None], message_ref.shape)
+        outer_across[h] = across.reshape(outer_across.shape[1:])
+    for z in range(-REACH, planes + REACH):
+        slope = moving(z + 1)[rows] - moving(z - 1)[rows]
+        if not 0 <= z < planes:
+            hats = [hats_ref[pl.ds(k * wide + z + REACH, 1), :] for k in range(coarse)]
+            slope = slope * functools.reduce(lambda a, b: a + b, hats)
+            slopes[1, z + REACH] = row_difference(moving(z), side)
+        slopes[0, z + REACH] = slope
+
+    @pl.when(lax.axis_index("gz") >= 0)
+    def _():
+        for z in range(-REACH, planes + REACH):
+            hats = [hats_ref[pl.ds(k * wide + z + REACH, 1), :] for k in range(coarse)]
+            if z < 0:
+                down, across = slopes[1, z + REACH], outer_across[0, z + REACH]
+            elif z < planes:
+                down, across = down_ref[z], across_ref[z]
+            else:
+                down, across = slopes[1, z + REACH], outer_across[1, z - planes]
+            plane = moving(z)[rows]
+            for c, slope in enumerate((slopes[0, z + REACH], down, across)):
+                u = shift_ref[c, 0]
+                for k in range(1, coarse):
+                    u = u + hats[k] * shift_ref[c, k]
+                plane = plane + u * slope
+            warped[z + REACH, rows] = plane
+        clear_edges(warped, side)
+
+        def fields(start):
+            i = [image(z)[start : start + 8] for z in range(-REACH, planes + REACH)]
+            w = [warped[z, PAD + start : PAD + start + 8] for z in range(wide)]
+            return (w, [b * b for b in w], [a * b for a, b in zip(i, w)])
+
+        of = box_sums(fields, planes, side, sums, threes, parts, box_ref)
+        for z in range(planes):
+            mean_w, mean_ww, mean_iw = [of(f, z) * (1.0 / 729.0) for f in range(3)]
+            mean_i = mean_ref[z]
+            sii = variance_ref[z]
+            sww = mean_ww - mean_w * mean_w
+            siw = mean_iw - mean_i * mean_w
+            ratio = siw / (sii * sww + EPSILON)
+            map_ref[z] = siw * ratio
+            weight[z] = (2.0 * ratio) * (
+                (image_ref[z] - mean_i)
+                - siw / (sww + EPSILON) * (warped[z + REACH, rows] - mean_w)
+            )
+        row = force_message(
+            lambda z: weight[z],
+            lambda z: (
+                warped[z + REACH + 1, rows] - warped[z + REACH - 1, rows],
+                row_difference(warped.at[z + REACH], side),
+                col_difference(warped[z + REACH, rows]),
+            ),
+            planes, cells_ref, rows_ref, cols_ref, marks_ref,
+        )
+        message_ref[...] = jnp.broadcast_to(row[None], message_ref.shape)
 
 
 def last_kernel(
@@ -491,7 +513,7 @@
     coarse_cols = width // GY
     coarse_rows = spread_ref.shape[1] // (3 * coarse * LANES)
     block_rows = rows // coarse_rows
-    grids, factor = regular_grid(
+    _, grids, factor = regular_grid(
         received_ref[...], spread_ref, coarse, block_rows, coarse_rows, coarse_cols
     )
     for r, grid in enumerate(grids):
@@ -562,7 +584,10 @@
         pltpu.VMEM((5, planes, side + 2 * PAD, width), F32),
         pltpu.VMEM((5, planes, side + 8, width), F32),
     ]
-    marks, hats, cells, rows, cols, box, slope, spread, hat_x, hat_y, own, own_across = call(
+    (
+        marks, hats, cells, rows, cols, box, slope, spread, hat_x, hat_y,
+        own, image, padded, down, across,
+    ) = call(
         functools.partial(table_kernel, block_rows=block_rows),
         [
             ((8, width), F32),
@@ -577,6 +602,9 @@
             ((width, width), BF16),
             ((5,) + field, F32),
             (field, F32),
+            ((planes, side + 2 * PAD, width), F32),
+            (field, F32),
+            (field, F32),
         ],
         boxes,
         jnp.stack([block_place, tissue]), fixed, moving,
@@ -584,33 +612,30 @@
 
     message = ((devices, 1, LANES), F32)
 
-    sent, mean, variance, image, shifted, across = call(
+    sent, mean, variance, halves = call(
         first_kernel,
-        [
-            message,
-            (field, F32),
-            (field, F32),
-            ((wide, side, width), F32),
-            ((wide + 2, side + 2 * PAD, width), F32),
-            ((2, REACH, side, width), F32),
-        ],
-        [pltpu.VMEM((2,) + halo[0], BF16)] + boxes + [pltpu.VMEM(field, F32)],
-        fixed, moving, near, far, marks, cells, rows, cols, box, slope, own,
+        [message, (field, F32), (field, F32), ((2,) + halo[0], BF16)],
+        boxes + [pltpu.VMEM(field, F32)],
+        image, padded, down, across, near, far, marks, cells, rows, cols, box, own,
     )
     received = lax.all_to_all(sent, ("blk", "gz"), 0, 0).reshape(devices, LANES)
     sent, correlation, velocity = call(
         second_kernel,
         [message, (field, F32), ((8 * block_rows * coarse_rows, LANES), F32)],
         [
+            pltpu.VMEM((2, REACH, side, width), F32),
+            pltpu.VMEM((2, REACH + 1, side + 2 * PAD, width), F32),
+            pltpu.VMEM((2, REACH, side, width), F32),
             pltpu.VMEM((2, wide, side, width), F32),
+            pltpu.VMEM((3, coarse, side, width), F32),
             pltpu.VMEM((wide, side + 2 * PAD, width), F32),
             pltpu.VMEM((3, planes, side + 2 * PAD, width), F32),
             pltpu.VMEM((3, planes, side + 8, width), F32),
             pltpu.VMEM((3 * planes * side // 2, 6 * width), BF16),
             pltpu.VMEM(field, F32),
         ],
-        received, image, shifted, marks,
-        mean, variance, hats, cells, rows, cols, box, own_across, across,
+        received, halves, image, padded, down, across, marks,
+        mean, variance, hats, cells, rows, cols, box, slope,
         spread, hat_x, hat_y,
     )
     received = lax.all_to_all(sent, ("blk", "gz"), 0, 0).reshape(devices, LANES)

time: 32.2 us -> 32.1 us (level)
  transfers between devices with their start and end apart: 2 -> 2, of which waited for: 1 -> 1; matrix products, arithmetic and copies ran while one was open for 0% -> 0% of each run, Pallas kernels for 2% -> 3%
where the time goes in v7:
time: 32.1 us; the launch traced here: 31.9 us
  blocking collectives  21.7 us (68%)
  Pallas kernels  4.95 us (15%)
  starting transfers between devices  3.11 us (10%)
  between operations  1.97 us (6%)
    all_to_all x2, blocking collectives, per_device(): received = lax.all_to_all(sent, ('blk', 'gz'), 0, 0).reshape(devices, LANES)  21.7 us
    pallas_call x5, Pallas kernels, call(): pl.pallas_call(kernel, out_shape=[jax.ShapeDtypeStruct(shape, dtype) for...  4.95 us
    ppermute x1, starting transfers between devices, per_device(): lax.ppermute(far, ('blk', 'gz'), far_pairs(lax.axis_size('blk'), depth_pa...  2.55 us
  transfers between devices with their start and end apart: 2, of which 1 were waited for; matrix products, arithmetic and copies ran while one was open for 0% of the time, Pallas kernels for 3%

profile of v7, /device:TPU:0, one launch (start us, length us, event | category | flops | bytes accessed | tf_op | source)
XLA Modules:
  0.0 31.9 jit_solution(9729651637381590970)
XLA Ops:
  0.6 0.9 %shard_map.59 = (bf16[9,32,128]{2,1,0:T(8,128)(2,1)S(1)}, bf16[9,32,128]{2,1,0:T(8,128)(2,1)S(1)}, bf16[8,32,128]{2,1,0:T(8,128)(2,1)S(1)}, bf16[8,32,128]{2,1,0:T(8,128)(2,1)S(1)}) custom-call(bf16[1,8,32,128]{3,2,1,0:T(8,128)(2,1)} %fixed_hbm.1, bf16[1,8,32,128]{3,2,1,0:T(8,128)(2,1)} %moving_hbm.1), custom_call_target="tpu_custom_call" | custom-call | tf_op jit(solution)/shard_map/pallas_call | solution.py:547
  1.5 0.6 %collective-permute-start = (bf16[9,32,128]{2,1,0:T(8,128)(2,1)S(1)}, bf16[9,32,128]{2,1,0:T(8,128)(2,1)S(1)}, u32[]{:S(2)}, u32[]{:S(2)}) collective-permute-start(bf16[9,32,128]{2,1,0:T(8,128)(2,1)S(1)} %get-tuple-element.34), channel_id=1, source_target_pairs={{0,1},{2,3},{1,0},{3,2},{4,5},{6,7},{5,4},{7,6},{8,9},{10,11},{9,8... | collective-permute-start | bytes 221192 | tf_op jit(solution)/shard_map/ppermute | solution.py:580
  2.1 2.6 %collective-permute-start.1 = (bf16[9,32,128]{2,1,0:T(8,128)(2,1)S(1)}, bf16[9,32,128]{2,1,0:T(8,128)(2,1)S(1)}, u32[]{:S(2)}, u32[]{:S(2)}) collective-permute-start(bf16[9,32,128]{2,1,0:T(8,128)(2,1)S(1)} %get-tuple-element.35), channel_id=1, source_target_pairs={{1,2},{2,1},{0,4},{3,7},{5,6},{6,5},{4,0},{7,3},{9,10},{10,9},{8,1... | collective-permute-start | bytes 221192 | tf_op jit(solution)/shard_map/ppermute | solution.py:578
  6.0 0.8 %shard_map.60 = (f32[8,128]{1,0:T(8,128)S(1)}, f32[32,128]{1,0:T(8,128)S(1)}, f32[16,128]{1,0:T(8,128)S(1)}, f32[2,32,128]{2,1,0:T(8,128)S(1)}, bf16[128,256]{1,...) custom-call(s32[2,1]{1,0:T(2,128)S(1)} %pad_add_fusion.both_ref, ...), custom_call_target="tpu_custom_call" | custom-call | tf_op jit(solution)/shard_map/pallas_call | solution.py:547
  6.8 0.0 collective-permute-done.near_ref
  6.8 0.2 collective-permute-done.1.far_ref
  7.0 0.9 %shard_map.61 = (f32[32,1,128]{2,1,0:T(1,128)S(1)}, f32[8,32,128]{2,1,0:T(8,128)S(1)}, f32[8,32,128]{2,1,0:T(8,128)S(1)}, bf16[2,9,32,128]{3,2,1,0:T(8,128)(2,1)S(1)}) custom-call(f32[8,32,128]{2,1,0:T(8,128)S(1)} %get-tuple-element.30.image_ref, f32[8,48,128]{2,1,0:T(8,128)S(1)} %get-tuple-element.31.planes_ref, ...), custom_call_target="tpu_custom_call" | custom-call | tf_op jit(solution)/shard_map/pallas_call | solution.py:547
  7.9 12.8 %all_to_all.10 = f32[32,1,128]{2,1,0:T(1,128)S(1)} all-to-all(f32[32,1,128]{2,1,0:T(1,128)S(1)} %get-tuple-element.42), channel_id=1, replica_groups=mesh['blk'=8,'gz'=4] {'blk','gz'}, dimensions={0} | all-to-all | bytes 32768 | tf_op jit(solution)/shard_map/all_to_all | solution.py:621
  20.7 1.4 %shard_map.62 = (f32[32,1,128]{2,1,0:T(1,128)S(1)}, f32[8,32,128]{2,1,0:T(8,128)S(1)}, f32[16,128]{1,0:T(8,128)S(1)}) custom-call(f32[32,128]{1,0:T(8,128)S(1)} %bitcast.6, bf16[2,9,32,128]{3,2,1,0:T(8,128)(2,1)S(1)} %get-tuple-element.43.halves, f32[8,32,128]{2,1,0:T(8,128)S(1)} %get-tuple-element.30.image_ref, ...), custom_call_target="tpu_custom_call" | custom-call | tf_op jit(solution)/shard_map/pallas_call | solution.py:547
  22.0 8.9 %all_to_all.11 = f32[32,1,128]{2,1,0:T(1,128)S(1)} all-to-all(f32[32,1,128]{2,1,0:T(1,128)S(1)} %get-tuple-element.51), channel_id=1, replica_groups=mesh['blk'=8,'gz'=4] {'blk','gz'}, dimensions={0} | all-to-all | bytes 32768 | tf_op jit(solution)/shard_map/all_to_all | solution.py:641
  30.9 1.0 %shard_map.63 = (f32[3,2,2,64]{3,2,1,0:T(2,128)}, f32[1,8,32,128]{3,2,1,0:T(8,128)}) custom-call(f32[32,128]{1,0:T(8,128)S(1)} %bitcast.7, f32[16,128]{1,0:T(8,128)S(1)} %get-tuple-element.52.velocity_ref, bf16[128,1536]{1,0:T(8,128)(2,1)S(1)} %get-tuple-element.48.spread_ref, f32[8,32,128]{2,1,0:T(8,128)S(1)} %get-tuple-element.53.map_ref), custom_call_target="tpu_custom_call" | custom-call | tf_op jit(solution)/shard_map/pallas_call | solution.py:547
  (1 shorter events, 0.0 us)
Async XLA Ops:
  1.5 5.2 %collective-permute-start = (bf16[9,32,128]{2,1,0:T(8,128)(2,1)S(1)}, bf16[9,32,128]{2,1,0:T(8,128)(2,1)S(1)}, u32[]{:S(2)}, u32[]{:S(2)}) collective-permute-start(bf16[9,32,128]{2,1,0:T(8,128)(2,1)S(1)} %get-tuple-element.34), channel_id=1, source_target_pairs={{0,1},{2,3},{1,0},{3,2},{4,5},{6,7},{5,4},{7,6},{8,9},{10,11},{9,8... | collective-permute-start | bytes 221192 | tf_op jit(solution)/shard_map/ppermute | solution.py:580
  2.1 4.9 %collective-permute-start.1 = (bf16[9,32,128]{2,1,0:T(8,128)(2,1)S(1)}, bf16[9,32,128]{2,1,0:T(8,128)(2,1)S(1)}, u32[]{:S(2)}, u32[]{:S(2)}) collective-permute-start(bf16[9,32,128]{2,1,0:T(8,128)(2,1)S(1)} %get-tuple-element.35), channel_id=1, source_target_pairs={{1,2},{2,1},{0,4},{3,7},{5,6},{6,5},{4,0},{7,3},{9,10},{10,9},{8,1... | collective-permute-start | bytes 221192 | tf_op jit(solution)/shard_map/ppermute | solution.py:578

commit v8 on v7

--- a/solution.py
+++ b/solution.py
@@ -76,14 +76,14 @@
     ref[..., PAD + side :, :] = edge
 
 
-def row_box(padded, three, side):
-    count = side + 8
-    three[...] = (
-        padded[PAD - 5 : PAD - 5 + count]
-        + padded[PAD - 4 : PAD - 4 + count]
-        + padded[PAD - 3 : PAD - 3 + count]
-    )
-    return three[1 : 1 + side] + three[4 : 4 + side] + three[7 : 7 + side]
+def row_box(value, padded, three):
+    side = value.shape[0]
+    rows = padded_rows(side)
+    middle = padded[PAD - 1 : PAD - 1 + side] + value + padded[PAD + 1 : PAD + 1 + side]
+    three[0:PAD] = padded[1 : PAD + 1]
+    three[rows] = middle
+    three[PAD + side :] = padded[PAD + side - 1 : 2 * PAD + side - 1]
+    return three[PAD - 3 : PAD - 3 + side] + middle + three[PAD + 3 : PAD + 3 + side]
 
 
 def row_difference(padded, side):
@@ -114,7 +114,7 @@
                 start = (i * count + f) * side
                 for h in range(2):
                     z = i + h * half
-                    total = row_box(sums.at[f, z], threes.at[f, z], side)
+                    total = row_box(sums[f, z, padded_rows(side)], sums.at[f, z], threes.at[f, z])
                     for part, rounded in enumerate(split(total, 3)):
                         lane = (2 * part + h) * LANES
                         parts[start : start + side, lane : lane + LANES] = rounded
@@ -341,8 +341,9 @@
         boxed = [of(f, i, h) for h in range(2) for i in range(REACH)]
         up, down = running(boxed), running(boxed[::-1])[::-1]
         for z in range(planes):
-            sums[f, z, padded_rows(side)] = up[z + REACH] if z < REACH else down[z - REACH]
-            own_ref[f, z] = row_box(sums.at[f, z], threes.at[f, z], side)
+            item = up[z + REACH] if z < REACH else down[z - REACH]
+            sums[f, z, padded_rows(side)] = item
+            own_ref[f, z] = row_box(item, sums.at[f, z], threes.at[f, z])
 
 
 def first_kernel(
@@ -362,14 +363,16 @@
         side, single, double, box_ref,
     )
     clear_edges(sums, side)
+    outer = []
     for f in range(5):
         low = running([of(f, i, 0) for i in range(REACH)][::-1])[::-1]
         high = running([of(f, i, 1) for i in range(REACH)])
-        for z, item in enumerate(low + high):
-            sums[f, z, padded_rows(side)] = item
+        outer.append(low + high)
+        for z, item in enumerate(outer[f]):
+            sums[f, z, rows] = item
     for z in range(planes):
         mean_i, mean_w, mean_ii, mean_ww, mean_iw = [
-            (row_box(sums.at[f, z], threes.at[f, z], side) + own_ref[f, z]) * (1.0 / 729.0)
+            (row_box(outer[f][z], sums.at[f, z], threes.at[f, z]) + own_ref[f, z]) * (1.0 / 729.0)
             for f in range(5)
         ]
         sii = mean_ii - mean_i * mean_i
@@ -582,7 +585,7 @@
         pltpu.VMEM((2 * REACH * side, 2 * width), BF16),
         pltpu.VMEM((3 * REACH * side, 4 * width), BF16),
         pltpu.VMEM((5, planes, side + 2 * PAD, width), F32),
-        pltpu.VMEM((5, planes, side + 8, width), F32),
+        pltpu.VMEM((5, planes, side + 2 * PAD, width), F32),
     ]
     (
         marks, hats, cells, rows, cols, box, slope, spread, hat_x, hat_y,
@@ -630,7 +633,7 @@
             pltpu.VMEM((3, coarse, side, width), F32),
             pltpu.VMEM((wide, side + 2 * PAD, width), F32),
             pltpu.VMEM((3, planes, side + 2 * PAD, width), F32),
-            pltpu.VMEM((3, planes, side + 8, width), F32),
+            pltpu.VMEM((3, planes, side + 2 * PAD, width), F32),
             pltpu.VMEM((3 * planes * side // 2, 6 * width), BF16),
             pltpu.VMEM(field, F32),
         ],

time: 32.1 us -> 32.1 us (level)
  transfers between devices with their start and end apart: 2 -> 2, of which waited for: 1 -> 1; matrix products, arithmetic and copies ran while one was open for 0% -> 0% of each run, Pallas kernels for 3% -> 2%
where the time goes in v8:
time: 32.1 us; the launch traced here: 31.9 us
  blocking collectives  21.7 us (68%)
  Pallas kernels  4.9 us (15%)
  starting transfers between devices  3.11 us (10%)
  between operations  1.98 us (6%)
    all_to_all x2, blocking collectives, per_device(): received = lax.all_to_all(sent, ('blk', 'gz'), 0, 0).reshape(devices, LANES)  21.7 us
    pallas_call x5, Pallas kernels, call(): pl.pallas_call(kernel, out_shape=[jax.ShapeDtypeStruct(shape, dtype) for...  4.9 us
    ppermute x1, starting transfers between devices, per_device(): lax.ppermute(far, ('blk', 'gz'), far_pairs(lax.axis_size('blk'), depth_pa...  2.55 us
  transfers between devices with their start and end apart: 2, of which 1 were waited for; matrix products, arithmetic and copies ran while one was open for 0% of the time, Pallas kernels for 2%

profile of v8, /device:TPU:0, one launch (start us, length us, event | category | flops | bytes accessed | tf_op | source)
XLA Modules:
  0.0 31.9 jit_solution(15197761340336937068)
XLA Ops:
  0.6 0.9 %shard_map.59 = (bf16[9,32,128]{2,1,0:T(8,128)(2,1)S(1)}, bf16[9,32,128]{2,1,0:T(8,128)(2,1)S(1)}, bf16[8,32,128]{2,1,0:T(8,128)(2,1)S(1)}, bf16[8,32,128]{2,1,0:T(8,128)(2,1)S(1)}) custom-call(bf16[1,8,32,128]{3,2,1,0:T(8,128)(2,1)} %fixed_hbm.1, bf16[1,8,32,128]{3,2,1,0:T(8,128)(2,1)} %moving_hbm.1), custom_call_target="tpu_custom_call" | custom-call | tf_op jit(solution)/shard_map/pallas_call | solution.py:550
  1.5 0.6 %collective-permute-start = (bf16[9,32,128]{2,1,0:T(8,128)(2,1)S(1)}, bf16[9,32,128]{2,1,0:T(8,128)(2,1)S(1)}, u32[]{:S(2)}, u32[]{:S(2)}) collective-permute-start(bf16[9,32,128]{2,1,0:T(8,128)(2,1)S(1)} %get-tuple-element.34), channel_id=1, source_target_pairs={{0,1},{2,3},{1,0},{3,2},{4,5},{6,7},{5,4},{7,6},{8,9},{10,11},{9,8... | collective-permute-start | bytes 221192 | tf_op jit(solution)/shard_map/ppermute | solution.py:583
  2.1 2.6 %collective-permute-start.1 = (bf16[9,32,128]{2,1,0:T(8,128)(2,1)S(1)}, bf16[9,32,128]{2,1,0:T(8,128)(2,1)S(1)}, u32[]{:S(2)}, u32[]{:S(2)}) collective-permute-start(bf16[9,32,128]{2,1,0:T(8,128)(2,1)S(1)} %get-tuple-element.35), channel_id=1, source_target_pairs={{1,2},{2,1},{0,4},{3,7},{5,6},{6,5},{4,0},{7,3},{9,10},{10,9},{8,1... | collective-permute-start | bytes 221192 | tf_op jit(solution)/shard_map/ppermute | solution.py:581
  6.0 0.8 %shard_map.60 = (f32[8,128]{1,0:T(8,128)S(1)}, f32[32,128]{1,0:T(8,128)S(1)}, f32[16,128]{1,0:T(8,128)S(1)}, f32[2,32,128]{2,1,0:T(8,128)S(1)}, bf16[128,256]{1,...) custom-call(s32[2,1]{1,0:T(2,128)S(1)} %pad_add_fusion.both_ref, ...), custom_call_target="tpu_custom_call" | custom-call | tf_op jit(solution)/shard_map/pallas_call | solution.py:550
  6.8 0.0 collective-permute-done.near_ref
  6.8 0.2 collective-permute-done.1.far_ref
  7.0 0.9 %shard_map.61 = (f32[32,1,128]{2,1,0:T(1,128)S(1)}, f32[8,32,128]{2,1,0:T(8,128)S(1)}, f32[8,32,128]{2,1,0:T(8,128)S(1)}, bf16[2,9,32,128]{3,2,1,0:T(8,128)(2,1)S(1)}) custom-call(f32[8,32,128]{2,1,0:T(8,128)S(1)} %get-tuple-element.30.image_ref, f32[8,48,128]{2,1,0:T(8,128)S(1)} %get-tuple-element.31.planes_ref, ...), custom_call_target="tpu_custom_call" | custom-call | tf_op jit(solution)/shard_map/pallas_call | solution.py:550
  7.9 12.8 %all_to_all.10 = f32[32,1,128]{2,1,0:T(1,128)S(1)} all-to-all(f32[32,1,128]{2,1,0:T(1,128)S(1)} %get-tuple-element.42), channel_id=1, replica_groups=mesh['blk'=8,'gz'=4] {'blk','gz'}, dimensions={0} | all-to-all | bytes 32768 | tf_op jit(solution)/shard_map/all_to_all | solution.py:624
  20.6 1.3 %shard_map.62 = (f32[32,1,128]{2,1,0:T(1,128)S(1)}, f32[8,32,128]{2,1,0:T(8,128)S(1)}, f32[16,128]{1,0:T(8,128)S(1)}) custom-call(f32[32,128]{1,0:T(8,128)S(1)} %bitcast.6, bf16[2,9,32,128]{3,2,1,0:T(8,128)(2,1)S(1)} %get-tuple-element.43.halves, f32[8,32,128]{2,1,0:T(8,128)S(1)} %get-tuple-element.30.image_ref, ...), custom_call_target="tpu_custom_call" | custom-call | tf_op jit(solution)/shard_map/pallas_call | solution.py:550
  22.0 8.9 %all_to_all.11 = f32[32,1,128]{2,1,0:T(1,128)S(1)} all-to-all(f32[32,1,128]{2,1,0:T(1,128)S(1)} %get-tuple-element.51), channel_id=1, replica_groups=mesh['blk'=8,'gz'=4] {'blk','gz'}, dimensions={0} | all-to-all | bytes 32768 | tf_op jit(solution)/shard_map/all_to_all | solution.py:644
  30.9 1.0 %shard_map.63 = (f32[3,2,2,64]{3,2,1,0:T(2,128)}, f32[1,8,32,128]{3,2,1,0:T(8,128)}) custom-call(f32[32,128]{1,0:T(8,128)S(1)} %bitcast.7, f32[16,128]{1,0:T(8,128)S(1)} %get-tuple-element.52.velocity_ref, bf16[128,1536]{1,0:T(8,128)(2,1)S(1)} %get-tuple-element.48.spread_ref, f32[8,32,128]{2,1,0:T(8,128)S(1)} %get-tuple-element.53.map_ref), custom_call_target="tpu_custom_call" | custom-call | tf_op jit(solution)/shard_map/pallas_call | solution.py:550
  (1 shorter events, 0.0 us)
Async XLA Ops:
  1.5 5.2 %collective-permute-start = (bf16[9,32,128]{2,1,0:T(8,128)(2,1)S(1)}, bf16[9,32,128]{2,1,0:T(8,128)(2,1)S(1)}, u32[]{:S(2)}, u32[]{:S(2)}) collective-permute-start(bf16[9,32,128]{2,1,0:T(8,128)(2,1)S(1)} %get-tuple-element.34), channel_id=1, source_target_pairs={{0,1},{2,3},{1,0},{3,2},{4,5},{6,7},{5,4},{7,6},{8,9},{10,11},{9,8... | collective-permute-start | bytes 221192 | tf_op jit(solution)/shard_map/ppermute | solution.py:583
  2.1 4.9 %collective-permute-start.1 = (bf16[9,32,128]{2,1,0:T(8,128)(2,1)S(1)}, bf16[9,32,128]{2,1,0:T(8,128)(2,1)S(1)}, u32[]{:S(2)}, u32[]{:S(2)}) collective-permute-start(bf16[9,32,128]{2,1,0:T(8,128)(2,1)S(1)} %get-tuple-element.35), channel_id=1, source_target_pairs={{1,2},{2,1},{0,4},{3,7},{5,6},{6,5},{4,0},{7,3},{9,10},{10,9},{8,1... | collective-permute-start | bytes 221192 | tf_op jit(solution)/shard_map/ppermute | solution.py:581

commit v9 on v8

--- a/solution.py
+++ b/solution.py
@@ -129,10 +129,10 @@
     return of
 
 
-def column_boxes(fixed, moving, side, single, double, box_ref):
-    step = REACH // 1
+def column_boxes(fixed, moving, side, pairs, single, double, box_ref):
+    step = pairs
     results = []
-    for first in range(0, REACH, step):
+    for first in range(0, pairs, step):
         for i in range(first, first + step):
             for h in range(2):
                 lane = h * LANES
@@ -334,7 +334,7 @@
     of = column_boxes(
         lambda i, h: fixed_ref[i + REACH * h],
         lambda i, h: moving_ref[i + REACH * h],
-        side, single, double, box_ref,
+        side, REACH, single, double, box_ref,
     )
     clear_edges(sums, side)
     for f in range(5):
@@ -346,34 +346,49 @@
             own_ref[f, z] = row_box(item, sums.at[f, z], threes.at[f, z])
 
 
+def add_side(planes_ref, below, box_ref, before_ref, after_ref, single, double, sums, threes):
+    side = planes_ref.shape[1]
+
+    def at(first, count, distance):
+        return planes_ref[first + jnp.where(below, count - distance, distance - 1)]
+
+    of = column_boxes(
+        lambda i, h: at(0, REACH, 1 + i + 2 * h),
+        lambda i, h: at(REACH, REACH + 1, 1 + i + 2 * h),
+        side, REACH // 2, single, double, box_ref,
+    )
+    clear_edges(sums, side)
+    for f in range(5):
+        boxed = [of(f, d % 2, d // 2) for d in range(REACH)]
+        for d, item in enumerate(running(boxed)):
+            sums[f, d, padded_rows(side)] = item
+            z = jnp.where(below, REACH - 1 - d, REACH + d)
+            other = jnp.where(below, REACH + d, REACH - 1 - d)
+            after_ref[f, z] = before_ref[f, z] + row_box(item, sums.at[f, d], threes.at[f, d])
+            after_ref[f, other] = before_ref[f, other]
+
+
+def near_kernel(near_ref, box_ref, own_ref, total_ref, *scratch):
+    odd = lax.axis_index("gz") % 2 == 1
+    add_side(near_ref, odd, box_ref, own_ref, total_ref, *scratch)
+
+
 def first_kernel(
     image_ref, planes_ref, down_ref, across_ref, near_ref, far_ref, marks_ref,
-    cells_ref, rows_ref, cols_ref, box_ref, own_ref,
+    cells_ref, rows_ref, cols_ref, box_ref, near_total_ref,
     message_ref, mean_ref, variance_ref, halves,
-    single, double, sums, threes, weight,
+    total_ref, weight, *scratch,
 ):
     planes, side, _ = image_ref.shape
     rows = padded_rows(side)
-    below = lax.rem(lax.axis_index("gz") + 1, 2)
+    odd = lax.axis_index("gz") % 2 == 1
+    add_side(far_ref, ~odd, box_ref, near_total_ref, total_ref, *scratch)
+    below = jnp.where(odd, 0, 1)
     halves[below] = near_ref[...]
     halves[1 - below] = far_ref[...]
-    of = column_boxes(
-        lambda i, h: halves[h, i],
-        lambda i, h: halves[h, REACH + i + 1 - h],
-        side, single, double, box_ref,
-    )
-    clear_edges(sums, side)
-    outer = []
-    for f in range(5):
-        low = running([of(f, i, 0) for i in range(REACH)][::-1])[::-1]
-        high = running([of(f, i, 1) for i in range(REACH)])
-        outer.append(low + high)
-        for z, item in enumerate(outer[f]):
-            sums[f, z, rows] = item
     for z in range(planes):
         mean_i, mean_w, mean_ii, mean_ww, mean_iw = [
-            (row_box(outer[f][z], sums.at[f, z], threes.at[f, z]) + own_ref[f, z]) * (1.0 / 729.0)
-            for f in range(5)
+            total_ref[f, z] * (1.0 / 729.0) for f in range(5)
         ]
         sii = mean_ii - mean_i * mean_i
         sww = mean_ww - mean_w * mean_w
@@ -615,11 +630,18 @@
 
     message = ((devices, 1, LANES), F32)
 
+    half_boxes = [
+        pltpu.VMEM((REACH * side, 2 * width), BF16),
+        pltpu.VMEM((3 * REACH // 2 * side, 4 * width), BF16),
+        pltpu.VMEM((5, REACH, side + 2 * PAD, width), F32),
+        pltpu.VMEM((5, REACH, side + 2 * PAD, width), F32),
+    ]
+    (total,) = call(near_kernel, [((5,) + field, F32)], half_boxes, near, box, own)
     sent, mean, variance, halves = call(
         first_kernel,
         [message, (field, F32), (field, F32), ((2,) + halo[0], BF16)],
-        boxes + [pltpu.VMEM(field, F32)],
-        image, padded, down, across, near, far, marks, cells, rows, cols, box, own,
+        [pltpu.VMEM((5,) + field, F32), pltpu.VMEM(field, F32)] + half_boxes,
+        image, padded, down, across, near, far, marks, cells, rows, cols, box, total,
     )
     received = lax.all_to_all(sent, ("blk", "gz"), 0, 0).reshape(devices, LANES)
     sent, correlation, velocity = call(

time: 32.1 us -> 32 us (level)
    pallas_call x5 -> x6, Pallas kernels: 4.9 us -> 5.1 us  [call(): pl.pallas_call(kernel, out_shape=[jax.ShapeDtypeStruct(shape, dtype) for...]
  transfers between devices with their start and end apart: 2 -> 2, of which waited for: 1 -> 0; matrix products, arithmetic and copies ran while one was open for 0% -> 0% of each run, Pallas kernels for 2% -> 4%
where the time goes in v9:
time: 32 us; the launch traced here: 31.7 us
  blocking collectives  21.5 us (67%)
  Pallas kernels  5.1 us (16%)
  starting transfers between devices  3.11 us (10%)
  between operations  1.99 us (6%)
    all_to_all x2, blocking collectives, per_device(): received = lax.all_to_all(sent, ('blk', 'gz'), 0, 0).reshape(devices, LANES)  21.5 us
    pallas_call x6, Pallas kernels, call(): pl.pallas_call(kernel, out_shape=[jax.ShapeDtypeStruct(shape, dtype) for...  5.1 us
    ppermute x1, starting transfers between devices, per_device(): lax.ppermute(far, ('blk', 'gz'), far_pairs(lax.axis_size('blk'), depth_pa...  2.55 us
  transfers between devices with their start and end apart: 2, of which 0 were waited for; matrix products, arithmetic and copies ran while one was open for 0% of the time, Pallas kernels for 4%

profile of v9, /device:TPU:0, one launch (start us, length us, event | category | flops | bytes accessed | tf_op | source)
XLA Modules:
  0.0 31.7 jit_solution(7214517656590595584)
XLA Ops:
  0.6 0.9 %shard_map.59 = (bf16[9,32,128]{2,1,0:T(8,128)(2,1)S(1)}, bf16[9,32,128]{2,1,0:T(8,128)(2,1)S(1)}, bf16[8,32,128]{2,1,0:T(8,128)(2,1)S(1)}, bf16[8,32,128]{2,1,0:T(8,128)(2,1)S(1)}) custom-call(bf16[1,8,32,128]{3,2,1,0:T(8,128)(2,1)} %fixed_hbm.1, bf16[1,8,32,128]{3,2,1,0:T(8,128)(2,1)} %moving_hbm.1), custom_call_target="tpu_custom_call" | custom-call | tf_op jit(solution)/shard_map/pallas_call | solution.py:565
  1.5 0.6 %collective-permute-start = (bf16[9,32,128]{2,1,0:T(8,128)(2,1)S(1)}, bf16[9,32,128]{2,1,0:T(8,128)(2,1)S(1)}, u32[]{:S(2)}, u32[]{:S(2)}) collective-permute-start(bf16[9,32,128]{2,1,0:T(8,128)(2,1)S(1)} %get-tuple-element.34), channel_id=1, source_target_pairs={{0,1},{2,3},{1,0},{3,2},{4,5},{6,7},{5,4},{7,6},{8,9},{10,11},{9,8... | collective-permute-start | bytes 221192 | tf_op jit(solution)/shard_map/ppermute | solution.py:598
  2.1 2.6 %collective-permute-start.1 = (bf16[9,32,128]{2,1,0:T(8,128)(2,1)S(1)}, bf16[9,32,128]{2,1,0:T(8,128)(2,1)S(1)}, u32[]{:S(2)}, u32[]{:S(2)}) collective-permute-start(bf16[9,32,128]{2,1,0:T(8,128)(2,1)S(1)} %get-tuple-element.35), channel_id=1, source_target_pairs={{1,2},{2,1},{0,4},{3,7},{5,6},{6,5},{4,0},{7,3},{9,10},{10,9},{8,1... | collective-permute-start | bytes 221192 | tf_op jit(solution)/shard_map/ppermute | solution.py:596
  6.0 0.8 %shard_map.60 = (f32[8,128]{1,0:T(8,128)S(1)}, f32[32,128]{1,0:T(8,128)S(1)}, f32[16,128]{1,0:T(8,128)S(1)}, f32[2,32,128]{2,1,0:T(8,128)S(1)}, bf16[128,256]{1,...) custom-call(s32[2,1]{1,0:T(2,128)S(1)} %pad_add_fusion.both_ref, ...), custom_call_target="tpu_custom_call" | custom-call | tf_op jit(solution)/shard_map/pallas_call | solution.py:565
  6.8 0.0 collective-permute-done.near_ref
  6.8 0.3 %shard_map.61.near_total_ref = f32[5,8,32,128]{3,2,1,0:T(8,128)S(1)} custom-call(bf16[9,32,128]{2,1,0:T(8,128)(2,1)S(1)} %collective-permute-done.near_ref, bf16[768,256]{1,0:T(8,128)(2,1)S(1)} %get-tuple-element.40.box_ref, f32[5,8,32,128]{3,2,1,0:T(8,128)S(1)} %get-tuple-element.41.own_ref), custom_call_target="tpu_custom_call" | custom-call | tf_op jit(solution)/shard_map/pallas_call | solution.py:565
  7.1 0.0 collective-permute-done.1.far_ref
  7.1 0.7 %shard_map.62 = (f32[32,1,128]{2,1,0:T(1,128)S(1)}, f32[8,32,128]{2,1,0:T(8,128)S(1)}, f32[8,32,128]{2,1,0:T(8,128)S(1)}, bf16[2,9,32,128]{3,2,1,0:T(8,128)(2,1)S(1)}) custom-call(f32[8,32,128]{2,1,0:T(8,128)S(1)} %get-tuple-element.30.image_ref, f32[8,48,128]{2,1,0:T(8,128)S(1)} %get-tuple-element.31.planes_ref, ...), custom_call_target="tpu_custom_call" | custom-call | tf_op jit(solution)/shard_map/pallas_call | solution.py:565
  7.9 12.7 %all_to_all.10 = f32[32,1,128]{2,1,0:T(1,128)S(1)} all-to-all(f32[32,1,128]{2,1,0:T(1,128)S(1)} %get-tuple-element.42), channel_id=1, replica_groups=mesh['blk'=8,'gz'=4] {'blk','gz'}, dimensions={0} | all-to-all | bytes 32768 | tf_op jit(solution)/shard_map/all_to_all | solution.py:646
  20.5 1.3 %shard_map.63 = (f32[32,1,128]{2,1,0:T(1,128)S(1)}, f32[8,32,128]{2,1,0:T(8,128)S(1)}, f32[16,128]{1,0:T(8,128)S(1)}) custom-call(f32[32,128]{1,0:T(8,128)S(1)} %bitcast.6, bf16[2,9,32,128]{3,2,1,0:T(8,128)(2,1)S(1)} %get-tuple-element.43.halves, f32[8,32,128]{2,1,0:T(8,128)S(1)} %get-tuple-element.30.image_ref, ...), custom_call_target="tpu_custom_call" | custom-call | tf_op jit(solution)/shard_map/pallas_call | solution.py:565
  21.9 8.9 %all_to_all.11 = f32[32,1,128]{2,1,0:T(1,128)S(1)} all-to-all(f32[32,1,128]{2,1,0:T(1,128)S(1)} %get-tuple-element.51), channel_id=1, replica_groups=mesh['blk'=8,'gz'=4] {'blk','gz'}, dimensions={0} | all-to-all | bytes 32768 | tf_op jit(solution)/shard_map/all_to_all | solution.py:666
  30.7 1.0 %shard_map.64 = (f32[3,2,2,64]{3,2,1,0:T(2,128)}, f32[1,8,32,128]{3,2,1,0:T(8,128)}) custom-call(f32[32,128]{1,0:T(8,128)S(1)} %bitcast.7, f32[16,128]{1,0:T(8,128)S(1)} %get-tuple-element.52.velocity_ref, bf16[128,1536]{1,0:T(8,128)(2,1)S(1)} %get-tuple-element.48.spread_ref, f32[8,32,128]{2,1,0:T(8,128)S(1)} %get-tuple-element.53.map_ref), custom_call_target="tpu_custom_call" | custom-call | tf_op jit(solution)/shard_map/pallas_call | solution.py:565
  (1 shorter events, 0.0 us)
Async XLA Ops:
  1.5 5.2 %collective-permute-start = (bf16[9,32,128]{2,1,0:T(8,128)(2,1)S(1)}, bf16[9,32,128]{2,1,0:T(8,128)(2,1)S(1)}, u32[]{:S(2)}, u32[]{:S(2)}) collective-permute-start(bf16[9,32,128]{2,1,0:T(8,128)(2,1)S(1)} %get-tuple-element.34), channel_id=1, source_target_pairs={{0,1},{2,3},{1,0},{3,2},{4,5},{6,7},{5,4},{7,6},{8,9},{10,11},{9,8... | collective-permute-start | bytes 221192 | tf_op jit(solution)/shard_map/ppermute | solution.py:598
  2.1 5.0 %collective-permute-start.1 = (bf16[9,32,128]{2,1,0:T(8,128)(2,1)S(1)}, bf16[9,32,128]{2,1,0:T(8,128)(2,1)S(1)}, u32[]{:S(2)}, u32[]{:S(2)}) collective-permute-start(bf16[9,32,128]{2,1,0:T(8,128)(2,1)S(1)} %get-tuple-element.35), channel_id=1, source_target_pairs={{1,2},{2,1},{0,4},{3,7},{5,6},{6,5},{4,0},{7,3},{9,10},{10,9},{8,1... | collective-permute-start | bytes 221192 | tf_op jit(solution)/shard_map/ppermute | solution.py:596

commit v10 on v9

--- a/solution.py
+++ b/solution.py
@@ -176,9 +176,10 @@
     total = [[None] * coarse for _ in range(3)]
     for z in range(planes):
         directions = slopes(z)
+        weight = weights(z)
         for k in range(coarse):
             index = k * planes + z
-            share = weights(z) * cells_ref[index : index + 1, :]
+            share = weight * cells_ref[index : index + 1, :]
             for c in range(3):
                 term = share * directions[c]
                 total[c][k] = term if z == 0 else total[c][k] + term
@@ -283,7 +284,7 @@
     row = sublane_index(cells_ref.shape)
     cells_ref[...] = cell_weights(part * planes + row % planes, row // planes)
     for a in range(coarse_rows):
-        rows_ref[a] = 0.5 * cell_weights(sublane_index((side, LANES)), a)
+        rows_ref[a] = cell_weights(sublane_index((side, LANES)), a)
     square = (LANES, LANES)
     cols = cell_weights(sublane_index(square), lane_index(square) % coarse_cols)
     for i, value in enumerate(split(cols, 2)):
@@ -377,7 +378,7 @@
     image_ref, planes_ref, down_ref, across_ref, near_ref, far_ref, marks_ref,
     cells_ref, rows_ref, cols_ref, box_ref, near_total_ref,
     message_ref, mean_ref, variance_ref, halves,
-    total_ref, weight, *scratch,
+    total_ref, *scratch,
 ):
     planes, side, _ = image_ref.shape
     rows = padded_rows(side)
@@ -386,7 +387,8 @@
     below = jnp.where(odd, 0, 1)
     halves[below] = near_ref[...]
     halves[1 - below] = far_ref[...]
-    for z in range(planes):
+
+    def weight(z):
         mean_i, mean_w, mean_ii, mean_ww, mean_iw = [
             total_ref[f, z] * (1.0 / 729.0) for f in range(5)
         ]
@@ -396,7 +398,7 @@
         mean_ref[z] = mean_i
         variance_ref[z] = sii
         ratio = siw / (sii * sww + EPSILON)
-        weight[z] = (2.0 * ratio) * (
+        return ratio * (
             (image_ref[z] - mean_i) - siw / (sww + EPSILON) * (planes_ref[z, rows] - mean_w)
         )
 
@@ -406,7 +408,7 @@
         return planes_ref[z, rows] if z < planes else halves[1, REACH + z - planes].astype(F32)
 
     row = force_message(
-        lambda z: weight[z],
+        weight,
         lambda z: (plane(z + 1) - plane(z - 1), down_ref[z], across_ref[z]),
         planes, cells_ref, rows_ref, cols_ref, marks_ref,
     )
@@ -418,7 +420,7 @@
     mean_ref, variance_ref, hats_ref, cells_ref, rows_ref, cols_ref, box_ref, slope_ref,
     spread_ref, hat_x_ref, hat_y_ref,
     message_ref, map_ref, velocity_ref,
-    images, outer, outer_across, slopes, shift_ref, warped, sums, threes, parts, weight,
+    images, outer, outer_across, slopes, shift_ref, warped, sums, threes, parts,
 ):
     planes, side, _ = mean_ref.shape
     wide = planes + 2 * REACH
@@ -498,7 +500,8 @@
             return (w, [b * b for b in w], [a * b for a, b in zip(i, w)])
 
         of = box_sums(fields, planes, side, sums, threes, parts, box_ref)
-        for z in range(planes):
+
+        def weight(z):
             mean_w, mean_ww, mean_iw = [of(f, z) * (1.0 / 729.0) for f in range(3)]
             mean_i = mean_ref[z]
             sii = variance_ref[z]
@@ -506,12 +509,13 @@
             siw = mean_iw - mean_i * mean_w
             ratio = siw / (sii * sww + EPSILON)
             map_ref[z] = siw * ratio
-            weight[z] = (2.0 * ratio) * (
+            return ratio * (
                 (image_ref[z] - mean_i)
                 - siw / (sww + EPSILON) * (warped[z + REACH, rows] - mean_w)
             )
+
         row = force_message(
-            lambda z: weight[z],
+            weight,
             lambda z: (
                 warped[z + REACH + 1, rows] - warped[z + REACH - 1, rows],
                 row_difference(warped.at[z + REACH], side),
@@ -640,7 +644,7 @@
     sent, mean, variance, halves = call(
         first_kernel,
         [message, (field, F32), (field, F32), ((2,) + halo[0], BF16)],
-        [pltpu.VMEM((5,) + field, F32), pltpu.VMEM(field, F32)] + half_boxes,
+        [pltpu.VMEM((5,) + field, F32)] + half_boxes,
         image, padded, down, across, near, far, marks, cells, rows, cols, box, total,
     )
     received = lax.all_to_all(sent, ("blk", "gz"), 0, 0).reshape(devices, LANES)
@@ -657,7 +661,6 @@
             pltpu.VMEM((3, planes, side + 2 * PAD, width), F32),
             pltpu.VMEM((3, planes, side + 2 * PAD, width), F32),
             pltpu.VMEM((3 * planes * side // 2, 6 * width), BF16),
-            pltpu.VMEM(field, F32),
         ],
         received, halves, image, padded, down, across, marks,
         mean, variance, hats, cells, rows, cols, box, slope,

time: 32 us -> 32 us (level)
  no operation moved by 1% of the time
where the time goes in v10:
time: 32 us; the launch traced here: 31.8 us
  blocking collectives  21.5 us (67%)
  Pallas kernels  5.13 us (16%)
  starting transfers between devices  3.11 us (10%)
  between operations  1.99 us (6%)
    all_to_all x2, blocking collectives, per_device(): received = lax.all_to_all(sent, ('blk', 'gz'), 0, 0).reshape(devices, LANES)  21.5 us
    pallas_call x6, Pallas kernels, call(): pl.pallas_call(kernel, out_shape=[jax.ShapeDtypeStruct(shape, dtype) for...  5.13 us
    ppermute x1, starting transfers between devices, per_device(): lax.ppermute(far, ('blk', 'gz'), far_pairs(lax.axis_size('blk'), depth_pa...  2.55 us
  transfers between devices with their start and end apart: 2, of which 0 were waited for; matrix products, arithmetic and copies ran while one was open for 0% of the time, Pallas kernels for 4%

profile of v10, /device:TPU:0, one launch (start us, length us, event | category | flops | bytes accessed | tf_op | source)
XLA Modules:
  0.0 31.8 jit_solution(16513601113569184937)
XLA Ops:
  0.6 0.9 %shard_map.59 = (bf16[9,32,128]{2,1,0:T(8,128)(2,1)S(1)}, bf16[9,32,128]{2,1,0:T(8,128)(2,1)S(1)}, bf16[8,32,128]{2,1,0:T(8,128)(2,1)S(1)}, bf16[8,32,128]{2,1,0:T(8,128)(2,1)S(1)}) custom-call(bf16[1,8,32,128]{3,2,1,0:T(8,128)(2,1)} %fixed_hbm.1, bf16[1,8,32,128]{3,2,1,0:T(8,128)(2,1)} %moving_hbm.1), custom_call_target="tpu_custom_call" | custom-call | tf_op jit(solution)/shard_map/pallas_call | solution.py:569
  1.5 0.6 %collective-permute-start = (bf16[9,32,128]{2,1,0:T(8,128)(2,1)S(1)}, bf16[9,32,128]{2,1,0:T(8,128)(2,1)S(1)}, u32[]{:S(2)}, u32[]{:S(2)}) collective-permute-start(bf16[9,32,128]{2,1,0:T(8,128)(2,1)S(1)} %get-tuple-element.34), channel_id=1, source_target_pairs={{0,1},{2,3},{1,0},{3,2},{4,5},{6,7},{5,4},{7,6},{8,9},{10,11},{9,8... | collective-permute-start | bytes 221192 | tf_op jit(solution)/shard_map/ppermute | solution.py:602
  2.1 2.6 %collective-permute-start.1 = (bf16[9,32,128]{2,1,0:T(8,128)(2,1)S(1)}, bf16[9,32,128]{2,1,0:T(8,128)(2,1)S(1)}, u32[]{:S(2)}, u32[]{:S(2)}) collective-permute-start(bf16[9,32,128]{2,1,0:T(8,128)(2,1)S(1)} %get-tuple-element.35), channel_id=1, source_target_pairs={{1,2},{2,1},{0,4},{3,7},{5,6},{6,5},{4,0},{7,3},{9,10},{10,9},{8,1... | collective-permute-start | bytes 221192 | tf_op jit(solution)/shard_map/ppermute | solution.py:600
  6.0 0.8 %shard_map.60 = (f32[8,128]{1,0:T(8,128)S(1)}, f32[32,128]{1,0:T(8,128)S(1)}, f32[16,128]{1,0:T(8,128)S(1)}, f32[2,32,128]{2,1,0:T(8,128)S(1)}, bf16[128,256]{1,...) custom-call(s32[2,1]{1,0:T(2,128)S(1)} %pad_add_fusion.both_ref, ...), custom_call_target="tpu_custom_call" | custom-call | tf_op jit(solution)/shard_map/pallas_call | solution.py:569
  6.8 0.0 collective-permute-done.near_ref
  6.8 0.3 %shard_map.61.near_total_ref = f32[5,8,32,128]{3,2,1,0:T(8,128)S(1)} custom-call(bf16[9,32,128]{2,1,0:T(8,128)(2,1)S(1)} %collective-permute-done.near_ref, bf16[768,256]{1,0:T(8,128)(2,1)S(1)} %get-tuple-element.40.box_ref, f32[5,8,32,128]{3,2,1,0:T(8,128)S(1)} %get-tuple-element.41.own_ref), custom_call_target="tpu_custom_call" | custom-call | tf_op jit(solution)/shard_map/pallas_call | solution.py:569
  7.1 0.0 collective-permute-done.1.far_ref
  7.1 0.7 %shard_map.62 = (f32[32,1,128]{2,1,0:T(1,128)S(1)}, f32[8,32,128]{2,1,0:T(8,128)S(1)}, f32[8,32,128]{2,1,0:T(8,128)S(1)}, bf16[2,9,32,128]{3,2,1,0:T(8,128)(2,1)S(1)}) custom-call(f32[8,32,128]{2,1,0:T(8,128)S(1)} %get-tuple-element.30.image_ref, f32[8,48,128]{2,1,0:T(8,128)S(1)} %get-tuple-element.31.planes_ref, ...), custom_call_target="tpu_custom_call" | custom-call | tf_op jit(solution)/shard_map/pallas_call | solution.py:569
  7.9 12.6 %all_to_all.10 = f32[32,1,128]{2,1,0:T(1,128)S(1)} all-to-all(f32[32,1,128]{2,1,0:T(1,128)S(1)} %get-tuple-element.42), channel_id=1, replica_groups=mesh['blk'=8,'gz'=4] {'blk','gz'}, dimensions={0} | all-to-all | bytes 32768 | tf_op jit(solution)/shard_map/all_to_all | solution.py:650
  20.5 1.4 %shard_map.63 = (f32[32,1,128]{2,1,0:T(1,128)S(1)}, f32[8,32,128]{2,1,0:T(8,128)S(1)}, f32[16,128]{1,0:T(8,128)S(1)}) custom-call(f32[32,128]{1,0:T(8,128)S(1)} %bitcast.6, bf16[2,9,32,128]{3,2,1,0:T(8,128)(2,1)S(1)} %get-tuple-element.43.halves, f32[8,32,128]{2,1,0:T(8,128)S(1)} %get-tuple-element.30.image_ref, ...), custom_call_target="tpu_custom_call" | custom-call | tf_op jit(solution)/shard_map/pallas_call | solution.py:569
  21.9 8.9 %all_to_all.11 = f32[32,1,128]{2,1,0:T(1,128)S(1)} all-to-all(f32[32,1,128]{2,1,0:T(1,128)S(1)} %get-tuple-element.51), channel_id=1, replica_groups=mesh['blk'=8,'gz'=4] {'blk','gz'}, dimensions={0} | all-to-all | bytes 32768 | tf_op jit(solution)/shard_map/all_to_all | solution.py:669
  30.8 1.0 %shard_map.64 = (f32[3,2,2,64]{3,2,1,0:T(2,128)}, f32[1,8,32,128]{3,2,1,0:T(8,128)}) custom-call(f32[32,128]{1,0:T(8,128)S(1)} %bitcast.7, f32[16,128]{1,0:T(8,128)S(1)} %get-tuple-element.52.velocity_ref, bf16[128,1536]{1,0:T(8,128)(2,1)S(1)} %get-tuple-element.48.spread_ref, f32[8,32,128]{2,1,0:T(8,128)S(1)} %get-tuple-element.53.map_ref), custom_call_target="tpu_custom_call" | custom-call | tf_op jit(solution)/shard_map/pallas_call | solution.py:569
  (1 shorter events, 0.0 us)
Async XLA Ops:
  1.5 5.2 %collective-permute-start = (bf16[9,32,128]{2,1,0:T(8,128)(2,1)S(1)}, bf16[9,32,128]{2,1,0:T(8,128)(2,1)S(1)}, u32[]{:S(2)}, u32[]{:S(2)}) collective-permute-start(bf16[9,32,128]{2,1,0:T(8,128)(2,1)S(1)} %get-tuple-element.34), channel_id=1, source_target_pairs={{0,1},{2,3},{1,0},{3,2},{4,5},{6,7},{5,4},{7,6},{8,9},{10,11},{9,8... | collective-permute-start | bytes 221192 | tf_op jit(solution)/shard_map/ppermute | solution.py:602
  2.1 5.0 %collective-permute-start.1 = (bf16[9,32,128]{2,1,0:T(8,128)(2,1)S(1)}, bf16[9,32,128]{2,1,0:T(8,128)(2,1)S(1)}, u32[]{:S(2)}, u32[]{:S(2)}) collective-permute-start(bf16[9,32,128]{2,1,0:T(8,128)(2,1)S(1)} %get-tuple-element.35), channel_id=1, source_target_pairs={{1,2},{2,1},{0,4},{3,7},{5,6},{6,5},{4,0},{7,3},{9,10},{10,9},{8,1... | collective-permute-start | bytes 221192 | tf_op jit(solution)/shard_map/ppermute | solution.py:600

commit v11 on v10

--- a/solution.py
+++ b/solution.py
@@ -254,14 +254,13 @@
     inner = (part > 0) & (part < lax.axis_size("gz") - 1)
     for copy in copies:
         copy.wait()
-    for ref, low, keep in ((far_ref, odd == 0, inner), (near_ref, odd == 1, None)):
-        i = fixed_ref[pl.ds(jnp.where(low, 0, planes - REACH), REACH)]
-        j = moving_ref[pl.ds(jnp.where(low, 0, planes - REACH - 1), REACH + 1)]
-        if keep is not None:
-            i = jnp.where(keep, i.astype(F32), 0.0).astype(BF16)
-            j = jnp.where(keep, j.astype(F32), 0.0).astype(BF16)
-        ref[0:REACH] = i
-        ref[REACH:] = j
+    for ref, low in ((far_ref, odd == 0), (near_ref, odd == 1)):
+        ref[0:REACH] = fixed_ref[pl.ds(jnp.where(low, 0, planes - REACH), REACH)]
+        ref[REACH:] = moving_ref[pl.ds(jnp.where(low, 0, planes - REACH - 1), REACH + 1)]
+
+    @pl.when(~inner)
+    def _():
+        far_ref[...] = jnp.zeros(far_ref.shape, BF16)
 
 
 def table_kernel(

time: 32 us -> 32 us (level)
  no operation moved by 1% of the time
where the time goes in v11:
time: 32 us; the launch traced here: 31.7 us
  blocking collectives  21.5 us (67%)
  Pallas kernels  5.13 us (16%)
  starting transfers between devices  3.11 us (10%)
  between operations  1.99 us (6%)
    all_to_all x2, blocking collectives, per_device(): received = lax.all_to_all(sent, ('blk', 'gz'), 0, 0).reshape(devices, LANES)  21.5 us
    pallas_call x6, Pallas kernels, call(): pl.pallas_call(kernel, out_shape=[jax.ShapeDtypeStruct(shape, dtype) for...  5.13 us
    ppermute x1, starting transfers between devices, per_device(): lax.ppermute(far, ('blk', 'gz'), far_pairs(lax.axis_size('blk'), depth_pa...  2.56 us
  transfers between devices with their start and end apart: 2, of which 0 were waited for; matrix products, arithmetic and copies ran while one was open for 0% of the time, Pallas kernels for 4%

profile of v11, /device:TPU:0, one launch (start us, length us, event | category | flops | bytes accessed | tf_op | source)
XLA Modules:
  0.0 31.7 jit_solution(13610109968093612556)
XLA Ops:
  0.6 0.9 %shard_map.59 = (bf16[9,32,128]{2,1,0:T(8,128)(2,1)S(1)}, bf16[9,32,128]{2,1,0:T(8,128)(2,1)S(1)}, bf16[8,32,128]{2,1,0:T(8,128)(2,1)S(1)}, bf16[8,32,128]{2,1,0:T(8,128)(2,1)S(1)}) custom-call(bf16[1,8,32,128]{3,2,1,0:T(8,128)(2,1)} %fixed_hbm.1, bf16[1,8,32,128]{3,2,1,0:T(8,128)(2,1)} %moving_hbm.1), custom_call_target="tpu_custom_call" | custom-call | tf_op jit(solution)/shard_map/pallas_call | solution.py:568
  1.5 0.5 %collective-permute-start = (bf16[9,32,128]{2,1,0:T(8,128)(2,1)S(1)}, bf16[9,32,128]{2,1,0:T(8,128)(2,1)S(1)}, u32[]{:S(2)}, u32[]{:S(2)}) collective-permute-start(bf16[9,32,128]{2,1,0:T(8,128)(2,1)S(1)} %get-tuple-element.34), channel_id=1, source_target_pairs={{0,1},{2,3},{1,0},{3,2},{4,5},{6,7},{5,4},{7,6},{8,9},{10,11},{9,8... | collective-permute-start | bytes 221192 | tf_op jit(solution)/shard_map/ppermute | solution.py:601
  2.1 2.6 %collective-permute-start.1 = (bf16[9,32,128]{2,1,0:T(8,128)(2,1)S(1)}, bf16[9,32,128]{2,1,0:T(8,128)(2,1)S(1)}, u32[]{:S(2)}, u32[]{:S(2)}) collective-permute-start(bf16[9,32,128]{2,1,0:T(8,128)(2,1)S(1)} %get-tuple-element.35), channel_id=1, source_target_pairs={{1,2},{2,1},{0,4},{3,7},{5,6},{6,5},{4,0},{7,3},{9,10},{10,9},{8,1... | collective-permute-start | bytes 221192 | tf_op jit(solution)/shard_map/ppermute | solution.py:599
  6.0 0.8 %shard_map.60 = (f32[8,128]{1,0:T(8,128)S(1)}, f32[32,128]{1,0:T(8,128)S(1)}, f32[16,128]{1,0:T(8,128)S(1)}, f32[2,32,128]{2,1,0:T(8,128)S(1)}, bf16[128,256]{1,...) custom-call(s32[2,1]{1,0:T(2,128)S(1)} %pad_add_fusion.both_ref, ...), custom_call_target="tpu_custom_call" | custom-call | tf_op jit(solution)/shard_map/pallas_call | solution.py:568
  6.8 0.0 collective-permute-done.near_ref
  6.8 0.3 %shard_map.61.near_total_ref = f32[5,8,32,128]{3,2,1,0:T(8,128)S(1)} custom-call(bf16[9,32,128]{2,1,0:T(8,128)(2,1)S(1)} %collective-permute-done.near_ref, bf16[768,256]{1,0:T(8,128)(2,1)S(1)} %get-tuple-element.40.box_ref, f32[5,8,32,128]{3,2,1,0:T(8,128)S(1)} %get-tuple-element.41.own_ref), custom_call_target="tpu_custom_call" | custom-call | tf_op jit(solution)/shard_map/pallas_call | solution.py:568
  7.1 0.0 collective-permute-done.1.far_ref
  7.1 0.7 %shard_map.62 = (f32[32,1,128]{2,1,0:T(1,128)S(1)}, f32[8,32,128]{2,1,0:T(8,128)S(1)}, f32[8,32,128]{2,1,0:T(8,128)S(1)}, bf16[2,9,32,128]{3,2,1,0:T(8,128)(2,1)S(1)}) custom-call(f32[8,32,128]{2,1,0:T(8,128)S(1)} %get-tuple-element.30.image_ref, f32[8,48,128]{2,1,0:T(8,128)S(1)} %get-tuple-element.31.planes_ref, ...), custom_call_target="tpu_custom_call" | custom-call | tf_op jit(solution)/shard_map/pallas_call | solution.py:568
  7.9 12.6 %all_to_all.10 = f32[32,1,128]{2,1,0:T(1,128)S(1)} all-to-all(f32[32,1,128]{2,1,0:T(1,128)S(1)} %get-tuple-element.42), channel_id=1, replica_groups=mesh['blk'=8,'gz'=4] {'blk','gz'}, dimensions={0} | all-to-all | bytes 32768 | tf_op jit(solution)/shard_map/all_to_all | solution.py:649
  20.5 1.4 %shard_map.63 = (f32[32,1,128]{2,1,0:T(1,128)S(1)}, f32[8,32,128]{2,1,0:T(8,128)S(1)}, f32[16,128]{1,0:T(8,128)S(1)}) custom-call(f32[32,128]{1,0:T(8,128)S(1)} %bitcast.6, bf16[2,9,32,128]{3,2,1,0:T(8,128)(2,1)S(1)} %get-tuple-element.43.halves, f32[8,32,128]{2,1,0:T(8,128)S(1)} %get-tuple-element.30.image_ref, ...), custom_call_target="tpu_custom_call" | custom-call | tf_op jit(solution)/shard_map/pallas_call | solution.py:568
  21.9 8.9 %all_to_all.11 = f32[32,1,128]{2,1,0:T(1,128)S(1)} all-to-all(f32[32,1,128]{2,1,0:T(1,128)S(1)} %get-tuple-element.51), channel_id=1, replica_groups=mesh['blk'=8,'gz'=4] {'blk','gz'}, dimensions={0} | all-to-all | bytes 32768 | tf_op jit(solution)/shard_map/all_to_all | solution.py:668
  30.7 1.0 %shard_map.64 = (f32[3,2,2,64]{3,2,1,0:T(2,128)}, f32[1,8,32,128]{3,2,1,0:T(8,128)}) custom-call(f32[32,128]{1,0:T(8,128)S(1)} %bitcast.7, f32[16,128]{1,0:T(8,128)S(1)} %get-tuple-element.52.velocity_ref, bf16[128,1536]{1,0:T(8,128)(2,1)S(1)} %get-tuple-element.48.spread_ref, f32[8,32,128]{2,1,0:T(8,128)S(1)} %get-tuple-element.53.map_ref), custom_call_target="tpu_custom_call" | custom-call | tf_op jit(solution)/shard_map/pallas_call | solution.py:568
  (1 shorter events, 0.0 us)
Async XLA Ops:
  1.5 5.2 %collective-permute-start = (bf16[9,32,128]{2,1,0:T(8,128)(2,1)S(1)}, bf16[9,32,128]{2,1,0:T(8,128)(2,1)S(1)}, u32[]{:S(2)}, u32[]{:S(2)}) collective-permute-start(bf16[9,32,128]{2,1,0:T(8,128)(2,1)S(1)} %get-tuple-element.34), channel_id=1, source_target_pairs={{0,1},{2,3},{1,0},{3,2},{4,5},{6,7},{5,4},{7,6},{8,9},{10,11},{9,8... | collective-permute-start | bytes 221192 | tf_op jit(solution)/shard_map/ppermute | solution.py:601
  2.1 5.0 %collective-permute-start.1 = (bf16[9,32,128]{2,1,0:T(8,128)(2,1)S(1)}, bf16[9,32,128]{2,1,0:T(8,128)(2,1)S(1)}, u32[]{:S(2)}, u32[]{:S(2)}) collective-permute-start(bf16[9,32,128]{2,1,0:T(8,128)(2,1)S(1)} %get-tuple-element.35), channel_id=1, source_target_pairs={{1,2},{2,1},{0,4},{3,7},{5,6},{6,5},{4,0},{7,3},{9,10},{10,9},{8,1... | collective-permute-start | bytes 221192 | tf_op jit(solution)/shard_map/ppermute | solution.py:599
